TPU v7x, 256 devices: a whole 4x4x8 slice. The times are simulated.
256 devices in a mesh: row: 8 (over x, y_lo), col: 32 (over z, y_hi, core).
Axes of the slice: x: 4, y: 4 (y_hi: 2, y_lo: 2; y = y_hi * 2 + y_lo), z: 8, core: 2. Of those that a mesh axis runs over, the one named last changes fastest.
Arguments:
- raw_spectra: float32 [1280, 64, 2, 512], P(('row', 'col')), may hold values from -250 to 250, as said below
- seg_valid: int32 [1280, 64], P(('row', 'col')), may hold values 0 or 1
- slot_order: int32 [1280], P(('row', 'col')), may hold values from 0 to 4, as said below
Outputs:
- stacked: bfloat16 [1280, 1280, 512], P('row', 'col')
Inputs may be any that keep to these rules, and one draw needn't show every extreme that they name: `raw_spectra`: spectra of noise segments; levels differ by channel, segment and frequency. `slot_order`: in each aligned block of 5 entries, a permutation of 0 to 4.
All inputs are finite; a program needn't handle non-finite values. No bound on the sum of `seg_valid` on one device may be relied on, other than what follows from the above.
Results may differ from a plain program's by a relative error of at most 0.0068.
Values may be sent and summed in bfloat16 or wider, within the bound.
No kernel may reach another device: no remote copies, remote signals or barrier semaphores. Data moves between devices by JAX's collectives and lax.ppermute only.
A program may use at most 192 MiB of HBM per device.

v0:
```python
import math

import jax
import jax.numpy as jnp
from jax import lax
from jax.sharding import PartitionSpec as P

SEG = 64
FREQ = 512
LAGS = 512
HALF_BAND = 64


def whiten(raw, valid):
    amplitude = jnp.sqrt(raw[:, :, 0, :] * raw[:, :, 0, :] + raw[:, :, 1, :] * raw[:, :, 1, :])
    bins = jnp.arange(FREQ, dtype=jnp.int32)
    band = (jnp.abs(bins[:, None] - bins[None, :]) <= HALF_BAND).astype(jnp.float32)
    counts = jnp.sum(band, axis=0)
    smooth = jnp.einsum("csf,fg->csg", amplitude, band, precision=lax.Precision.HIGHEST) / counts
    scaled = raw / (smooth + 1e-06)[:, :, None, :] * valid.astype(jnp.float32)[:, :, None, None]
    return scaled.astype(jnp.bfloat16)


def lag_table():
    bins = jnp.arange(FREQ, dtype=jnp.int32)
    shifts = jnp.arange(LAGS, dtype=jnp.int32)
    product = bins[:, None] * shifts[None, :] % (2 * FREQ)
    angle = product.astype(jnp.float32) * jnp.float32(math.pi / FREQ)
    return (jnp.cos(angle) * jnp.float32(1.0 / math.sqrt(SEG * FREQ))).astype(jnp.bfloat16)


def pair_tile(first, second, table):
    cross = jnp.einsum("asxf,bsxf->fab", first, second, preferred_element_type=jnp.float32).astype(
        jnp.bfloat16
    )
    return jnp.einsum("fab,ft->abt", cross, table, preferred_element_type=jnp.float32).astype(
        jnp.bfloat16
    )


def shards(raw_spectra, seg_valid, slot_order):
    white = whiten(raw_spectra, seg_valid)
    placed = jnp.take(white, slot_order, axis=0)
    table = lag_table()
    first_all = lax.all_gather(white, "col", axis=0, tiled=True)
    return pair_tile(first_all, lax.all_gather(placed, "row", axis=0, tiled=True), table)


def solution(mesh):
    placed = (P(("row", "col"), None, None, None), P(("row", "col"), None), P(("row", "col")))
    return jax.shard_map(
        shards, mesh=mesh, in_specs=placed, out_specs=P("row", "col", None), check_vma=False
    )
```

profile of v0, /device:TPU:1, one launch (start us, length us, event | category | flops | bytes accessed | tf_op | source)
XLA Modules:
  0.0 410.3 jit_solution(682094604706706483)
XLA Ops:
  6.5 0.0 copy-start.1
  6.5 0.0 all-gather.5.cloned.1.call-start
  6.5 0.1 convert_reduce_fusion
  6.7 0.7 compare_select_fusion
  7.4 0.7 compare_and_fusion
  8.1 2.9 fusion.31
  11.0 0.7 convert_element_type.22
  11.7 0.9 fusion.2
  12.6 0.0 copy-done.1
  12.6 0.3 fusion.1
  12.9 0.0 copy-start
  12.9 0.6 gather_fusion
  13.5 1.0 broadcast_select_fusion
  14.5 0.0 all-gather.5.cloned.1.call-update
  14.5 0.0 all-gather.3.cloned.1.call-start
  14.6 0.0 copy-done
  14.6 0.7 all-gather.3.cloned.1.call-update
  15.3 115.1 %all-gather.5.cloned.1.call-done = bf16[40,64,2,512]{3,1,2,0:T(8,128)(2,1)} async-done(((bf16[5,64,2,512]{3,1,2,0:T(8,128)(2,1)}), bf16[40,64,2,512]{3,1,2,0:T(8,128)(2,1)}) %all-gather.5.cloned.1.call-update) | async-done | bytes 5242896 | tf_op jit(solution)/shard_map/all_gather | solution.py:46
  130.4 13.3 %copy.10 = bf16[40,64,2,512]{1,0,2,3:T(8,128)(2,1)} copy(bf16[40,64,2,512]{3,1,2,0:T(8,128)(2,1)} %all-gather.5.cloned.1.call-done) | data formatting | bytes 10485760 | tf_op jit(solution)/shard_map/all_gather | solution.py:46
  143.7 149.8 %all-gather.3.cloned.1.call-done = bf16[160,64,2,512]{3,1,2,0:T(8,128)(2,1)} async-done(((bf16[5,64,2,512]{3,1,2,0:T(8,128)(2,1)}), bf16[160,64,2,512]{3,1,2,0:T(8,128)(2,1)}) %all-gather.3.cloned.1.call-update) | async-done | bytes 20971536 | tf_op jit(solution)/shard_map/all_gather | solution.py:45
  293.4 57.8 %copy.9 = bf16[160,64,2,512]{1,0,2,3:T(8,128)(2,1)} copy(bf16[160,64,2,512]{3,1,2,0:T(8,128)(2,1)} %all-gather.3.cloned.1.call-done) | data formatting | bytes 41943040 | tf_op jit(solution)/shard_map/all_gather | solution.py:45
  351.3 23.4 %bitcast_convert_fusion = bf16[512,160,40]{1,2,0:T(8,128)(2,1)} fusion(bf16[160,64,2,512]{1,0,2,3:T(8,128)(2,1)} %copy.9, bf16[40,64,2,512]{1,0,2,3:T(8,128)(2,1)} %copy.10), kind=kOutput, calls=%fused_computation.1 | convolution fusion | flops 842137600 | bytes 32768000 | tf_op jit(solution)/shard_map/asxf,bsxf->fab/dot_general | solution.py:33
  374.7 16.7 %copy.11 = bf16[512,160,40]{0,2,1:T(8,128)(2,1)} copy(bf16[512,160,40]{1,2,0:T(8,128)(2,1)} %bitcast_convert_fusion) | data formatting | bytes 13107200 | tf_op jit(solution)/shard_map/convert_element_type | solution.py:33
  391.4 12.1 %convolution_convert_fusion = bf16[160,40,512]{2,1,0:T(8,128)(2,1)} fusion(bf16[512,160,40]{0,2,1:T(8,128)(2,1)} %copy.11), kind=kOutput, calls=%fused_computation.2 | convolution fusion | flops 3362914304 | bytes 13107200 | tf_op jit(solution)/shard_map/fab,ft->abt/dot_general | solution.py:36
  (1 shorter events, 0.0 us)
Async XLA Ops:
  6.5 6.1 %copy-start.1 = (f32[5,64,2,512]{3,2,1,0:T(2,128)S(1)}, f32[5,64,2,512]{3,2,1,0:T(2,128)}, u32[]{:S(2)}) copy-start(f32[5,64,2,512]{3,2,1,0:T(2,128)} %param.3) | copy-start | bytes 3932164
  6.5 123.8 %all-gather.5.cloned.1.call-start = ((), (), s32[]{:S(2)}) async-start(), calls=%async_computation.1 | async-start | bytes 5898240 | tf_op jit(solution)/shard_map/all_gather | solution.py:46
  12.9 1.7 copy-start
  14.5 278.9 %all-gather.3.cloned.1.call-start = ((), (), s32[]{:S(2)}) async-start(), calls=%async_computation | async-start | bytes 21626880 | tf_op jit(solution)/shard_map/all_gather | solution.py:45
Sparse Core Ops, SparseCore 0:
  14.6 115.6 all-gather.4
  133.1 160.2 all-gather.2
where the time goes:
time: 413 us; the launch traced here: 410 us
  waiting for transfers between devices  266 us (64%)
  local copies, waits for them, and re-layouts  91.3 us (22%)
  matrix products  36.4 us (9%)
  between operations  13.5 us (3%)
    all_gather x1, waiting for transfers between devices, shards(): first_all = lax.all_gather(white, 'col', axis=0, tiled=True)  150 us
    all_gather x1, waiting for transfers between devices, shards(): lax.all_gather(placed, 'row', axis=0, tiled=True)  115 us
    all_gather x1, local copies, waits for them, and re-layouts, shards(): first_all = lax.all_gather(white, 'col', axis=0, tiled=True)  57.8 us
    dot_general x1, matrix products, pair_tile(): jnp.einsum('asxf,bsxf->fab', first, second, preferred_element_type=jnp.fl...  23.4 us
    convert_element_type x1, local copies, waits for them, and re-layouts, pair_tile(): jnp.einsum('asxf,bsxf->fab', first, second, preferred_element_type=jnp.fl...  16.7 us
    all_gather x1, local copies, waits for them, and re-layouts, shards(): lax.all_gather(placed, 'row', axis=0, tiled=True)  13.3 us
    dot_general x1, matrix products, pair_tile(): jnp.einsum('fab,ft->abt', cross, table, preferred_element_type=jnp.float32)  12.1 us
  transfers between devices with their start and end apart: 2, of which 2 were waited for; matrix products, arithmetic and copies ran while one was open for 3% of the time, Pallas kernels for 0%

commit v1 on v0

v1 whole, which is shorter than its diff:
```python
import functools
import math

import jax
import jax.numpy as jnp
from jax import lax
from jax.experimental import pallas as pl
from jax.experimental.pallas import tpu as pltpu
from jax.sharding import Mesh, PartitionSpec as P

CH = 5
SEG = 64
FREQ = 512
LAGS = 512
HALF_BAND = 64
K = 2 * SEG
HALF = FREQ // 2
N_X, N_YL, N_Z, N_YH, N_C = 4, 2, 8, 2, 2
SIZES = {"x": N_X, "yl": N_YL, "z": N_Z, "yh": N_YH, "c": N_C}
COLS = 40
BOTH = 2 * COLS
FB = 128
VMEM = 56 * 1024 * 1024


def lag_table():
    bins = jnp.arange(FREQ, dtype=jnp.int32)
    shifts = jnp.arange(LAGS, dtype=jnp.int32)
    product = bins[:, None] * shifts[None, :] % (2 * FREQ)
    angle = product.astype(jnp.float32) * jnp.float32(math.pi / FREQ)
    return (jnp.cos(angle) * jnp.float32(1.0 / math.sqrt(SEG * FREQ))).astype(jnp.bfloat16)


def shift(x, axis, step):
    n = SIZES[axis]
    return lax.ppermute(x, axis, [(i, (i + step) % n) for i in range(n)])


def params():
    return pltpu.CompilerParams(vmem_limit_bytes=VMEM)


def whiten_kernel(scal, raw, valid, mine, other):
    c = scal[0]
    rows = lax.broadcasted_iota(jnp.int32, (FREQ, FREQ), 0)
    cols = lax.broadcasted_iota(jnp.int32, (FREQ, FREQ), 1)
    band = (jnp.abs(rows - cols) <= HALF_BAND).astype(jnp.bfloat16)
    bins = lax.broadcasted_iota(jnp.int32, (1, FREQ), 1)
    count = jnp.minimum(bins + HALF_BAND, FREQ - 1) - jnp.maximum(bins - HALF_BAND, 0) + 1
    count = count.astype(jnp.float32)

    def part(j, x):
        tiles = [raw[pl.ds(j * SEG * 8 + 2 * b + x, SEG, stride=8), :] for b in range(4)]
        return jnp.concatenate(tiles, axis=1)

    for j in range(CH):
        re, im = part(j, 0), part(j, 1)
        amp = jnp.sqrt(re * re + im * im)
        hi = amp.astype(jnp.bfloat16)
        left = amp - hi.astype(jnp.float32)
        mid = left.astype(jnp.bfloat16)
        low = (left - mid.astype(jnp.float32)).astype(jnp.bfloat16)
        total = jnp.dot(hi, band, preferred_element_type=jnp.float32)
        total += jnp.dot(mid, band, preferred_element_type=jnp.float32)
        total += jnp.dot(low, band, preferred_element_type=jnp.float32)
        smooth = total / count + 1e-06
        keep = valid[j * SEG : (j + 1) * SEG, :].astype(jnp.float32)
        white = jnp.concatenate([re / smooth * keep, im / smooth * keep], axis=0)
        for b in range(4):
            tile = white[:, b * 128 : (b + 1) * 128].T.astype(jnp.bfloat16)
            at = (pl.ds((b % 2) * 128, 128), pl.ds(j * K, K))

            @pl.when(c == b // 2)
            def _():
                mine[(0,) + at] = tile

            @pl.when(c != b // 2)
            def _():
                other[(0,) + at] = tile

    for k in range(CH):
        src = pl.ds(pl.multiple_of(scal[1 + k] * K, K), K)
        mine[1, :, pl.ds(k * K, K)] = mine[0, :, src]
        other[1, :, pl.ds(k * K, K)] = other[0, :, src]


def whiten(raw, valid, order, c):
    view = raw.reshape(CH, SEG, 2, 4, 128).transpose(0, 1, 3, 2, 4).reshape(CH * SEG * 8, 128)
    scal = jnp.concatenate([c.reshape(1), order]).astype(jnp.int32)
    msg = jax.ShapeDtypeStruct((2, HALF, CH * K), jnp.bfloat16)
    return pl.pallas_call(
        whiten_kernel,
        out_shape=(msg, msg),
        in_specs=[
            pl.BlockSpec(memory_space=pltpu.SMEM),
            pl.BlockSpec(memory_space=pltpu.VMEM),
            pl.BlockSpec(memory_space=pltpu.VMEM),
        ],
        out_specs=(pl.BlockSpec(memory_space=pltpu.VMEM),) * 2,
        compiler_params=params(),
        cost_estimate=pl.CostEstimate(flops=10**9, bytes_accessed=3 * 10**6, transcendentals=0),
        name="whiten",
    )(scal, view, valid.reshape(CH * SEG, 1))


def columns_kernel(scal, *refs):
    pieces, out, flat = refs[:8], refs[8], refs[9]
    block = out.shape[0]
    for p in range(8):
        r = scal[p]
        for q in range(2):
            for k in range(CH):
                at = pl.multiple_of((q * COLS + r * CH + k) * block, block)
                flat[pl.ds(at, block), :] = pieces[p][q, :, k * K : (k + 1) * K].astype(jnp.float32)

    def body(i, carry):
        for u in range(8):
            f = i * 8 + u
            out[f] = flat[pl.ds(f, BOTH, stride=block), :].astype(jnp.bfloat16)
        return carry

    lax.fori_loop(0, block // 8, body, 0)


def columns(scal, pieces):
    block = 64
    piece = pl.BlockSpec((2, block, CH * K), lambda i, s: (0, i, 0))
    return pl.pallas_call(
        columns_kernel,
        out_shape=jax.ShapeDtypeStruct((HALF, BOTH, K), jnp.bfloat16),
        grid_spec=pltpu.PrefetchScalarGridSpec(
            num_scalar_prefetch=1,
            grid=(HALF // block,),
            in_specs=[piece] * 8,
            out_specs=pl.BlockSpec((block, BOTH, K), lambda i, s: (i, 0, 0)),
            scratch_shapes=[pltpu.VMEM((BOTH * block, K), jnp.float32)],
        ),
        compiler_params=params(),
        cost_estimate=pl.CostEstimate(flops=10**8, bytes_accessed=20 * 10**6, transcendentals=0),
        name="columns",
    )(scal, *pieces)


def cross_kernel(n, scal, *refs):
    pieces, cols, keep, send, flat, acc = refs[: 2 * n], refs[2 * n], *refs[2 * n + 1 :]
    rows = 20 * n
    c, yh = scal[0], scal[1]
    for p in range(2 * n):
        g, h = p // 2, p % 2
        for q in range(2):
            base = g * 20 + (yh ^ h) * 10 + (c ^ q) * 5
            for k in range(CH):
                at = pl.multiple_of((base + k) * FB, FB)
                flat[pl.ds(at, FB), :] = pieces[p][q, :, k * K : (k + 1) * K].astype(jnp.float32)

    def body(i, carry):
        for u in range(8):
            f = i * 8 + u
            first = flat[pl.ds(f, rows, stride=FB), :].astype(jnp.bfloat16)
            pair = lax.dot_general(
                first, cols[f], (((1,), (1,)), ((), ())), preferred_element_type=jnp.float32
            )
            acc[pl.ds(f, rows, stride=FB), 0:BOTH] = pair
        return carry

    lax.fori_loop(0, FB // 8, body, 0)
    for a in range(rows):
        tile = acc[a * FB : (a + 1) * FB, :].T
        keep[a] = tile[0:COLS].astype(jnp.bfloat16)
        send[a] = tile[COLS:BOTH].astype(jnp.bfloat16)


def cross(scal, pieces, cols):
    n = len(pieces) // 2
    rows = 20 * n
    piece = pl.BlockSpec((2, FB, CH * K), lambda i, s: (0, i, 0))
    part = pl.BlockSpec((rows, COLS, FB), lambda i, s: (0, 0, i))
    shape = jax.ShapeDtypeStruct((rows, COLS, HALF), jnp.bfloat16)
    return pl.pallas_call(
        functools.partial(cross_kernel, n),
        out_shape=(shape, shape),
        grid_spec=pltpu.PrefetchScalarGridSpec(
            num_scalar_prefetch=1,
            grid=(HALF // FB,),
            in_specs=[piece] * (2 * n) + [pl.BlockSpec((FB, BOTH, K), lambda i, s: (i, 0, 0))],
            out_specs=(part, part),
            scratch_shapes=[pltpu.VMEM((rows * FB, K), jnp.float32)] * 2,
        ),
        compiler_params=params(),
        cost_estimate=pl.CostEstimate(flops=10**10, bytes_accessed=10**7, transcendentals=0),
        name="cross",
    )(scal, *pieces, cols)


def lags_kernel(scal, keep, recv, near, far, *rest):
    out = rest[-1]
    total = jnp.dot(keep[...], near[0], preferred_element_type=jnp.float32)
    total += jnp.dot(recv[...], far[0], preferred_element_type=jnp.float32)
    out[...] = total.astype(jnp.bfloat16)


def lags(scal, keep, recv, table, prior):
    n = keep.shape[0] // 20
    rows = 20 * COLS
    half = pl.BlockSpec((rows, HALF), lambda i, s: (i, 0))
    extra = [] if prior is None else [prior]
    return pl.pallas_call(
        lags_kernel,
        out_shape=jax.ShapeDtypeStruct((N_Z * rows, LAGS), jnp.bfloat16),
        grid_spec=pltpu.PrefetchScalarGridSpec(
            num_scalar_prefetch=1,
            grid=(n,),
            in_specs=[
                half,
                half,
                pl.BlockSpec((1, HALF, LAGS), lambda i, s: (s[0], 0, 0)),
                pl.BlockSpec((1, HALF, LAGS), lambda i, s: (1 - s[0], 0, 0)),
            ]
            + [pl.BlockSpec(memory_space=pl.ANY)] * len(extra),
            out_specs=pl.BlockSpec((rows, LAGS), lambda i, s: (s[1 + i], 0)),
        ),
        input_output_aliases={5: 0} if extra else {},
        compiler_params=params(),
        cost_estimate=pl.CostEstimate(flops=2 * 10**9, bytes_accessed=3 * 10**6, transcendentals=0),
        name="lags",
    )(scal, keep.reshape(n * rows, HALF), recv.reshape(n * rows, HALF), table, table, *extra)


def shards(raw_spectra, seg_valid, slot_order):
    x, yl, z, yh, c = (lax.axis_index(a).astype(jnp.int32) for a in ("x", "yl", "z", "yh", "c"))
    mine, other = whiten(raw_spectra, seg_valid, slot_order, c)
    got = shift(other, "c", 1)
    row = jnp.stack([mine[0], got[0]])
    col = jnp.stack([mine[1], got[1]])
    table = lag_table().reshape(2, HALF, LAGS)

    R, C = {(0, 0): row}, {(0, 0): col}
    R[1, 0], R[-1, 0] = shift(row, "z", 1), shift(row, "z", -1)
    C[1, 0], C[-1, 0] = shift(col, "x", 1), shift(col, "x", -1)
    R[0, 1], C[0, 1] = shift(row, "yh", 1), shift(col, "yl", 1)
    R[2, 0], R[-2, 0] = shift(R[1, 0], "z", 1), shift(R[-1, 0], "z", -1)
    C[1, 1], C[-1, 1] = shift(C[0, 1], "x", 1), shift(C[0, 1], "x", -1)
    C[2, 0], C[2, 1] = shift(C[1, 0], "x", 1), shift(C[-1, 1], "x", -1)
    R[3, 0], R[-3, 0] = shift(R[2, 0], "z", 1), shift(R[-2, 0], "z", -1)
    R[4, 0] = shift(R[3, 0], "z", 1)
    for d in (1, -1, 2, -2, 3, -3, 4):
        step = 1 if d > 0 else -1
        R[d, 1] = shift(R[d, 0], "yh", 1) if d in (3, 4) else shift(R[d - step, 1], "z", step)

    order = [(dx, dy) for dx in (0, 1, -1, 2) for dy in (0, 1)]
    rows_of = jnp.stack([((x - dx) % N_X) * N_YL + (yl ^ dy) for dx, dy in order])
    cols = columns(rows_of, [C[o] for o in order])

    here = jnp.stack([c, yh])
    out = None
    for group in ((0,), (1, -1), (2, -2), (3, -3), (4,)):
        pieces = [R[d, h] for d in group for h in (0, 1)]
        keep, send = cross(here, pieces, cols)
        recv = shift(send, "c", 1)
        place = jnp.stack([c] + [(z - d) % N_Z for d in group])
        out = lags(place, keep, recv, table, out)
    return out.reshape(N_Z * 20, COLS, LAGS)


def solution(mesh):
    fine = Mesh(mesh.devices.reshape(N_X, N_YL, N_Z, N_YH, N_C), ("x", "yl", "z", "yh", "c"))
    every = ("x", "yl", "z", "yh", "c")
    return jax.shard_map(
        shards,
        mesh=fine,
        in_specs=(P(every, None, None, None), P(every, None), P(every)),
        out_specs=P(("x", "yl"), ("z", "yh", "c"), None),
        check_vma=False,
    )
```

time: 413 us -> 194 us (0.47)
  waiting for transfers between devices: 266 us -> 34.9 us
  Pallas kernels: 0 us -> 98.3 us
  local copies, waits for them, and re-layouts: 91.3 us -> 10.4 us
  starting transfers between devices: 0.04 us -> 39.9 us
  matrix products: 36.4 us -> 0 us
  between operations: 13.5 us -> 0.18 us
  other arithmetic: 3.48 us -> 9.9 us
    all_gather x2 -> x0, waiting for transfers between devices: 265 us -> none  [the longest x1 150 us: shards(): first_all = lax.all_gather(white, 'col', axis=0, tiled=True)]
    pallas_call x0 -> x12, Pallas kernels: none -> 98.3 us  [the longest x5 61.9 us: cross(): pl.pallas_call(functools.partial(cross_kernel, n), out_shape=(shape, shap...]
    all_gather x2 -> x0, local copies, waits for them, and re-layouts: 71.1 us -> none  [the longest x1 57.8 us: shards(): first_all = lax.all_gather(white, 'col', axis=0, tiled=True)]
    ppermute x0 -> x28, starting transfers between devices: none -> 39.9 us  [shift(): return lax.ppermute(x, axis, [(i, (i + step) % n) for i in range(n)])]
    dot_general x3 -> x0, matrix products: 36.4 us -> none  [the longest x1 23.4 us: pair_tile(): jnp.einsum('asxf,bsxf->fab', first, second, preferred_element_type=jnp.fl...]
    ppermute x0 -> x28, waiting for transfers between devices: none -> 34.9 us  [shift(): return lax.ppermute(x, axis, [(i, (i + step) % n) for i in range(n)])]
    convert_element_type x1 -> x0, local copies, waits for them, and re-layouts: 16.7 us -> none  [pair_tile(): jnp.einsum('asxf,bsxf->fab', first, second, preferred_element_type=jnp.fl...]
    unnamed x4 -> x42, local copies, waits for them, and re-layouts: 0.01 us -> 7.01 us
  transfers between devices with their start and end apart: 2 -> 28, of which waited for: 2 -> 5; matrix products, arithmetic and copies ran while one was open for 3% -> 5% of each run, Pallas kernels for 0% -> 46%
where the time goes in v1:
time: 194 us
  Pallas kernels  98.3 us (51%)
  starting transfers between devices  39.9 us (21%)
  waiting for transfers between devices  34.9 us (18%)
  local copies, waits for them, and re-layouts  10.4 us (5%)
  other arithmetic  9.9 us (5%)
    pallas_call x5, Pallas kernels, cross(): pl.pallas_call(functools.partial(cross_kernel, n), out_shape=(shape, shap...  61.9 us
    ppermute x28, starting transfers between devices, shift(): return lax.ppermute(x, axis, [(i, (i + step) % n) for i in range(n)])  39.9 us
    ppermute x28, waiting for transfers between devices, shift(): return lax.ppermute(x, axis, [(i, (i + step) % n) for i in range(n)])  34.9 us
    pallas_call x5, Pallas kernels, lags(): pl.pallas_call(lags_kernel, out_shape=jax.ShapeDtypeStruct((N_Z * rows, L...  19 us
    pallas_call x1, Pallas kernels, columns(): pl.pallas_call(columns_kernel, out_shape=jax.ShapeDtypeStruct((HALF, BOTH...  11.2 us
    unnamed x42, local copies, waits for them, and re-layouts  7.01 us
    pallas_call x1, Pallas kernels, whiten(): pl.pallas_call(whiten_kernel, out_shape=(msg, msg), in_specs=[pl.BlockSpe...  6.16 us
    convert_element_type x1, other arithmetic, lag_table(): (jnp.cos(angle) * jnp.float32(1.0 / math.sqrt(SEG * FREQ))).astype(jnp.bf...  4.88 us
  transfers between devices with their start and end apart: 28, of which 5 were waited for; matrix products, arithmetic and copies ran while one was open for 5% of the time, Pallas kernels for 46%

profile of v1, /device:TPU:1, one launch (start us, length us, event | category | flops | bytes accessed | tf_op | source)
XLA Modules:
  0.0 193.6 jit_solution(1285320411714735709)
XLA Ops:
  0.0 1.5 reshape.70.valid
  2.7 6.2 %whiten.1 = (bf16[2,256,640]{2,1,0:T(8,128)(2,1)}, bf16[2,256,640]{2,1,0:T(8,128)(2,1)}) custom-call(s32[6]{0:T(128)} %pad_add_fusion.2.scal, f32[2560,128]{1,0:T(8,128)} %bitcast.44, s32[320,1]{1,0:T(8,128)} %reshape.70.valid), custom_call_target="tpu_custom_call" | custom-call | flops 1000000000 | bytes 3000000 | tf_op jit(solution)/shard_map/whiten/pallas_call | solution.py:91
  8.9 3.2 %collective-permute-start = (bf16[2,256,640]{2,1,0:T(8,128)(2,1)}, bf16[2,256,640]{2,1,0:T(8,128)(2,1)S(1)}, u32[]{:S(2)}, u32[]{:S(2)}) collective-permute-start(bf16[2,256,640]{2,1,0:T(8,128)(2,1)} %get-tuple-element.18), channel_id=1, source_target_pairs={{0,1},{1,0},{2,3},{3,2},{4,5},{5,4},{6,7},{7,6},{8,9},{9,8},{10,11... | collective-permute-start | bytes 1966088 | tf_op jit(solution)/shard_map/ppermute | solution.py:36
  14.4 1.3 collective-permute-start.6
  16.9 1.5 collective-permute-start.9
  18.3 2.6 %collective-permute-start.18 = (bf16[2,256,640]{2,1,0:T(8,128)(2,1)S(1)}, bf16[2,256,640]{2,1,0:T(8,128)(2,1)}, u32[]{:S(2)}, u32[]{:S(2)}) collective-permute-start(bf16[2,256,640]{2,1,0:T(8,128)(2,1)S(1)} %pad_maximum_fusion.refs_0_), channel_id=1, source_target_pairs={{0,2},{2,0},{1,3},{3,1},{4,6},{6,4},{5,7},{7,5},{8,10},{10,8},{9,1... | collective-permute-start | bytes 1966088 | tf_op jit(solution)/shard_map/ppermute | solution.py:36
  20.9 12.1 %collective-permute-done.1.refs_0_ = bf16[2,256,640]{2,1,0:T(8,128)(2,1)} collective-permute-done((bf16[2,256,640]{2,1,0:T(8,128)(2,1)S(1)}, bf16[2,256,640]{2,1,0:T(8,128)(2,1)}, u32[]{:S(2)}, u32[]{:S(2)}) %collective-permute-start.1) | collective-permute-done | bytes 655392 | tf_op jit(solution)/shard_map/ppermute | solution.py:36
  35.7 1.5 collective-permute-start.10
  39.7 6.8 %collective-permute-done.18.refs_1_ = bf16[2,256,640]{2,1,0:T(8,128)(2,1)} collective-permute-done((bf16[2,256,640]{2,1,0:T(8,128)(2,1)S(1)}, bf16[2,256,640]{2,1,0:T(8,128)(2,1)}, u32[]{:S(2)}, u32[]{:S(2)}) %collective-permute-start.18) | collective-permute-done | bytes 655392 | tf_op jit(solution)/shard_map/ppermute | solution.py:36
  46.6 4.3 %collective-permute-start.19 = (bf16[2,256,640]{2,1,0:T(8,128)(2,1)}, bf16[2,256,640]{2,1,0:T(8,128)(2,1)S(1)}, u32[]{:S(2)}, u32[]{:S(2)}) collective-permute-start(bf16[2,256,640]{2,1,0:T(8,128)(2,1)} %collective-permute-done.18.refs_1_), channel_id=1, source_target_pairs={{0,28},{4,0},{8,4},{12,8},{16,12},{20,16},{24,20},{28,24},{1,29},{... | collective-permute-start | bytes 1966088 | tf_op jit(solution)/shard_map/ppermute | solution.py:36
  50.9 1.5 collective-permute-start.11
  52.3 2.4 %collective-permute-start.16 = (bf16[2,256,640]{2,1,0:T(8,128)(2,1)}, bf16[2,256,640]{2,1,0:T(8,128)(2,1)S(1)}, u32[]{:S(2)}, u32[]{:S(2)}) collective-permute-start(bf16[2,256,640]{2,1,0:T(8,128)(2,1)} %collective-permute-done.15.refs_2_), channel_id=1, source_target_pairs={{0,28},{4,0},{8,4},{12,8},{16,12},{20,16},{24,20},{28,24},{1,29},{... | collective-permute-start | bytes 1966088 | tf_op jit(solution)/shard_map/ppermute | solution.py:36
  54.8 1.5 collective-permute-start.12
  58.0 4.9 %fusion.5.near.far = bf16[2,256,512]{2,1,0:T(8,128)(2,1)} fusion(s32[2,256]{1,0:T(2,128)S(1)} %multiply_add_fusion), kind=kLoop, calls=%fused_computation.8 | loop fusion | flops 4194304 | bytes 526336 | tf_op jit(solution)/shard_map/convert_element_type | solution.py:31
  62.9 3.9 %collective-permute-done.11.refs_6_ = bf16[2,256,640]{2,1,0:T(8,128)(2,1)S(1)} collective-permute-done((bf16[2,256,640]{2,1,0:T(8,128)(2,1)S(1)}, bf16[2,256,640]{2,1,0:T(8,128)(2,1)S(1)}, u32[]{:S(2)}, u32[]{:S(2)}) %collective-permute-start.11) | collective-permute-done | bytes 655392 | tf_op jit(solution)/shard_map/ppermute | solution.py:36
  66.8 11.2 %collective-permute-done.16.refs_2_ = bf16[2,256,640]{2,1,0:T(8,128)(2,1)S(1)} collective-permute-done((bf16[2,256,640]{2,1,0:T(8,128)(2,1)}, bf16[2,256,640]{2,1,0:T(8,128)(2,1)S(1)}, u32[]{:S(2)}, u32[]{:S(2)}) %collective-permute-start.16) | collective-permute-done | bytes 655392 | tf_op jit(solution)/shard_map/ppermute | solution.py:36
  78.0 3.3 %collective-permute-start.17 = (bf16[2,256,640]{2,1,0:T(8,128)(2,1)S(1)}, bf16[2,256,640]{2,1,0:T(8,128)(2,1)}, u32[]{:S(2)}, u32[]{:S(2)}) collective-permute-start(bf16[2,256,640]{2,1,0:T(8,128)(2,1)S(1)} %collective-permute-done.16.refs_2_), channel_id=1, source_target_pairs={{0,28},{4,0},{8,4},{12,8},{16,12},{20,16},{24,20},{28,24},{1,29},{... | collective-permute-start | bytes 1966088 | tf_op jit(solution)/shard_map/ppermute | solution.py:36
  81.4 1.4 collective-permute-start.24
  83.7 11.2 %columns.1.refs_2_.refs_4_ = bf16[256,80,128]{2,1,0:T(8,128)(2,1)} custom-call(s32[8]{0:T(128)} %stack.100.scal, bf16[2,256,640]{2,1,0:T(8,128)(2,1)} %copy-done, bf16[2,256,640]{2,1,0:T(8,128)(2,1)} %copy-done.5, bf16[2,256,640]{2,1,0:T(8,128)(2,1)} %copy-done.6, bf16[2,256,640]{2,1,0:T(8,128)(2,1)} %collective-permute-done.8.refs_3_, ...), custom_call_target="tpu_custom_call" | custom-call | flops 100000000 | bytes 20000000 | tf_op jit(solution)/shard_map/columns/pallas_call | solution.py:128
  95.0 10.8 %cross.9 = (bf16[20,40,256]{2,1,0:T(8,128)(2,1)}, bf16[20,40,256]{2,1,0:T(8,128)(2,1)}) custom-call(s32[2]{0:T(128)} %pad_add_fusion.1.scal, bf16[2,256,640]{2,1,0:T(8,128)(2,1)} %copy-done.4, bf16[2,256,640]{2,1,0:T(8,128)(2,1)} %collective-permute-done.18.refs_1_, bf16[256,80,128]{2,1,0:T(8,128)(2,1)} %columns.1.refs_2_.refs_4_), custom_call_target="tpu_custom_call" | custom-call | flops 10000000000 | bytes 10000000 | tf_op jit(solution)/shard_map/cross/pallas_call | solution.py:179
  105.9 3.0 %collective-permute-start.27 = (bf16[20,40,256]{2,1,0:T(8,128)(2,1)}, bf16[20,40,256]{2,1,0:T(8,128)(2,1)S(1)}, u32[]{:S(2)}, u32[]{:S(2)}) collective-permute-start(bf16[20,40,256]{2,1,0:T(8,128)(2,1)} %get-tuple-element.28), channel_id=1, source_target_pairs={{0,1},{1,0},{2,3},{3,2},{4,5},{5,4},{6,7},{7,6},{8,9},{9,8},{10,11... | collective-permute-start | bytes 1228808 | tf_op jit(solution)/shard_map/ppermute | solution.py:36
  108.9 13.4 %cross.8 = (bf16[40,40,256]{2,1,0:T(8,128)(2,1)}, bf16[40,40,256]{2,1,0:T(8,128)(2,1)}) custom-call(s32[2]{0:T(128)} %pad_add_fusion.1.scal, bf16[2,256,640]{2,1,0:T(8,128)(2,1)} %collective-permute-done.1.refs_0_, bf16[2,256,640]{2,1,0:T(8,128)(2,1)} %copy-done.15, bf16[2,256,640]{2,1,0:T(8,128)(2,1)} %collective-permute-done.15.refs_2_, ...), custom_call_target="tpu_custom_call" | custom-call | flops 10000000000 | bytes 10000000 | tf_op jit(solution)/shard_map/cross/pallas_call | solution.py:179
  122.8 2.7 %collective-permute-start.21 = (bf16[2,256,640]{2,1,0:T(8,128)(2,1)}, bf16[2,256,640]{2,1,0:T(8,128)(2,1)S(1)}, u32[]{:S(2)}, u32[]{:S(2)}) collective-permute-start(bf16[2,256,640]{2,1,0:T(8,128)(2,1)} %collective-permute-done.20.refs_3_), channel_id=1, source_target_pairs={{0,28},{4,0},{8,4},{12,8},{16,12},{20,16},{24,20},{28,24},{1,29},{... | collective-permute-start | bytes 1966088 | tf_op jit(solution)/shard_map/ppermute | solution.py:36
  125.4 13.4 %cross.7 = (bf16[40,40,256]{2,1,0:T(8,128)(2,1)}, bf16[40,40,256]{2,1,0:T(8,128)(2,1)}) custom-call(s32[2]{0:T(128)} %pad_add_fusion.1.scal, bf16[2,256,640]{2,1,0:T(8,128)(2,1)} %collective-permute-done.2.refs_0_, bf16[2,256,640]{2,1,0:T(8,128)(2,1)} %collective-permute-done.24.refs_1_, bf16[2,256,640]{2,1,0:T(8,128)(2,1)} %copy-done.13, ...), custom_call_target="tpu_custom_call" | custom-call | flops 10000000000 | bytes 10000000 | tf_op jit(solution)/shard_map/cross/pallas_call | solution.py:179
  139.9 3.4 %lags.5.rest_0_ = bf16[6400,512]{1,0:T(8,128)(2,1)} custom-call(s32[2]{0:T(128)} %pad_add_fusion.6.scal, bf16[800,256]{1,0:T(8,128)(2,1)} %bitcast.40, bf16[800,256]{1,0:T(8,128)(2,1)} %bitcast.42, bf16[2,256,512]{2,1,0:T(8,128)(2,1)} %fusion.5.near.far, bf16[2,256,512]{2,1,0:T(8,128)(2,1)} %fusion.5.near.far), custom_call_target="tpu_custom_call" | custom-call | flops 2000000000 | bytes 3000000 | tf_op jit(solution)/shard_map/lags/pallas_call | solution.py:207
  144.0 2.7 %collective-permute-start.5 = (bf16[2,256,640]{2,1,0:T(8,128)(2,1)S(1)}, bf16[2,256,640]{2,1,0:T(8,128)(2,1)S(1)}, u32[]{:S(2)}, u32[]{:S(2)}) collective-permute-start(bf16[2,256,640]{2,1,0:T(8,128)(2,1)S(1)} %collective-permute-done.4.refs_0_), channel_id=1, source_target_pairs={{0,2},{2,0},{1,3},{3,1},{4,6},{6,4},{5,7},{7,5},{8,10},{10,8},{9,1... | collective-permute-start | bytes 1966088 | tf_op jit(solution)/shard_map/ppermute | solution.py:36
  148.3 13.4 %cross.6 = (bf16[40,40,256]{2,1,0:T(8,128)(2,1)}, bf16[40,40,256]{2,1,0:T(8,128)(2,1)}) custom-call(s32[2]{0:T(128)} %pad_add_fusion.1.scal, bf16[2,256,640]{2,1,0:T(8,128)(2,1)} %copy-done.14, bf16[2,256,640]{2,1,0:T(8,128)(2,1)} %copy-done.18, bf16[2,256,640]{2,1,0:T(8,128)(2,1)} %collective-permute-done.17.refs_2_, bf16[2,256,640]{2,1,0:T(8,128)(2,1)} %copy-done.19, ...), custom_call_target="tpu_custom_call" | custom-call | flops 10000000000 | bytes 10000000 | tf_op jit(solution)/shard_map/cross/pallas_call | solution.py:179
  163.0 10.9 %cross.5 = (bf16[20,40,256]{2,1,0:T(8,128)(2,1)}, bf16[20,40,256]{2,1,0:T(8,128)(2,1)}) custom-call(s32[2]{0:T(128)} %pad_add_fusion.1.scal, bf16[2,256,640]{2,1,0:T(8,128)(2,1)} %copy-done.17, bf16[2,256,640]{2,1,0:T(8,128)(2,1)} %copy-done.20, bf16[256,80,128]{2,1,0:T(8,128)(2,1)} %columns.1.refs_2_.refs_4_), custom_call_target="tpu_custom_call" | custom-call | flops 10000000000 | bytes 10000000 | tf_op jit(solution)/shard_map/cross/pallas_call | solution.py:179
  175.4 4.1 %lags.6.rest_0_ = bf16[6400,512]{1,0:T(8,128)(2,1)} custom-call(s32[3]{0:T(128)} %pad_add_fusion.5.scal, bf16[1600,256]{1,0:T(8,128)(2,1)} %bitcast.34, bf16[1600,256]{1,0:T(8,128)(2,1)} %bitcast.38, bf16[2,256,512]{2,1,0:T(8,128)(2,1)} %fusion.5.near.far, bf16[2,256,512]{2,1,0:T(8,128)(2,1)} %fusion.5.near.far, ...), custom_call_target="tpu_custom_call", output_to_operand_aliasing={{}: (5, {})} | custom-call | flops 2000000000 | bytes 3000000 | tf_op jit(solution)/shard_map/lags/pallas_call | solution.py:207
  180.4 4.1 %lags.7.rest_0_ = bf16[6400,512]{1,0:T(8,128)(2,1)} custom-call(s32[3]{0:T(128)} %pad_add_fusion.4.scal, bf16[1600,256]{1,0:T(8,128)(2,1)} %bitcast.35, bf16[1600,256]{1,0:T(8,128)(2,1)} %bitcast.36, bf16[2,256,512]{2,1,0:T(8,128)(2,1)} %fusion.5.near.far, bf16[2,256,512]{2,1,0:T(8,128)(2,1)} %fusion.5.near.far, ...), custom_call_target="tpu_custom_call", output_to_operand_aliasing={{}: (5, {})} | custom-call | flops 2000000000 | bytes 3000000 | tf_op jit(solution)/shard_map/lags/pallas_call | solution.py:207
  185.4 4.1 %lags.8.rest_0_ = bf16[6400,512]{1,0:T(8,128)(2,1)} custom-call(s32[3]{0:T(128)} %pad_add_fusion.3.scal, bf16[1600,256]{1,0:T(8,128)(2,1)} %bitcast.37, bf16[1600,256]{1,0:T(8,128)(2,1)} %bitcast.39, bf16[2,256,512]{2,1,0:T(8,128)(2,1)} %fusion.5.near.far, bf16[2,256,512]{2,1,0:T(8,128)(2,1)} %fusion.5.near.far, ...), custom_call_target="tpu_custom_call", output_to_operand_aliasing={{}: (5, {})} | custom-call | flops 2000000000 | bytes 3000000 | tf_op jit(solution)/shard_map/lags/pallas_call | solution.py:207
  190.2 3.4 %lags.9 = bf16[6400,512]{1,0:T(8,128)(2,1)} custom-call(s32[2]{0:T(128)} %pad_add_fusion.scal, bf16[800,256]{1,0:T(8,128)(2,1)} %bitcast.41, bf16[800,256]{1,0:T(8,128)(2,1)} %bitcast.43, bf16[2,256,512]{2,1,0:T(8,128)(2,1)} %fusion.5.near.far, bf16[2,256,512]{2,1,0:T(8,128)(2,1)} %fusion.5.near.far, ...), custom_call_target="tpu_custom_call", output_to_operand_aliasing={{}: (5, {})} | custom-call | flops 2000000000 | bytes 3000000 | tf_op jit(solution)/shard_map/lags/pallas_call | solution.py:207
  (93 shorter events, 21.9 us)
Async XLA Ops:
  8.9 5.2 %collective-permute-start = (bf16[2,256,640]{2,1,0:T(8,128)(2,1)}, bf16[2,256,640]{2,1,0:T(8,128)(2,1)S(1)}, u32[]{:S(2)}, u32[]{:S(2)}) collective-permute-start(bf16[2,256,640]{2,1,0:T(8,128)(2,1)} %get-tuple-element.18), channel_id=1, source_target_pairs={{0,1},{1,0},{2,3},{3,2},{4,5},{5,4},{6,7},{7,6},{8,9},{9,8},{10,11... | collective-permute-start | bytes 1966088 | tf_op jit(solution)/shard_map/ppermute | solution.py:36
  14.2 80.8 %copy-start.4 = (bf16[2,256,640]{2,1,0:T(8,128)(2,1)}, bf16[2,256,640]{2,1,0:T(8,128)(2,1)S(1)}, u32[]{:S(2)}) copy-start(bf16[2,256,640]{2,1,0:T(8,128)(2,1)S(1)} %pad_maximum_fusion.refs_0_) | copy-start | bytes 1966084
  14.2 18.8 %collective-permute-start.1 = (bf16[2,256,640]{2,1,0:T(8,128)(2,1)S(1)}, bf16[2,256,640]{2,1,0:T(8,128)(2,1)}, u32[]{:S(2)}, u32[]{:S(2)}) collective-permute-start(bf16[2,256,640]{2,1,0:T(8,128)(2,1)S(1)} %pad_maximum_fusion.refs_0_), channel_id=1, source_target_pairs={{0,4},{4,8},{8,12},{12,16},{16,20},{20,24},{24,28},{28,0},{1,5},{5... | collective-permute-start | bytes 1966088 | tf_op jit(solution)/shard_map/ppermute | solution.py:36
  14.4 68.5 %copy-start = (bf16[2,256,640]{2,1,0:T(8,128)(2,1)}, bf16[2,256,640]{2,1,0:T(8,128)(2,1)S(1)}, u32[]{:S(2)}) copy-start(bf16[2,256,640]{2,1,0:T(8,128)(2,1)S(1)} %pad_maximum_fusion.1.refs_0_) | copy-start | bytes 1966084
  14.4 19.8 %collective-permute-start.6 = (bf16[2,256,640]{2,1,0:T(8,128)(2,1)S(1)}, bf16[2,256,640]{2,1,0:T(8,128)(2,1)S(1)}, u32[]{:S(2)}, u32[]{:S(2)}) collective-permute-start(bf16[2,256,640]{2,1,0:T(8,128)(2,1)S(1)} %pad_maximum_fusion.1.refs_0_), channel_id=1, source_target_pairs={{0,32},{32,0},{1,33},{33,1},{2,34},{34,2},{3,35},{35,3},{4,36},{36... | collective-permute-start | bytes 1966088 | tf_op jit(solution)/shard_map/ppermute | solution.py:36
  15.6 18.9 %collective-permute-start.7 = (bf16[2,256,640]{2,1,0:T(8,128)(2,1)S(1)}, bf16[2,256,640]{2,1,0:T(8,128)(2,1)S(1)}, u32[]{:S(2)}, u32[]{:S(2)}) collective-permute-start(bf16[2,256,640]{2,1,0:T(8,128)(2,1)S(1)} %pad_maximum_fusion.1.refs_0_), channel_id=1, source_target_pairs={{0,64},{64,128},{128,192},{192,0},{1,65},{65,129},{129,193},{193,1... | collective-permute-start | bytes 1966088 | tf_op jit(solution)/shard_map/ppermute | solution.py:36
  16.9 18.9 %collective-permute-start.9 = (bf16[2,256,640]{2,1,0:T(8,128)(2,1)S(1)}, bf16[2,256,640]{2,1,0:T(8,128)(2,1)S(1)}, u32[]{:S(2)}, u32[]{:S(2)}) collective-permute-start(bf16[2,256,640]{2,1,0:T(8,128)(2,1)S(1)} %pad_maximum_fusion.1.refs_0_), channel_id=1, source_target_pairs={{0,192},{64,0},{128,64},{192,128},{1,193},{65,1},{129,65},{193,129... | collective-permute-start | bytes 1966088 | tf_op jit(solution)/shard_map/ppermute | solution.py:36
  18.3 28.2 %collective-permute-start.18 = (bf16[2,256,640]{2,1,0:T(8,128)(2,1)S(1)}, bf16[2,256,640]{2,1,0:T(8,128)(2,1)}, u32[]{:S(2)}, u32[]{:S(2)}) collective-permute-start(bf16[2,256,640]{2,1,0:T(8,128)(2,1)S(1)} %pad_maximum_fusion.refs_0_), channel_id=1, source_target_pairs={{0,2},{2,0},{1,3},{3,1},{4,6},{6,4},{5,7},{7,5},{8,10},{10,8},{9,1... | collective-permute-start | bytes 1966088 | tf_op jit(solution)/shard_map/ppermute | solution.py:36
  33.0 17.8 %collective-permute-start.15 = (bf16[2,256,640]{2,1,0:T(8,128)(2,1)S(1)}, bf16[2,256,640]{2,1,0:T(8,128)(2,1)}, u32[]{:S(2)}, u32[]{:S(2)}) collective-permute-start(bf16[2,256,640]{2,1,0:T(8,128)(2,1)S(1)} %pad_maximum_fusion.refs_0_), channel_id=1, source_target_pairs={{0,28},{4,0},{8,4},{12,8},{16,12},{20,16},{24,20},{28,24},{1,29},{... | collective-permute-start | bytes 1966088 | tf_op jit(solution)/shard_map/ppermute | solution.py:36
  34.2 48.7 %copy-start.5 = (bf16[2,256,640]{2,1,0:T(8,128)(2,1)}, bf16[2,256,640]{2,1,0:T(8,128)(2,1)S(1)}, u32[]{:S(2)}) copy-start(bf16[2,256,640]{2,1,0:T(8,128)(2,1)S(1)} %collective-permute-done.6.refs_1_) | copy-start | bytes 1966084
  34.2 16.7 %collective-permute-start.2 = (bf16[2,256,640]{2,1,0:T(8,128)(2,1)}, bf16[2,256,640]{2,1,0:T(8,128)(2,1)}, u32[]{:S(2)}, u32[]{:S(2)}) collective-permute-start(bf16[2,256,640]{2,1,0:T(8,128)(2,1)} %collective-permute-done.1.refs_0_), channel_id=1, source_target_pairs={{0,4},{4,8},{8,12},{12,16},{16,20},{20,24},{24,28},{28,0},{1,5},{5... | collective-permute-start | bytes 1966088 | tf_op jit(solution)/shard_map/ppermute | solution.py:36
  34.5 48.3 %copy-start.6 = (bf16[2,256,640]{2,1,0:T(8,128)(2,1)}, bf16[2,256,640]{2,1,0:T(8,128)(2,1)S(1)}, u32[]{:S(2)}) copy-start(bf16[2,256,640]{2,1,0:T(8,128)(2,1)S(1)} %collective-permute-done.7.refs_2_) | copy-start | bytes 1966084
  34.5 17.8 %collective-permute-start.8 = (bf16[2,256,640]{2,1,0:T(8,128)(2,1)S(1)}, bf16[2,256,640]{2,1,0:T(8,128)(2,1)}, u32[]{:S(2)}, u32[]{:S(2)}) collective-permute-start(bf16[2,256,640]{2,1,0:T(8,128)(2,1)S(1)} %collective-permute-done.6.refs_1_), channel_id=1, source_target_pairs={{0,64},{64,128},{128,192},{192,0},{1,65},{65,129},{129,193},{193,1... | collective-permute-start | bytes 1966088 | tf_op jit(solution)/shard_map/ppermute | solution.py:36
  35.7 19.0 %collective-permute-start.10 = (bf16[2,256,640]{2,1,0:T(8,128)(2,1)S(1)}, bf16[2,256,640]{2,1,0:T(8,128)(2,1)}, u32[]{:S(2)}, u32[]{:S(2)}) collective-permute-start(bf16[2,256,640]{2,1,0:T(8,128)(2,1)S(1)} %collective-permute-done.6.refs_1_), channel_id=1, source_target_pairs={{0,192},{64,0},{128,64},{192,128},{1,193},{65,1},{129,65},{193,129... | collective-permute-start | bytes 1966088 | tf_op jit(solution)/shard_map/ppermute | solution.py:36
  46.6 34.8 %collective-permute-start.19 = (bf16[2,256,640]{2,1,0:T(8,128)(2,1)}, bf16[2,256,640]{2,1,0:T(8,128)(2,1)S(1)}, u32[]{:S(2)}, u32[]{:S(2)}) collective-permute-start(bf16[2,256,640]{2,1,0:T(8,128)(2,1)} %collective-permute-done.18.refs_1_), channel_id=1, source_target_pairs={{0,28},{4,0},{8,4},{12,8},{16,12},{20,16},{24,20},{28,24},{1,29},{... | collective-permute-start | bytes 1966088 | tf_op jit(solution)/shard_map/ppermute | solution.py:36
  50.9 30.6 %collective-permute-start.23 = (bf16[2,256,640]{2,1,0:T(8,128)(2,1)}, bf16[2,256,640]{2,1,0:T(8,128)(2,1)S(1)}, u32[]{:S(2)}, u32[]{:S(2)}) collective-permute-start(bf16[2,256,640]{2,1,0:T(8,128)(2,1)} %collective-permute-done.18.refs_1_), channel_id=1, source_target_pairs={{0,4},{4,8},{8,12},{12,16},{16,20},{20,24},{24,28},{28,0},{1,5},{5... | collective-permute-start | bytes 1966088 | tf_op jit(solution)/shard_map/ppermute | solution.py:36
  50.9 16.0 %collective-permute-start.11 = (bf16[2,256,640]{2,1,0:T(8,128)(2,1)S(1)}, bf16[2,256,640]{2,1,0:T(8,128)(2,1)S(1)}, u32[]{:S(2)}, u32[]{:S(2)}) collective-permute-start(bf16[2,256,640]{2,1,0:T(8,128)(2,1)S(1)} %collective-permute-done.7.refs_2_), channel_id=1, source_target_pairs={{0,64},{64,128},{128,192},{192,0},{1,65},{65,129},{129,193},{193,1... | collective-permute-start | bytes 1966088 | tf_op jit(solution)/shard_map/ppermute | solution.py:36
  52.3 25.7 %collective-permute-start.16 = (bf16[2,256,640]{2,1,0:T(8,128)(2,1)}, bf16[2,256,640]{2,1,0:T(8,128)(2,1)S(1)}, u32[]{:S(2)}, u32[]{:S(2)}) collective-permute-start(bf16[2,256,640]{2,1,0:T(8,128)(2,1)} %collective-permute-done.15.refs_2_), channel_id=1, source_target_pairs={{0,28},{4,0},{8,4},{12,8},{16,12},{20,16},{24,20},{28,24},{1,29},{... | collective-permute-start | bytes 1966088 | tf_op jit(solution)/shard_map/ppermute | solution.py:36
  54.8 28.1 %collective-permute-start.12 = (bf16[2,256,640]{2,1,0:T(8,128)(2,1)}, bf16[2,256,640]{2,1,0:T(8,128)(2,1)S(1)}, u32[]{:S(2)}, u32[]{:S(2)}) collective-permute-start(bf16[2,256,640]{2,1,0:T(8,128)(2,1)} %collective-permute-done.10.refs_5_), channel_id=1, source_target_pairs={{0,192},{64,0},{128,64},{192,128},{1,193},{65,1},{129,65},{193,129... | collective-permute-start | bytes 1966088 | tf_op jit(solution)/shard_map/ppermute | solution.py:36
  66.8 42.1 %collective-permute-start.3 = (bf16[2,256,640]{2,1,0:T(8,128)(2,1)}, bf16[2,256,640]{2,1,0:T(8,128)(2,1)S(1)}, u32[]{:S(2)}, u32[]{:S(2)}) collective-permute-start(bf16[2,256,640]{2,1,0:T(8,128)(2,1)} %collective-permute-done.2.refs_0_), channel_id=1, source_target_pairs={{0,4},{4,8},{8,12},{12,16},{16,20},{20,24},{24,28},{28,0},{1,5},{5... | collective-permute-start | bytes 1966088 | tf_op jit(solution)/shard_map/ppermute | solution.py:36
  78.0 65.3 %collective-permute-start.17 = (bf16[2,256,640]{2,1,0:T(8,128)(2,1)S(1)}, bf16[2,256,640]{2,1,0:T(8,128)(2,1)}, u32[]{:S(2)}, u32[]{:S(2)}) collective-permute-start(bf16[2,256,640]{2,1,0:T(8,128)(2,1)S(1)} %collective-permute-done.16.refs_2_), channel_id=1, source_target_pairs={{0,28},{4,0},{8,4},{12,8},{16,12},{20,16},{24,20},{28,24},{1,29},{... | collective-permute-start | bytes 1966088 | tf_op jit(solution)/shard_map/ppermute | solution.py:36
  81.3 41.0 %collective-permute-start.20 = (bf16[2,256,640]{2,1,0:T(8,128)(2,1)S(1)}, bf16[2,256,640]{2,1,0:T(8,128)(2,1)}, u32[]{:S(2)}, u32[]{:S(2)}) collective-permute-start(bf16[2,256,640]{2,1,0:T(8,128)(2,1)S(1)} %collective-permute-done.19.refs_3_), channel_id=1, source_target_pairs={{0,28},{4,0},{8,4},{12,8},{16,12},{20,16},{24,20},{28,24},{1,29},{... | collective-permute-start | bytes 1966088 | tf_op jit(solution)/shard_map/ppermute | solution.py:36
  81.4 41.3 %collective-permute-start.24 = (bf16[2,256,640]{2,1,0:T(8,128)(2,1)S(1)}, bf16[2,256,640]{2,1,0:T(8,128)(2,1)}, u32[]{:S(2)}, u32[]{:S(2)}) collective-permute-start(bf16[2,256,640]{2,1,0:T(8,128)(2,1)S(1)} %collective-permute-done.23.refs_1_), channel_id=1, source_target_pairs={{0,4},{4,8},{8,12},{12,16},{16,20},{20,24},{24,28},{28,0},{1,5},{5... | collective-permute-start | bytes 1966088 | tf_op jit(solution)/shard_map/ppermute | solution.py:36
  105.9 33.0 %collective-permute-start.27 = (bf16[20,40,256]{2,1,0:T(8,128)(2,1)}, bf16[20,40,256]{2,1,0:T(8,128)(2,1)S(1)}, u32[]{:S(2)}, u32[]{:S(2)}) collective-permute-start(bf16[20,40,256]{2,1,0:T(8,128)(2,1)} %get-tuple-element.28), channel_id=1, source_target_pairs={{0,1},{1,0},{2,3},{3,2},{4,5},{5,4},{6,7},{7,6},{8,9},{9,8},{10,11... | collective-permute-start | bytes 1228808 | tf_op jit(solution)/shard_map/ppermute | solution.py:36
  108.9 35.1 %collective-permute-start.4 = (bf16[2,256,640]{2,1,0:T(8,128)(2,1)S(1)}, bf16[2,256,640]{2,1,0:T(8,128)(2,1)S(1)}, u32[]{:S(2)}, u32[]{:S(2)}) collective-permute-start(bf16[2,256,640]{2,1,0:T(8,128)(2,1)S(1)} %collective-permute-done.3.refs_0_), channel_id=1, source_target_pairs={{0,4},{4,8},{8,12},{12,16},{16,20},{20,24},{24,28},{28,0},{1,5},{5... | collective-permute-start | bytes 1966088 | tf_op jit(solution)/shard_map/ppermute | solution.py:36
  122.3 24.4 %collective-permute-start.14 = (bf16[2,256,640]{2,1,0:T(8,128)(2,1)S(1)}, bf16[2,256,640]{2,1,0:T(8,128)(2,1)S(1)}, u32[]{:S(2)}, u32[]{:S(2)}) collective-permute-start(bf16[2,256,640]{2,1,0:T(8,128)(2,1)S(1)} %collective-permute-done.3.refs_0_), channel_id=1, source_target_pairs={{0,2},{2,0},{1,3},{3,1},{4,6},{6,4},{5,7},{7,5},{8,10},{10,8},{9,1... | collective-permute-start | bytes 1966088 | tf_op jit(solution)/shard_map/ppermute | solution.py:36
  122.8 23.9 %collective-permute-start.21 = (bf16[2,256,640]{2,1,0:T(8,128)(2,1)}, bf16[2,256,640]{2,1,0:T(8,128)(2,1)S(1)}, u32[]{:S(2)}, u32[]{:S(2)}) collective-permute-start(bf16[2,256,640]{2,1,0:T(8,128)(2,1)} %collective-permute-done.20.refs_3_), channel_id=1, source_target_pairs={{0,28},{4,0},{8,4},{12,8},{16,12},{20,16},{24,20},{28,24},{1,29},{... | collective-permute-start | bytes 1966088 | tf_op jit(solution)/shard_map/ppermute | solution.py:36
  138.9 40.6 %collective-permute-start.25 = (bf16[40,40,256]{2,1,0:T(8,128)(2,1)}, bf16[40,40,256]{2,1,0:T(8,128)(2,1)S(1)}, u32[]{:S(2)}, u32[]{:S(2)}) collective-permute-start(bf16[40,40,256]{2,1,0:T(8,128)(2,1)} %get-tuple-element.24), channel_id=1, source_target_pairs={{0,1},{1,0},{2,3},{3,2},{4,5},{5,4},{6,7},{7,6},{8,9},{9,8},{10,11... | collective-permute-start | bytes 2457608 | tf_op jit(solution)/shard_map/ppermute | solution.py:36
  143.3 31.1 %collective-permute-start.26 = (bf16[40,40,256]{2,1,0:T(8,128)(2,1)S(1)}, bf16[40,40,256]{2,1,0:T(8,128)(2,1)S(1)}, u32[]{:S(2)}, u32[]{:S(2)}) collective-permute-start(bf16[40,40,256]{2,1,0:T(8,128)(2,1)S(1)} %copy-done.12), channel_id=1, source_target_pairs={{0,1},{1,0},{2,3},{3,2},{4,5},{5,4},{6,7},{7,6},{8,9},{9,8},{10,11... | collective-permute-start | bytes 2457608 | tf_op jit(solution)/shard_map/ppermute | solution.py:36
  144.0 18.1 %collective-permute-start.5 = (bf16[2,256,640]{2,1,0:T(8,128)(2,1)S(1)}, bf16[2,256,640]{2,1,0:T(8,128)(2,1)S(1)}, u32[]{:S(2)}, u32[]{:S(2)}) collective-permute-start(bf16[2,256,640]{2,1,0:T(8,128)(2,1)S(1)} %collective-permute-done.4.refs_0_), channel_id=1, source_target_pairs={{0,2},{2,0},{1,3},{3,1},{4,6},{6,4},{5,7},{7,5},{8,10},{10,8},{9,1... | collective-permute-start | bytes 1966088 | tf_op jit(solution)/shard_map/ppermute | solution.py:36
  161.7 22.7 %collective-permute-start.22 = (bf16[40,40,256]{2,1,0:T(8,128)(2,1)}, bf16[40,40,256]{2,1,0:T(8,128)(2,1)S(1)}, u32[]{:S(2)}, u32[]{:S(2)}) collective-permute-start(bf16[40,40,256]{2,1,0:T(8,128)(2,1)} %get-tuple-element.22), channel_id=1, source_target_pairs={{0,1},{1,0},{2,3},{3,2},{4,5},{5,4},{6,7},{7,6},{8,9},{9,8},{10,11... | collective-permute-start | bytes 2457608 | tf_op jit(solution)/shard_map/ppermute | solution.py:36
  173.9 15.6 %collective-permute-start.13 = (bf16[20,40,256]{2,1,0:T(8,128)(2,1)}, bf16[20,40,256]{2,1,0:T(8,128)(2,1)S(1)}, u32[]{:S(2)}, u32[]{:S(2)}) collective-permute-start(bf16[20,40,256]{2,1,0:T(8,128)(2,1)} %get-tuple-element.20), channel_id=1, source_target_pairs={{0,1},{1,0},{2,3},{3,2},{4,5},{5,4},{6,7},{7,6},{8,9},{9,8},{10,11... | collective-permute-start | bytes 1228808 | tf_op jit(solution)/shard_map/ppermute | solution.py:36
  (17 other events, 183.4 us)

commit v2 on v1

v2 whole, which is shorter than its diff:
```python
import functools
import math

import jax
import jax.numpy as jnp
import numpy as np
from jax import lax
from jax.experimental import pallas as pl
from jax.experimental.pallas import tpu as pltpu
from jax.sharding import Mesh, PartitionSpec as P

CH = 5
SEG = 64
FREQ = 512
LAGS = 512
HALF_BAND = 64
K = 2 * SEG
HALF = FREQ // 2
N_X, N_YL, N_Z, N_YH, N_C = 4, 2, 8, 2, 2
SIZES = {"x": N_X, "yl": N_YL, "z": N_Z, "yh": N_YH, "c": N_C}
COLS = 40
BOTH = 2 * COLS
FB = 128
VMEM = 60 * 1024 * 1024


def lag_table():
    product = np.arange(FREQ)[:, None] * np.arange(LAGS)[None, :] % (2 * FREQ)
    wave = np.cos(product * (math.pi / FREQ)) / math.sqrt(SEG * FREQ)
    return jnp.asarray(wave.astype(np.float32)).astype(jnp.bfloat16).reshape(2, HALF, LAGS)


def shift(x, axis, step):
    n = SIZES[axis]
    return lax.ppermute(x, axis, [(i, (i + step) % n) for i in range(n)])


def params():
    return pltpu.CompilerParams(vmem_limit_bytes=VMEM)


def whiten_kernel(scal, raw, valid, mine, other):
    c = scal[4]
    rows = lax.broadcasted_iota(jnp.int32, (FREQ, FREQ), 0)
    cols = lax.broadcasted_iota(jnp.int32, (FREQ, FREQ), 1)
    band = (jnp.abs(rows - cols) <= HALF_BAND).astype(jnp.bfloat16)
    bins = lax.broadcasted_iota(jnp.int32, (1, FREQ), 1)
    count = jnp.minimum(bins + HALF_BAND, FREQ - 1) - jnp.maximum(bins - HALF_BAND, 0) + 1
    count = count.astype(jnp.float32)

    def part(x):
        tiles = [raw[pl.ds(2 * b + x, CH * SEG, stride=8), :] for b in range(4)]
        return jnp.concatenate(tiles, axis=1)

    re, im = part(0), part(1)
    amp = jnp.sqrt(re * re + im * im)
    hi = amp.astype(jnp.bfloat16)
    left = amp - hi.astype(jnp.float32)
    mid = left.astype(jnp.bfloat16)
    low = (left - mid.astype(jnp.float32)).astype(jnp.bfloat16)
    parts = jnp.concatenate([hi, mid, low], axis=0)
    sums = jnp.dot(parts, band, preferred_element_type=jnp.float32)
    n = CH * SEG
    smooth = (sums[:n] + sums[n : 2 * n] + sums[2 * n :]) / count + 1e-06
    scale = 1.0 / smooth
    re, im = re * scale, im * scale
    for j in range(CH):
        keep = valid[j : j + 1, :].astype(jnp.float32)
        keep = jnp.concatenate([keep, keep], axis=1)
        for b in range(4):
            at = (slice(j * SEG, (j + 1) * SEG), slice(b * 128, (b + 1) * 128))
            tile = jnp.concatenate([re[at], im[at]], axis=0).T
            tile = (tile * keep).astype(jnp.bfloat16)
            to = (0, pl.ds((b % 2) * 128, 128), pl.ds(j * K, K))

            @pl.when(c == b // 2)
            def _():
                mine[to] = tile

            @pl.when(c != b // 2)
            def _():
                other[to] = tile

    for k in range(CH):
        src = pl.ds(pl.multiple_of(scal[5 + k] * K, K), K)
        mine[1, :, pl.ds(k * K, K)] = mine[0, :, src]
        other[1, :, pl.ds(k * K, K)] = other[0, :, src]


def whiten(scal, raw, valid):
    view = raw.reshape(CH, SEG, 2, 4, 128).transpose(0, 1, 3, 2, 4).reshape(CH * SEG * 8, 128)
    msg = jax.ShapeDtypeStruct((2, HALF, CH * K), jnp.bfloat16)
    return pl.pallas_call(
        whiten_kernel,
        out_shape=(msg, msg),
        in_specs=[
            pl.BlockSpec(memory_space=pltpu.SMEM),
            pl.BlockSpec(memory_space=pltpu.VMEM),
            pl.BlockSpec(memory_space=pltpu.VMEM),
        ],
        out_specs=(pl.BlockSpec(memory_space=pltpu.VMEM),) * 2,
        compiler_params=params(),
        cost_estimate=pl.CostEstimate(flops=10**9, bytes_accessed=3 * 10**6, transcendentals=0),
        name="whiten",
    )(scal, view, valid)


ORDER = [(dx, dy) for dx in (0, 1, -1, 2) for dy in (0, 1)]
UNROLL = 16


def cross_kernel(n, scal, *refs):
    rows = 20 * n
    pieces, cols = refs[: 2 * n], refs[2 * n : 2 * n + 8]
    keep, send, flat, side, acc = refs[2 * n + 8 :]
    x, yl, yh, c = scal[0], scal[1], scal[3], scal[4]

    def spread(piece, q, into, base):
        for k in range(CH):
            at = pl.multiple_of((base + k) * FB, FB)
            into[pl.ds(at, FB), :] = piece[q, :, k * K : (k + 1) * K].astype(jnp.float32)

    for p in range(8):
        dx, dy = ORDER[p]
        r = lax.rem(x - dx + N_X, N_X) * N_YL + (yl ^ dy)
        for q in range(2):
            spread(cols[p], q, side, q * COLS + r * CH)
    for p in range(2 * n):
        for q in range(2):
            spread(pieces[p], q, flat, (p // 2) * 20 + (yh ^ (p % 2)) * 10 + (c ^ q) * 5)

    def body(i, carry):
        at = [i * UNROLL + u for u in range(UNROLL)]
        pairs = []
        for f in at:
            first = flat[pl.ds(f, rows, stride=FB), :].astype(jnp.bfloat16)
            second = side[pl.ds(f, BOTH, stride=FB), :].astype(jnp.bfloat16)
            pairs.append(
                lax.dot_general(
                    first, second, (((1,), (1,)), ((), ())), preferred_element_type=jnp.float32
                )
            )
        for f, pair in zip(at, pairs):
            acc[pl.ds(f, rows, stride=FB), 0:BOTH] = pair
        return carry

    lax.fori_loop(0, FB // UNROLL, body, 0)
    for a in range(rows):
        tile = acc[a * FB : (a + 1) * FB, :].T
        keep[a] = tile[0:COLS].astype(jnp.bfloat16)
        send[a] = tile[COLS:BOTH].astype(jnp.bfloat16)


def cross(scal, pieces, cols):
    n = len(pieces) // 2
    rows = 20 * n
    piece = pl.BlockSpec((2, FB, CH * K), lambda i, s: (0, i, 0))
    part = pl.BlockSpec((rows, COLS, FB), lambda i, s: (0, 0, i))
    shape = jax.ShapeDtypeStruct((rows, COLS, HALF), jnp.bfloat16)
    return pl.pallas_call(
        functools.partial(cross_kernel, n),
        out_shape=(shape, shape),
        grid_spec=pltpu.PrefetchScalarGridSpec(
            num_scalar_prefetch=1,
            grid=(HALF // FB,),
            in_specs=[piece] * (2 * n + 8),
            out_specs=(part, part),
            scratch_shapes=[
                pltpu.VMEM((rows * FB, K), jnp.float32),
                pltpu.VMEM((BOTH * FB, K), jnp.float32),
                pltpu.VMEM((rows * FB, K), jnp.float32),
            ],
        ),
        compiler_params=params(),
        cost_estimate=pl.CostEstimate(flops=10**10, bytes_accessed=10**7, transcendentals=0),
        name="cross",
    )(scal, *pieces, *cols)


def lags_kernel(scal, keep, recv, near, far, *rest):
    out = rest[-1]
    total = jnp.dot(keep[...], near[0], preferred_element_type=jnp.float32)
    total += jnp.dot(recv[...], far[0], preferred_element_type=jnp.float32)
    out[...] = total.astype(jnp.bfloat16)


def lags(scal, group, keep, recv, table, prior):
    n = len(group)
    rows = 20 * COLS
    half = pl.BlockSpec((rows, HALF), lambda i, s: (i, 0))
    extra = [] if prior is None else [prior]

    def place(i, s):
        back = sum(jnp.where(i == g, d, 0) for g, d in enumerate(group))
        return lax.rem(s[2] - back + N_Z, N_Z), 0

    return pl.pallas_call(
        lags_kernel,
        out_shape=jax.ShapeDtypeStruct((N_Z * rows, LAGS), jnp.bfloat16),
        grid_spec=pltpu.PrefetchScalarGridSpec(
            num_scalar_prefetch=1,
            grid=(n,),
            in_specs=[
                half,
                half,
                pl.BlockSpec((1, HALF, LAGS), lambda i, s: (s[4], 0, 0)),
                pl.BlockSpec((1, HALF, LAGS), lambda i, s: (1 - s[4], 0, 0)),
            ]
            + [pl.BlockSpec(memory_space=pl.ANY)] * len(extra),
            out_specs=pl.BlockSpec((rows, LAGS), place),
        ),
        input_output_aliases={5: 0} if extra else {},
        compiler_params=params(),
        cost_estimate=pl.CostEstimate(flops=2 * 10**9, bytes_accessed=3 * 10**6, transcendentals=0),
        name="lags",
    )(scal, keep.reshape(n * rows, HALF), recv.reshape(n * rows, HALF), table, table, *extra)


GROUPS = ((0, 1, -1, 2, -2), (3, -3, 4))


def shards(raw_spectra, seg_valid, slot_order):
    where = [lax.axis_index(a).astype(jnp.int32) for a in ("x", "yl", "z", "yh", "c")]
    scal = jnp.concatenate([jnp.stack(where), slot_order])
    mine, other = whiten(scal, raw_spectra, seg_valid)
    got = shift(other, "c", 1)
    row = jnp.stack([mine[0], got[0]])
    col = jnp.stack([mine[1], got[1]])
    table = lag_table()

    R, C = {(0, 0): row}, {(0, 0): col}
    R[1, 0], R[-1, 0] = shift(row, "z", 1), shift(row, "z", -1)
    C[1, 0], C[-1, 0] = shift(col, "x", 1), shift(col, "x", -1)
    R[0, 1] = shift(row, "yh", 1)
    late, R[0, 1] = lax.optimization_barrier((col, R[0, 1]))
    C[0, 1] = shift(late, "yl", 1)
    R[2, 0], R[-2, 0] = shift(R[1, 0], "z", 1), shift(R[-1, 0], "z", -1)
    C[1, 1], C[-1, 1] = shift(C[0, 1], "x", 1), shift(C[0, 1], "x", -1)
    C[2, 0], C[2, 1] = shift(C[1, 0], "x", 1), shift(C[-1, 1], "x", -1)
    R[3, 0], R[-3, 0] = shift(R[2, 0], "z", 1), shift(R[-2, 0], "z", -1)
    R[4, 0] = shift(R[3, 0], "z", 1)
    for d in (1, -1, 2, -2, 3, -3, 4):
        step = 1 if d > 0 else -1
        R[d, 1] = shift(R[d, 0], "yh", 1) if d in (3, 4) else shift(R[d - step, 1], "z", step)

    cols = [C[o] for o in ORDER]
    out = None
    for g, group in enumerate(GROUPS):
        pieces = [R[d, h] for d in group for h in (0, 1)]
        if g == 0:
            pieces, _, _ = lax.optimization_barrier((pieces, R[4, 0], R[-2, 1]))
        keep, send = cross(scal, pieces, cols)
        recv = shift(send, "c", 1)
        out = lags(scal, group, keep, recv, table, out)
    return out.reshape(N_Z * 20, COLS, LAGS)


def solution(mesh):
    fine = Mesh(mesh.devices.reshape(N_X, N_YL, N_Z, N_YH, N_C), ("x", "yl", "z", "yh", "c"))
    every = ("x", "yl", "z", "yh", "c")
    return jax.shard_map(
        shards,
        mesh=fine,
        in_specs=(P(every, None, None, None), P(every, None), P(every)),
        out_specs=P(("x", "yl"), ("z", "yh", "c"), None),
        check_vma=False,
    )
```

time: 194 us -> 181 us (0.933)
  waiting for transfers between devices: 34.9 us -> 69.8 us
  Pallas kernels: 98.3 us -> 69.7 us
  other arithmetic: 9.9 us -> 0.15 us
  local copies, waits for them, and re-layouts: 10.4 us -> 4.88 us
  starting transfers between devices: 39.9 us -> 36.2 us
    ppermute x28 -> x25, waiting for transfers between devices: 34.9 us -> 69.8 us  [shift(): return lax.ppermute(x, axis, [(i, (i + step) % n) for i in range(n)])]
    pallas_call x1 -> x0, Pallas kernels: 11.2 us -> none  [columns(): pl.pallas_call(columns_kernel, out_shape=jax.ShapeDtypeStruct((HALF, BOTH...]
    pallas_call x5 -> x2, Pallas kernels: 61.9 us -> 51.4 us  [cross(): pl.pallas_call(functools.partial(cross_kernel, n), out_shape=(shape, shap...]
    pallas_call x5 -> x2, Pallas kernels: 19 us -> 13 us  [lags(): pl.pallas_call(lags_kernel, out_shape=jax.ShapeDtypeStruct((N_Z * rows, L...]
    convert_element_type x1 -> x0, other arithmetic: 4.88 us -> none  [lag_table(): (jnp.cos(angle) * jnp.float32(1.0 / math.sqrt(SEG * FREQ))).astype(jnp.bf...]
    unnamed x42 -> x34, local copies, waits for them, and re-layouts: 7.01 us -> 2.48 us
    ppermute x28 -> x25, starting transfers between devices: 39.9 us -> 36.2 us  [shift(): return lax.ppermute(x, axis, [(i, (i + step) % n) for i in range(n)])]
    another operation x6 -> x0, other arithmetic: 3.66 us -> none  [the longest x5 3.02 us: shards(): place = jnp.stack([c] + [(z - d) % N_Z for d in group])]
  transfers between devices with their start and end apart: 28 -> 25, of which waited for: 5 -> 7; matrix products, arithmetic and copies ran while one was open for 5% -> 1% of each run, Pallas kernels for 46% -> 33%
where the time goes in v2:
time: 181 us
  waiting for transfers between devices  69.8 us (39%)
  Pallas kernels  69.7 us (39%)
  starting transfers between devices  36.2 us (20%)
  local copies, waits for them, and re-layouts  4.88 us (3%)
    ppermute x25, waiting for transfers between devices, shift(): return lax.ppermute(x, axis, [(i, (i + step) % n) for i in range(n)])  69.8 us
    pallas_call x2, Pallas kernels, cross(): pl.pallas_call(functools.partial(cross_kernel, n), out_shape=(shape, shap...  51.4 us
    ppermute x25, starting transfers between devices, shift(): return lax.ppermute(x, axis, [(i, (i + step) % n) for i in range(n)])  36.2 us
    pallas_call x2, Pallas kernels, lags(): pl.pallas_call(lags_kernel, out_shape=jax.ShapeDtypeStruct((N_Z * rows, L...  13 us
    pallas_call x1, Pallas kernels, whiten(): pl.pallas_call(whiten_kernel, out_shape=(msg, msg), in_specs=[pl.BlockSpe...  5.33 us
  transfers between devices with their start and end apart: 25, of which 7 were waited for; matrix products, arithmetic and copies ran while one was open for 1% of the time, Pallas kernels for 33%

profile of v2, /device:TPU:1, one launch (start us, length us, event | category | flops | bytes accessed | tf_op | source)
XLA Modules:
  0.0 180.8 jit_solution(4608647500137928442)
XLA Ops:
  0.0 1.2 concatenate.3.scal
  1.2 5.3 %whiten.1 = (bf16[2,256,640]{2,1,0:T(8,128)(2,1)}, bf16[2,256,640]{2,1,0:T(8,128)(2,1)}) custom-call(s32[10]{0:T(128)} %concatenate.3.scal, f32[2560,128]{1,0:T(8,128)} %bitcast.19, s32[5,64]{1,0:T(8,128)} %valid.1), custom_call_target="tpu_custom_call" | custom-call | flops 1000000000 | bytes 3000000 | tf_op jit(solution)/shard_map/whiten/pallas_call | solution.py:93
  6.6 3.2 %collective-permute-start = (bf16[2,256,640]{2,1,0:T(8,128)(2,1)}, bf16[2,256,640]{2,1,0:T(8,128)(2,1)S(1)}, u32[]{:S(2)}, u32[]{:S(2)}) collective-permute-start(bf16[2,256,640]{2,1,0:T(8,128)(2,1)} %get-tuple-element.24), channel_id=1, source_target_pairs={{0,1},{1,0},{2,3},{3,2},{4,5},{5,4},{6,7},{7,6},{8,9},{9,8},{10,11... | collective-permute-start | bytes 1966088 | tf_op jit(solution)/shard_map/ppermute | solution.py:35
  9.8 1.1 fusion
  10.9 0.8 collective-permute-done
  12.0 2.8 %collective-permute-start.8 = (bf16[2,256,640]{2,1,0:T(8,128)(2,1)S(1)}, bf16[2,256,640]{2,1,0:T(8,128)(2,1)S(1)}, u32[]{:S(2)}, u32[]{:S(2)}) collective-permute-start(bf16[2,256,640]{2,1,0:T(8,128)(2,1)S(1)} %pad_maximum_fusion.refs_0_), channel_id=1, source_target_pairs={{0,2},{2,0},{1,3},{3,1},{4,6},{6,4},{5,7},{7,5},{8,10},{10,8},{9,1... | collective-permute-start | bytes 1966088 | tf_op jit(solution)/shard_map/ppermute | solution.py:35
  14.8 4.0 %collective-permute-start.5 = (bf16[2,256,640]{2,1,0:T(8,128)(2,1)S(1)}, bf16[2,256,640]{2,1,0:T(8,128)(2,1)S(1)}, u32[]{:S(2)}, u32[]{:S(2)}) collective-permute-start(bf16[2,256,640]{2,1,0:T(8,128)(2,1)S(1)} %pad_maximum_fusion.refs_0_), channel_id=1, source_target_pairs={{0,28},{4,0},{8,4},{12,8},{16,12},{20,16},{24,20},{28,24},{1,29},{... | collective-permute-start | bytes 1966088 | tf_op jit(solution)/shard_map/ppermute | solution.py:35
  18.9 11.7 %collective-permute-done.1.refs_2_ = bf16[2,256,640]{2,1,0:T(8,128)(2,1)S(1)} collective-permute-done((bf16[2,256,640]{2,1,0:T(8,128)(2,1)S(1)}, bf16[2,256,640]{2,1,0:T(8,128)(2,1)S(1)}, u32[]{:S(2)}, u32[]{:S(2)}) %collective-permute-start.1) | collective-permute-done | bytes 655392 | tf_op jit(solution)/shard_map/ppermute | solution.py:35
  30.6 1.2 collective-permute-start.15
  31.8 2.7 %collective-permute-start.9 = (bf16[2,256,640]{2,1,0:T(8,128)(2,1)S(1)}, bf16[2,256,640]{2,1,0:T(8,128)(2,1)S(1)}, u32[]{:S(2)}, u32[]{:S(2)}) collective-permute-start(bf16[2,256,640]{2,1,0:T(8,128)(2,1)S(1)} %collective-permute-done.8.refs_1_), channel_id=1, source_target_pairs={{0,28},{4,0},{8,4},{12,8},{16,12},{20,16},{24,20},{28,24},{1,29},{... | collective-permute-start | bytes 1966088 | tf_op jit(solution)/shard_map/ppermute | solution.py:35
  34.5 1.3 collective-permute-start.14
  35.8 11.4 %collective-permute-done.2.refs_6_ = bf16[2,256,640]{2,1,0:T(8,128)(2,1)S(1)} collective-permute-done((bf16[2,256,640]{2,1,0:T(8,128)(2,1)S(1)}, bf16[2,256,640]{2,1,0:T(8,128)(2,1)S(1)}, u32[]{:S(2)}, u32[]{:S(2)}) %collective-permute-start.2) | collective-permute-done | bytes 655392 | tf_op jit(solution)/shard_map/ppermute | solution.py:35
  47.2 2.7 %collective-permute-start.6 = (bf16[2,256,640]{2,1,0:T(8,128)(2,1)S(1)}, bf16[2,256,640]{2,1,0:T(8,128)(2,1)}, u32[]{:S(2)}, u32[]{:S(2)}) collective-permute-start(bf16[2,256,640]{2,1,0:T(8,128)(2,1)S(1)} %collective-permute-done.5.refs_4_), channel_id=1, source_target_pairs={{0,28},{4,0},{8,4},{12,8},{16,12},{20,16},{24,20},{28,24},{1,29},{... | collective-permute-start | bytes 1966088 | tf_op jit(solution)/shard_map/ppermute | solution.py:35
  49.9 0.6 collective-permute-start.10
  50.5 2.0 %collective-permute-start.18 = (bf16[2,256,640]{2,1,0:T(8,128)(2,1)S(1)}, bf16[2,256,640]{2,1,0:T(8,128)(2,1)S(1)}, u32[]{:S(2)}, u32[]{:S(2)}) collective-permute-start(bf16[2,256,640]{2,1,0:T(8,128)(2,1)S(1)} %collective-permute-done.14.refs_7_.refs_11_), channel_id=1, source_target_pairs={{0,192},{64,0},{128,64},{192,128},{1,193},{65,1},{129,65},{193,129... | collective-permute-start | bytes 1966088 | tf_op jit(solution)/shard_map/ppermute | solution.py:35
  52.4 8.8 %collective-permute-done.22.refs_3_ = bf16[2,256,640]{2,1,0:T(8,128)(2,1)S(1)} collective-permute-done((bf16[2,256,640]{2,1,0:T(8,128)(2,1)S(1)}, bf16[2,256,640]{2,1,0:T(8,128)(2,1)S(1)}, u32[]{:S(2)}, u32[]{:S(2)}) %collective-permute-start.22) | collective-permute-done | bytes 655392 | tf_op jit(solution)/shard_map/ppermute | solution.py:35
  61.2 14.1 %collective-permute-done.3.refs_0_ = bf16[2,256,640]{2,1,0:T(8,128)(2,1)} collective-permute-done((bf16[2,256,640]{2,1,0:T(8,128)(2,1)S(1)}, bf16[2,256,640]{2,1,0:T(8,128)(2,1)}, u32[]{:S(2)}, u32[]{:S(2)}) %collective-permute-start.3) | collective-permute-done | bytes 655392 | tf_op jit(solution)/shard_map/ppermute | solution.py:35
  75.4 2.5 %collective-permute-start.17 = (bf16[2,256,640]{2,1,0:T(8,128)(2,1)S(1)}, bf16[2,256,640]{2,1,0:T(8,128)(2,1)S(1)}, u32[]{:S(2)}, u32[]{:S(2)}) collective-permute-start(bf16[2,256,640]{2,1,0:T(8,128)(2,1)S(1)} %pad_maximum_fusion.1.refs_6_.refs_10_), channel_id=1, source_target_pairs={{0,192},{64,0},{128,64},{192,128},{1,193},{65,1},{129,65},{193,129... | collective-permute-start | bytes 1966088 | tf_op jit(solution)/shard_map/ppermute | solution.py:35
  77.9 0.2 collective-permute-start.16
  78.1 11.2 %collective-permute-done.23.refs_7_ = bf16[2,256,640]{2,1,0:T(8,128)(2,1)S(1)} collective-permute-done((bf16[2,256,640]{2,1,0:T(8,128)(2,1)S(1)}, bf16[2,256,640]{2,1,0:T(8,128)(2,1)S(1)}, u32[]{:S(2)}, u32[]{:S(2)}) %collective-permute-start.23) | collective-permute-done | bytes 655392 | tf_op jit(solution)/shard_map/ppermute | solution.py:35
  89.3 2.5 %collective-permute-start.20 = (bf16[2,256,640]{2,1,0:T(8,128)(2,1)S(1)}, bf16[2,256,640]{2,1,0:T(8,128)(2,1)}, u32[]{:S(2)}, u32[]{:S(2)}) collective-permute-start(bf16[2,256,640]{2,1,0:T(8,128)(2,1)S(1)} %collective-permute-done.18.refs_11_.refs_15_), channel_id=1, source_target_pairs={{0,192},{64,0},{128,64},{192,128},{1,193},{65,1},{129,65},{193,129... | collective-permute-start | bytes 1966088 | tf_op jit(solution)/shard_map/ppermute | solution.py:35
  91.8 11.7 %collective-permute-done.12.refs_4_ = bf16[2,256,640]{2,1,0:T(8,128)(2,1)} collective-permute-done((bf16[2,256,640]{2,1,0:T(8,128)(2,1)}, bf16[2,256,640]{2,1,0:T(8,128)(2,1)}, u32[]{:S(2)}, u32[]{:S(2)}) %collective-permute-start.12) | collective-permute-done | bytes 655392 | tf_op jit(solution)/shard_map/ppermute | solution.py:35
  103.5 3.0 %collective-permute-start.4 = (bf16[2,256,640]{2,1,0:T(8,128)(2,1)}, bf16[2,256,640]{2,1,0:T(8,128)(2,1)}, u32[]{:S(2)}, u32[]{:S(2)}) collective-permute-start(bf16[2,256,640]{2,1,0:T(8,128)(2,1)} %collective-permute-done.3.refs_0_), channel_id=1, source_target_pairs={{0,2},{2,0},{1,3},{3,1},{4,6},{6,4},{5,7},{7,5},{8,10},{10,8},{9,1... | collective-permute-start | bytes 1966088 | tf_op jit(solution)/shard_map/ppermute | solution.py:35
  106.5 0.2 collective-permute-start.11
  106.7 2.1 %collective-permute-start.13 = (bf16[2,256,640]{2,1,0:T(8,128)(2,1)}, bf16[2,256,640]{2,1,0:T(8,128)(2,1)}, u32[]{:S(2)}, u32[]{:S(2)}) collective-permute-start(bf16[2,256,640]{2,1,0:T(8,128)(2,1)} %collective-permute-done.12.refs_4_), channel_id=1, source_target_pairs={{0,2},{2,0},{1,3},{3,1},{4,6},{6,4},{5,7},{7,5},{8,10},{10,8},{9,1... | collective-permute-start | bytes 1966088 | tf_op jit(solution)/shard_map/ppermute | solution.py:35
  108.9 29.7 %cross.3 = (bf16[100,40,256]{2,1,0:T(8,128)(2,1)}, bf16[100,40,256]{2,1,0:T(8,128)(2,1)}) custom-call(s32[10]{0:T(128)} %concatenate.3.scal, bf16[2,256,640]{2,1,0:T(8,128)(2,1)} %copy-done.3, bf16[2,256,640]{2,1,0:T(8,128)(2,1)} %copy-done.6, bf16[2,256,640]{2,1,0:T(8,128)(2,1)} %copy-done.5, bf16[2,256,640]{2,1,0:T(8,128)(2,1)} %copy-done.11, ...), custom_call_target="tpu_custom_call" | custom-call | flops 10000000000 | bytes 10000000 | tf_op jit(solution)/shard_map/cross/pallas_call | solution.py:160
  138.6 5.0 %collective-permute-start.24 = (bf16[100,40,256]{2,1,0:T(8,128)(2,1)}, bf16[100,40,256]{2,1,0:T(8,128)(2,1)S(1)}, u32[]{:S(2)}, u32[]{:S(2)}) collective-permute-start(bf16[100,40,256]{2,1,0:T(8,128)(2,1)} %get-tuple-element.40), channel_id=1, source_target_pairs={{0,1},{1,0},{2,3},{3,2},{4,5},{5,4},{6,7},{7,6},{8,9},{9,8},{10,11... | collective-permute-start | bytes 6144008 | tf_op jit(solution)/shard_map/ppermute | solution.py:35
  143.6 21.7 %cross.2 = (bf16[60,40,256]{2,1,0:T(8,128)(2,1)}, bf16[60,40,256]{2,1,0:T(8,128)(2,1)}) custom-call(s32[10]{0:T(128)} %concatenate.3.scal, bf16[2,256,640]{2,1,0:T(8,128)(2,1)} %collective-permute-done.3.refs_0_, bf16[2,256,640]{2,1,0:T(8,128)(2,1)} %collective-permute-done.4.refs_1_, bf16[2,256,640]{2,1,0:T(8,128)(2,1)} %collective-permute-done.7.refs_2_, ...), custom_call_target="tpu_custom_call" | custom-call | flops 10000000000 | bytes 10000000 | tf_op jit(solution)/shard_map/cross/pallas_call | solution.py:160
  165.4 1.3 copy-done
  166.7 7.5 %lags.2.rest_0_ = bf16[6400,512]{1,0:T(8,128)(2,1)} custom-call(s32[10]{0:T(128)} %concatenate.3.scal, bf16[4000,256]{1,0:T(8,128)(2,1)} %bitcast.15, bf16[4000,256]{1,0:T(8,128)(2,1)} %bitcast.16, bf16[2,256,512]{2,1,0:T(8,128)(2,1)} %constant.28.near.far, bf16[2,256,512]{2,1,0:T(8,128)(2,1)} %constant.28.near.far), custom_call_target="tpu_custom_call" | custom-call | flops 2000000000 | bytes 3000000 | tf_op jit(solution)/shard_map/lags/pallas_call | solution.py:197
  174.3 1.1 copy-done.1
  175.4 5.5 %lags.3 = bf16[6400,512]{1,0:T(8,128)(2,1)} custom-call(s32[10]{0:T(128)} %concatenate.3.scal, bf16[2400,256]{1,0:T(8,128)(2,1)} %bitcast.17, bf16[2400,256]{1,0:T(8,128)(2,1)} %bitcast.18, bf16[2,256,512]{2,1,0:T(8,128)(2,1)} %constant.28.near.far, bf16[2,256,512]{2,1,0:T(8,128)(2,1)} %constant.28.near.far, ...), custom_call_target="tpu_custom_call", output_to_operand_aliasing={{}: (5, {})} | custom-call | flops 2000000000 | bytes 3000000 | tf_op jit(solution)/shard_map/lags/pallas_call | solution.py:197
  (62 shorter events, 0.5 us)
Async XLA Ops:
  6.6 5.2 %collective-permute-start = (bf16[2,256,640]{2,1,0:T(8,128)(2,1)}, bf16[2,256,640]{2,1,0:T(8,128)(2,1)S(1)}, u32[]{:S(2)}, u32[]{:S(2)}) collective-permute-start(bf16[2,256,640]{2,1,0:T(8,128)(2,1)} %get-tuple-element.24), channel_id=1, source_target_pairs={{0,1},{1,0},{2,3},{3,2},{4,5},{5,4},{6,7},{7,6},{8,9},{9,8},{10,11... | collective-permute-start | bytes 1966088 | tf_op jit(solution)/shard_map/ppermute | solution.py:35
  11.9 97.0 %copy-start.3 = (bf16[2,256,640]{2,1,0:T(8,128)(2,1)}, bf16[2,256,640]{2,1,0:T(8,128)(2,1)S(1)}, u32[]{:S(2)}) copy-start(bf16[2,256,640]{2,1,0:T(8,128)(2,1)S(1)} %pad_maximum_fusion.refs_0_) | copy-start | bytes 1966084
  11.9 18.7 %collective-permute-start.1 = (bf16[2,256,640]{2,1,0:T(8,128)(2,1)S(1)}, bf16[2,256,640]{2,1,0:T(8,128)(2,1)S(1)}, u32[]{:S(2)}, u32[]{:S(2)}) collective-permute-start(bf16[2,256,640]{2,1,0:T(8,128)(2,1)S(1)} %pad_maximum_fusion.refs_0_), channel_id=1, source_target_pairs={{0,4},{4,8},{8,12},{12,16},{16,20},{20,24},{24,28},{28,0},{1,5},{5... | collective-permute-start | bytes 1966088 | tf_op jit(solution)/shard_map/ppermute | solution.py:35
  12.0 19.9 %collective-permute-start.8 = (bf16[2,256,640]{2,1,0:T(8,128)(2,1)S(1)}, bf16[2,256,640]{2,1,0:T(8,128)(2,1)S(1)}, u32[]{:S(2)}, u32[]{:S(2)}) collective-permute-start(bf16[2,256,640]{2,1,0:T(8,128)(2,1)S(1)} %pad_maximum_fusion.refs_0_), channel_id=1, source_target_pairs={{0,2},{2,0},{1,3},{3,1},{4,6},{6,4},{5,7},{7,5},{8,10},{10,8},{9,1... | collective-permute-start | bytes 1966088 | tf_op jit(solution)/shard_map/ppermute | solution.py:35
  14.8 21.0 %collective-permute-start.5 = (bf16[2,256,640]{2,1,0:T(8,128)(2,1)S(1)}, bf16[2,256,640]{2,1,0:T(8,128)(2,1)S(1)}, u32[]{:S(2)}, u32[]{:S(2)}) collective-permute-start(bf16[2,256,640]{2,1,0:T(8,128)(2,1)S(1)} %pad_maximum_fusion.refs_0_), channel_id=1, source_target_pairs={{0,28},{4,0},{8,4},{12,8},{16,12},{20,16},{24,20},{28,24},{1,29},{... | collective-permute-start | bytes 1966088 | tf_op jit(solution)/shard_map/ppermute | solution.py:35
  18.9 90.0 %copy-start.2 = (bf16[2,256,640]{2,1,0:T(8,128)(2,1)}, bf16[2,256,640]{2,1,0:T(8,128)(2,1)S(1)}, u32[]{:S(2)}) copy-start(bf16[2,256,640]{2,1,0:T(8,128)(2,1)S(1)} %pad_maximum_fusion.1.refs_6_.refs_10_) | copy-start | bytes 1966084
  30.6 78.3 %copy-start.5 = (bf16[2,256,640]{2,1,0:T(8,128)(2,1)}, bf16[2,256,640]{2,1,0:T(8,128)(2,1)S(1)}, u32[]{:S(2)}) copy-start(bf16[2,256,640]{2,1,0:T(8,128)(2,1)S(1)} %collective-permute-done.1.refs_2_) | copy-start | bytes 1966084
  30.6 16.6 %collective-permute-start.2 = (bf16[2,256,640]{2,1,0:T(8,128)(2,1)S(1)}, bf16[2,256,640]{2,1,0:T(8,128)(2,1)S(1)}, u32[]{:S(2)}, u32[]{:S(2)}) collective-permute-start(bf16[2,256,640]{2,1,0:T(8,128)(2,1)S(1)} %collective-permute-done.1.refs_2_), channel_id=1, source_target_pairs={{0,4},{4,8},{8,12},{12,16},{16,20},{20,24},{24,28},{28,0},{1,5},{5... | collective-permute-start | bytes 1966088 | tf_op jit(solution)/shard_map/ppermute | solution.py:35
  30.6 16.6 %collective-permute-start.15 = (bf16[2,256,640]{2,1,0:T(8,128)(2,1)S(1)}, bf16[2,256,640]{2,1,0:T(8,128)(2,1)S(1)}, u32[]{:S(2)}, u32[]{:S(2)}) collective-permute-start(bf16[2,256,640]{2,1,0:T(8,128)(2,1)S(1)} %pad_maximum_fusion.1.refs_6_.refs_10_), channel_id=1, source_target_pairs={{0,64},{64,128},{128,192},{192,0},{1,65},{65,129},{129,193},{193,1... | collective-permute-start | bytes 1966088 | tf_op jit(solution)/shard_map/ppermute | solution.py:35
  31.8 77.1 %copy-start.6 = (bf16[2,256,640]{2,1,0:T(8,128)(2,1)}, bf16[2,256,640]{2,1,0:T(8,128)(2,1)S(1)}, u32[]{:S(2)}) copy-start(bf16[2,256,640]{2,1,0:T(8,128)(2,1)S(1)} %collective-permute-done.8.refs_1_) | copy-start | bytes 1966084
  31.8 18.0 %collective-permute-start.9 = (bf16[2,256,640]{2,1,0:T(8,128)(2,1)S(1)}, bf16[2,256,640]{2,1,0:T(8,128)(2,1)S(1)}, u32[]{:S(2)}, u32[]{:S(2)}) collective-permute-start(bf16[2,256,640]{2,1,0:T(8,128)(2,1)S(1)} %collective-permute-done.8.refs_1_), channel_id=1, source_target_pairs={{0,28},{4,0},{8,4},{12,8},{16,12},{20,16},{24,20},{28,24},{1,29},{... | collective-permute-start | bytes 1966088 | tf_op jit(solution)/shard_map/ppermute | solution.py:35
  34.5 16.0 %collective-permute-start.14 = (bf16[2,256,640]{2,1,0:T(8,128)(2,1)S(1)}, bf16[2,256,640]{2,1,0:T(8,128)(2,1)S(1)}, u32[]{:S(2)}, u32[]{:S(2)}) collective-permute-start(bf16[2,256,640]{2,1,0:T(8,128)(2,1)S(1)} %pad_maximum_fusion.1.refs_6_.refs_10_), channel_id=1, source_target_pairs={{0,32},{32,0},{1,33},{33,1},{2,34},{34,2},{3,35},{35,3},{4,36},{36... | collective-permute-start | bytes 1966088 | tf_op jit(solution)/shard_map/ppermute | solution.py:35
  35.8 70.9 %copy-start.8 = (bf16[2,256,640]{2,1,0:T(8,128)(2,1)}, bf16[2,256,640]{2,1,0:T(8,128)(2,1)S(1)}, u32[]{:S(2)}) copy-start(bf16[2,256,640]{2,1,0:T(8,128)(2,1)S(1)} %collective-permute-done.5.refs_4_) | copy-start | bytes 1966084
  35.8 25.4 %collective-permute-start.22 = (bf16[2,256,640]{2,1,0:T(8,128)(2,1)S(1)}, bf16[2,256,640]{2,1,0:T(8,128)(2,1)S(1)}, u32[]{:S(2)}, u32[]{:S(2)}) collective-permute-start(bf16[2,256,640]{2,1,0:T(8,128)(2,1)S(1)} %collective-permute-done.8.refs_1_), channel_id=1, source_target_pairs={{0,4},{4,8},{8,12},{12,16},{16,20},{20,24},{24,28},{28,0},{1,5},{5... | collective-permute-start | bytes 1966088 | tf_op jit(solution)/shard_map/ppermute | solution.py:35
  47.2 61.6 %copy-start.9 = (bf16[2,256,640]{2,1,0:T(8,128)(2,1)}, bf16[2,256,640]{2,1,0:T(8,128)(2,1)S(1)}, u32[]{:S(2)}) copy-start(bf16[2,256,640]{2,1,0:T(8,128)(2,1)S(1)} %collective-permute-done.2.refs_6_) | copy-start | bytes 1966084
  47.2 28.2 %collective-permute-start.3 = (bf16[2,256,640]{2,1,0:T(8,128)(2,1)S(1)}, bf16[2,256,640]{2,1,0:T(8,128)(2,1)}, u32[]{:S(2)}, u32[]{:S(2)}) collective-permute-start(bf16[2,256,640]{2,1,0:T(8,128)(2,1)S(1)} %collective-permute-done.2.refs_6_), channel_id=1, source_target_pairs={{0,4},{4,8},{8,12},{12,16},{16,20},{20,24},{24,28},{28,0},{1,5},{5... | collective-permute-start | bytes 1966088 | tf_op jit(solution)/shard_map/ppermute | solution.py:35
  47.2 61.7 %copy-start.4 = (bf16[2,256,640]{2,1,0:T(8,128)(2,1)}, bf16[2,256,640]{2,1,0:T(8,128)(2,1)S(1)}, u32[]{:S(2)}) copy-start(bf16[2,256,640]{2,1,0:T(8,128)(2,1)S(1)} %collective-permute-done.15.refs_8_.refs_12_) | copy-start | bytes 1966084
  47.2 28.2 %collective-permute-start.6 = (bf16[2,256,640]{2,1,0:T(8,128)(2,1)S(1)}, bf16[2,256,640]{2,1,0:T(8,128)(2,1)}, u32[]{:S(2)}, u32[]{:S(2)}) collective-permute-start(bf16[2,256,640]{2,1,0:T(8,128)(2,1)S(1)} %collective-permute-done.5.refs_4_), channel_id=1, source_target_pairs={{0,28},{4,0},{8,4},{12,8},{16,12},{20,16},{24,20},{28,24},{1,29},{... | collective-permute-start | bytes 1966088 | tf_op jit(solution)/shard_map/ppermute | solution.py:35
  49.9 28.0 %collective-permute-start.10 = (bf16[2,256,640]{2,1,0:T(8,128)(2,1)S(1)}, bf16[2,256,640]{2,1,0:T(8,128)(2,1)}, u32[]{:S(2)}, u32[]{:S(2)}) collective-permute-start(bf16[2,256,640]{2,1,0:T(8,128)(2,1)S(1)} %collective-permute-done.9.refs_5_), channel_id=1, source_target_pairs={{0,28},{4,0},{8,4},{12,8},{16,12},{20,16},{24,20},{28,24},{1,29},{... | collective-permute-start | bytes 1966088 | tf_op jit(solution)/shard_map/ppermute | solution.py:35
  50.5 27.4 %collective-permute-start.18 = (bf16[2,256,640]{2,1,0:T(8,128)(2,1)S(1)}, bf16[2,256,640]{2,1,0:T(8,128)(2,1)S(1)}, u32[]{:S(2)}, u32[]{:S(2)}) collective-permute-start(bf16[2,256,640]{2,1,0:T(8,128)(2,1)S(1)} %collective-permute-done.14.refs_7_.refs_11_), channel_id=1, source_target_pairs={{0,192},{64,0},{128,64},{192,128},{1,193},{65,1},{129,65},{193,129... | collective-permute-start | bytes 1966088 | tf_op jit(solution)/shard_map/ppermute | solution.py:35
  61.2 28.1 %collective-permute-start.23 = (bf16[2,256,640]{2,1,0:T(8,128)(2,1)S(1)}, bf16[2,256,640]{2,1,0:T(8,128)(2,1)S(1)}, u32[]{:S(2)}, u32[]{:S(2)}) collective-permute-start(bf16[2,256,640]{2,1,0:T(8,128)(2,1)S(1)} %collective-permute-done.22.refs_3_), channel_id=1, source_target_pairs={{0,4},{4,8},{8,12},{12,16},{16,20},{20,24},{24,28},{28,0},{1,5},{5... | collective-permute-start | bytes 1966088 | tf_op jit(solution)/shard_map/ppermute | solution.py:35
  75.4 28.1 %collective-permute-start.12 = (bf16[2,256,640]{2,1,0:T(8,128)(2,1)}, bf16[2,256,640]{2,1,0:T(8,128)(2,1)}, u32[]{:S(2)}, u32[]{:S(2)}) collective-permute-start(bf16[2,256,640]{2,1,0:T(8,128)(2,1)} %collective-permute-done.3.refs_0_), channel_id=1, source_target_pairs={{0,4},{4,8},{8,12},{12,16},{16,20},{20,24},{24,28},{28,0},{1,5},{5... | collective-permute-start | bytes 1966088 | tf_op jit(solution)/shard_map/ppermute | solution.py:35
  75.4 28.1 %collective-permute-start.17 = (bf16[2,256,640]{2,1,0:T(8,128)(2,1)S(1)}, bf16[2,256,640]{2,1,0:T(8,128)(2,1)S(1)}, u32[]{:S(2)}, u32[]{:S(2)}) collective-permute-start(bf16[2,256,640]{2,1,0:T(8,128)(2,1)S(1)} %pad_maximum_fusion.1.refs_6_.refs_10_), channel_id=1, source_target_pairs={{0,192},{64,0},{128,64},{192,128},{1,193},{65,1},{129,65},{193,129... | collective-permute-start | bytes 1966088 | tf_op jit(solution)/shard_map/ppermute | solution.py:35
  77.9 28.6 %collective-permute-start.19 = (bf16[2,256,640]{2,1,0:T(8,128)(2,1)S(1)}, bf16[2,256,640]{2,1,0:T(8,128)(2,1)S(1)}, u32[]{:S(2)}, u32[]{:S(2)}) collective-permute-start(bf16[2,256,640]{2,1,0:T(8,128)(2,1)S(1)} %collective-permute-done.15.refs_8_.refs_12_), channel_id=1, source_target_pairs={{0,64},{64,128},{128,192},{192,0},{1,65},{65,129},{129,193},{193,1... | collective-permute-start | bytes 1966088 | tf_op jit(solution)/shard_map/ppermute | solution.py:35
  77.9 28.8 %collective-permute-start.16 = (bf16[2,256,640]{2,1,0:T(8,128)(2,1)S(1)}, bf16[2,256,640]{2,1,0:T(8,128)(2,1)S(1)}, u32[]{:S(2)}, u32[]{:S(2)}) collective-permute-start(bf16[2,256,640]{2,1,0:T(8,128)(2,1)S(1)} %collective-permute-done.14.refs_7_.refs_11_), channel_id=1, source_target_pairs={{0,64},{64,128},{128,192},{192,0},{1,65},{65,129},{129,193},{193,1... | collective-permute-start | bytes 1966088 | tf_op jit(solution)/shard_map/ppermute | solution.py:35
  89.3 19.6 %collective-permute-start.20 = (bf16[2,256,640]{2,1,0:T(8,128)(2,1)S(1)}, bf16[2,256,640]{2,1,0:T(8,128)(2,1)}, u32[]{:S(2)}, u32[]{:S(2)}) collective-permute-start(bf16[2,256,640]{2,1,0:T(8,128)(2,1)S(1)} %collective-permute-done.18.refs_11_.refs_15_), channel_id=1, source_target_pairs={{0,192},{64,0},{128,64},{192,128},{1,193},{65,1},{129,65},{193,129... | collective-permute-start | bytes 1966088 | tf_op jit(solution)/shard_map/ppermute | solution.py:35
  103.5 40.1 %collective-permute-start.7 = (bf16[2,256,640]{2,1,0:T(8,128)(2,1)}, bf16[2,256,640]{2,1,0:T(8,128)(2,1)}, u32[]{:S(2)}, u32[]{:S(2)}) collective-permute-start(bf16[2,256,640]{2,1,0:T(8,128)(2,1)} %collective-permute-done.6.refs_8_), channel_id=1, source_target_pairs={{0,28},{4,0},{8,4},{12,8},{16,12},{20,16},{24,20},{28,24},{1,29},{... | collective-permute-start | bytes 1966088 | tf_op jit(solution)/shard_map/ppermute | solution.py:35
  103.5 40.1 %collective-permute-start.4 = (bf16[2,256,640]{2,1,0:T(8,128)(2,1)}, bf16[2,256,640]{2,1,0:T(8,128)(2,1)}, u32[]{:S(2)}, u32[]{:S(2)}) collective-permute-start(bf16[2,256,640]{2,1,0:T(8,128)(2,1)} %collective-permute-done.3.refs_0_), channel_id=1, source_target_pairs={{0,2},{2,0},{1,3},{3,1},{4,6},{6,4},{5,7},{7,5},{8,10},{10,8},{9,1... | collective-permute-start | bytes 1966088 | tf_op jit(solution)/shard_map/ppermute | solution.py:35
  106.5 37.1 %collective-permute-start.11 = (bf16[2,256,640]{2,1,0:T(8,128)(2,1)}, bf16[2,256,640]{2,1,0:T(8,128)(2,1)}, u32[]{:S(2)}, u32[]{:S(2)}) collective-permute-start(bf16[2,256,640]{2,1,0:T(8,128)(2,1)} %collective-permute-done.10.refs_9_), channel_id=1, source_target_pairs={{0,28},{4,0},{8,4},{12,8},{16,12},{20,16},{24,20},{28,24},{1,29},{... | collective-permute-start | bytes 1966088 | tf_op jit(solution)/shard_map/ppermute | solution.py:35
  106.7 36.9 %collective-permute-start.13 = (bf16[2,256,640]{2,1,0:T(8,128)(2,1)}, bf16[2,256,640]{2,1,0:T(8,128)(2,1)}, u32[]{:S(2)}, u32[]{:S(2)}) collective-permute-start(bf16[2,256,640]{2,1,0:T(8,128)(2,1)} %collective-permute-done.12.refs_4_), channel_id=1, source_target_pairs={{0,2},{2,0},{1,3},{3,1},{4,6},{6,4},{5,7},{7,5},{8,10},{10,8},{9,1... | collective-permute-start | bytes 1966088 | tf_op jit(solution)/shard_map/ppermute | solution.py:35
  138.6 26.8 %collective-permute-start.24 = (bf16[100,40,256]{2,1,0:T(8,128)(2,1)}, bf16[100,40,256]{2,1,0:T(8,128)(2,1)S(1)}, u32[]{:S(2)}, u32[]{:S(2)}) collective-permute-start(bf16[100,40,256]{2,1,0:T(8,128)(2,1)} %get-tuple-element.40), channel_id=1, source_target_pairs={{0,1},{1,0},{2,3},{3,2},{4,5},{5,4},{6,7},{7,6},{8,9},{9,8},{10,11... | collective-permute-start | bytes 6144008 | tf_op jit(solution)/shard_map/ppermute | solution.py:35
  165.3 9.0 %collective-permute-start.21 = (bf16[60,40,256]{2,1,0:T(8,128)(2,1)}, bf16[60,40,256]{2,1,0:T(8,128)(2,1)S(1)}, u32[]{:S(2)}, u32[]{:S(2)}) collective-permute-start(bf16[60,40,256]{2,1,0:T(8,128)(2,1)} %get-tuple-element.28), channel_id=1, source_target_pairs={{0,1},{1,0},{2,3},{3,2},{4,5},{5,4},{6,7},{7,6},{8,9},{9,8},{10,11... | collective-permute-start | bytes 3686408 | tf_op jit(solution)/shard_map/ppermute | solution.py:35
  (10 other events, 227.8 us)

commit v3 on v2

--- a/solution.py
+++ b/solution.py
@@ -105,55 +105,56 @@
     )(scal, view, valid)
 
 
-ORDER = [(dx, dy) for dx in (0, 1, -1, 2) for dy in (0, 1)]
 UNROLL = 16
+PITCH = FB + 8
+STEPS = (0, 1, -1, 2)
 
 
 def cross_kernel(n, scal, *refs):
-    rows = 20 * n
-    pieces, cols = refs[: 2 * n], refs[2 * n : 2 * n + 8]
-    keep, send, flat, side, acc = refs[2 * n + 8 :]
-    x, yl, yh, c = scal[0], scal[1], scal[3], scal[4]
-
-    def spread(piece, q, into, base):
+    rows = 10 * n
+    pieces, cols = refs[:n], refs[n : n + 8]
+    keep, send, flat, side, acc = refs[n + 8 :]
+    x, yl, c = scal[0], scal[1], scal[4]
+
+    def spread(piece, into, base):
         for k in range(CH):
-            at = pl.multiple_of((base + k) * FB, FB)
-            into[pl.ds(at, FB), :] = piece[q, :, k * K : (k + 1) * K].astype(jnp.float32)
-
-    for p in range(8):
-        dx, dy = ORDER[p]
-        r = lax.rem(x - dx + N_X, N_X) * N_YL + (yl ^ dy)
+            at = pl.multiple_of((base + k) * PITCH, 8)
+            into[pl.ds(at, FB), :] = piece[:, k * K : (k + 1) * K].astype(jnp.float32)
+
+    for p in range(4):
+        for h in range(2):
+            r = lax.rem(x - STEPS[p] + N_X, N_X) * N_YL + (yl ^ h)
+            for q in range(2):
+                spread(cols[2 * p + h].at[q], side, q * COLS + r * CH)
+    for p in range(n):
         for q in range(2):
-            spread(cols[p], q, side, q * COLS + r * CH)
-    for p in range(2 * n):
-        for q in range(2):
-            spread(pieces[p], q, flat, (p // 2) * 20 + (yh ^ (p % 2)) * 10 + (c ^ q) * 5)
+            spread(pieces[p].at[q], flat, p * 10 + (c ^ q) * 5)
 
     def body(i, carry):
         at = [i * UNROLL + u for u in range(UNROLL)]
         pairs = []
         for f in at:
-            first = flat[pl.ds(f, rows, stride=FB), :].astype(jnp.bfloat16)
-            second = side[pl.ds(f, BOTH, stride=FB), :].astype(jnp.bfloat16)
+            first = flat[pl.ds(f, rows, stride=PITCH), :].astype(jnp.bfloat16)
+            second = side[pl.ds(f, BOTH, stride=PITCH), :].astype(jnp.bfloat16)
             pairs.append(
                 lax.dot_general(
                     first, second, (((1,), (1,)), ((), ())), preferred_element_type=jnp.float32
                 )
             )
         for f, pair in zip(at, pairs):
-            acc[pl.ds(f, rows, stride=FB), 0:BOTH] = pair
+            acc[pl.ds(f, rows, stride=PITCH), 0:BOTH] = pair
         return carry
 
     lax.fori_loop(0, FB // UNROLL, body, 0)
     for a in range(rows):
-        tile = acc[a * FB : (a + 1) * FB, :].T
+        tile = acc[a * PITCH : a * PITCH + FB, :].T
         keep[a] = tile[0:COLS].astype(jnp.bfloat16)
         send[a] = tile[COLS:BOTH].astype(jnp.bfloat16)
 
 
 def cross(scal, pieces, cols):
-    n = len(pieces) // 2
-    rows = 20 * n
+    n = len(pieces)
+    rows = 10 * n
     piece = pl.BlockSpec((2, FB, CH * K), lambda i, s: (0, i, 0))
     part = pl.BlockSpec((rows, COLS, FB), lambda i, s: (0, 0, i))
     shape = jax.ShapeDtypeStruct((rows, COLS, HALF), jnp.bfloat16)
@@ -163,12 +164,12 @@
         grid_spec=pltpu.PrefetchScalarGridSpec(
             num_scalar_prefetch=1,
             grid=(HALF // FB,),
-            in_specs=[piece] * (2 * n + 8),
+            in_specs=[piece] * (n + 8),
             out_specs=(part, part),
             scratch_shapes=[
-                pltpu.VMEM((rows * FB, K), jnp.float32),
-                pltpu.VMEM((BOTH * FB, K), jnp.float32),
-                pltpu.VMEM((rows * FB, K), jnp.float32),
+                pltpu.VMEM((rows * PITCH, K), jnp.float32),
+                pltpu.VMEM((BOTH * PITCH, K), jnp.float32),
+                pltpu.VMEM((rows * PITCH, K), jnp.float32),
             ],
         ),
         compiler_params=params(),
@@ -178,25 +179,26 @@
 
 
 def lags_kernel(scal, keep, recv, near, far, *rest):
-    out = rest[-1]
-    total = jnp.dot(keep[...], near[0], preferred_element_type=jnp.float32)
-    total += jnp.dot(recv[...], far[0], preferred_element_type=jnp.float32)
-    out[...] = total.astype(jnp.bfloat16)
+    both = jnp.concatenate([keep[...], recv[...]], axis=1)
+    table = jnp.concatenate([near[0], far[0]], axis=0)
+    total = jnp.dot(both, table, preferred_element_type=jnp.float32)
+    rest[-1][...] = total.astype(jnp.bfloat16)
 
 
 def lags(scal, group, keep, recv, table, prior):
     n = len(group)
-    rows = 20 * COLS
+    rows = 10 * COLS
     half = pl.BlockSpec((rows, HALF), lambda i, s: (i, 0))
     extra = [] if prior is None else [prior]
 
     def place(i, s):
-        back = sum(jnp.where(i == g, d, 0) for g, d in enumerate(group))
-        return lax.rem(s[2] - back + N_Z, N_Z), 0
+        back = sum(jnp.where(i == g, d, 0) for g, (d, _) in enumerate(group))
+        side = sum(jnp.where(i == g, h, 0) for g, (_, h) in enumerate(group))
+        return lax.rem(s[2] - back + N_Z, N_Z) * N_YH + (s[3] ^ side), 0
 
     return pl.pallas_call(
         lags_kernel,
-        out_shape=jax.ShapeDtypeStruct((N_Z * rows, LAGS), jnp.bfloat16),
+        out_shape=jax.ShapeDtypeStruct((N_Z * N_YH * rows, LAGS), jnp.bfloat16),
         grid_spec=pltpu.PrefetchScalarGridSpec(
             num_scalar_prefetch=1,
             grid=(n,),
@@ -216,7 +218,16 @@
     )(scal, keep.reshape(n * rows, HALF), recv.reshape(n * rows, HALF), table, table, *extra)
 
 
-GROUPS = ((0, 1, -1, 2, -2), (3, -3, 4))
+OWN = tuple((d, 0) for d in (0, 1, -1, 2, -2, 3, -3))
+GROUPS = (
+    OWN + ((1, 1), (-1, 1)),
+    ((0, 1), (-2, 1), (4, 0), (2, 1), (-3, 1)),
+    ((3, 1), (4, 1)),
+)
+
+
+def after(value, *earlier):
+    return lax.optimization_barrier((value, earlier))[0]
 
 
 def shards(raw_spectra, seg_valid, slot_order):
@@ -230,28 +241,36 @@
 
     R, C = {(0, 0): row}, {(0, 0): col}
     R[1, 0], R[-1, 0] = shift(row, "z", 1), shift(row, "z", -1)
+    C[0, 1] = shift(col, "yl", 1)
     C[1, 0], C[-1, 0] = shift(col, "x", 1), shift(col, "x", -1)
-    R[0, 1] = shift(row, "yh", 1)
-    late, R[0, 1] = lax.optimization_barrier((col, R[0, 1]))
-    C[0, 1] = shift(late, "yl", 1)
-    R[2, 0], R[-2, 0] = shift(R[1, 0], "z", 1), shift(R[-1, 0], "z", -1)
-    C[1, 1], C[-1, 1] = shift(C[0, 1], "x", 1), shift(C[0, 1], "x", -1)
-    C[2, 0], C[2, 1] = shift(C[1, 0], "x", 1), shift(C[-1, 1], "x", -1)
-    R[3, 0], R[-3, 0] = shift(R[2, 0], "z", 1), shift(R[-2, 0], "z", -1)
-    R[4, 0] = shift(R[3, 0], "z", 1)
-    for d in (1, -1, 2, -2, 3, -3, 4):
-        step = 1 if d > 0 else -1
-        R[d, 1] = shift(R[d, 0], "yh", 1) if d in (3, 4) else shift(R[d - step, 1], "z", step)
-
-    cols = [C[o] for o in ORDER]
+
+    R[2, 0] = shift(R[1, 0], "z", 1)
+    R[-2, 0] = shift(after(R[-1, 0], R[1, 0]), "z", -1)
+    both = shift(after(jnp.stack([R[1, 0], R[-1, 0]]), C[0, 1]), "yh", 1)
+    R[1, 1], R[-1, 1] = both[0], both[1]
+    C[1, 1] = shift(after(C[0, 1], R[-1, 0], C[1, 0]), "x", 1)
+    C[-1, 1] = shift(after(C[0, 1], C[1, 0], C[-1, 0]), "x", -1)
+
+    R[3, 0] = shift(after(R[2, 0], C[-1, 0]), "z", 1)
+    R[-3, 0] = shift(after(R[-2, 0], R[2, 0]), "z", -1)
+    C[2, 0] = shift(after(C[1, 0], C[1, 1], R[-2, 0]), "x", 1)
+    C[2, 1] = shift(after(C[-1, 1], C[1, 1]), "x", -1)
+    R[0, 1] = shift(after(row, both, C[-1, 1]), "yh", 1)
+
+    both = shift(after(jnp.stack([R[3, 0], R[1, 1]]), C[-1, 1]), "z", 1)
+    R[4, 0], R[2, 1] = both[0], both[1]
+    R[-2, 1] = shift(after(R[-1, 1], R[-3, 0], R[3, 0]), "z", -1)
+    R[-3, 1] = shift(R[-2, 1], "z", -1)
+    R[3, 1] = shift(R[2, 1], "z", 1)
+    R[4, 1] = shift(R[-3, 1], "z", -1)
+
+    cols = [C[dx, dy] for dx in STEPS for dy in (0, 1)]
+    gates = ((R[3, 0], R[-3, 0]), (R[4, 0], R[-3, 1]), ())
     out = None
-    for g, group in enumerate(GROUPS):
-        pieces = [R[d, h] for d in group for h in (0, 1)]
-        if g == 0:
-            pieces, _, _ = lax.optimization_barrier((pieces, R[4, 0], R[-2, 1]))
+    for group, gate in zip(GROUPS, gates):
+        pieces = after([R[p] for p in group], *gate)
         keep, send = cross(scal, pieces, cols)
-        recv = shift(send, "c", 1)
-        out = lags(scal, group, keep, recv, table, out)
+        out = lags(scal, group, keep, shift(send, "c", 1), table, out)
     return out.reshape(N_Z * 20, COLS, LAGS)
 
 

time: 181 us -> 154 us (0.85)
  waiting for transfers between devices: 69.8 us -> 43.1 us
  Pallas kernels: 69.7 us -> 59.2 us
  local copies, waits for them, and re-layouts: 4.88 us -> 9.2 us
  starting transfers between devices: 36.2 us -> 39.2 us
  other arithmetic: 0.15 us -> 2.33 us
    ppermute x25 -> x24, waiting for transfers between devices: 69.8 us -> 43.1 us  [shift(): return lax.ppermute(x, axis, [(i, (i + step) % n) for i in range(n)])]
    pallas_call x2 -> x3, Pallas kernels: 51.4 us -> 34.6 us  [cross(): pl.pallas_call(functools.partial(cross_kernel, n), out_shape=(shape, shap...]
    pallas_call x2 -> x3, Pallas kernels: 13 us -> 19.3 us  [lags(): pl.pallas_call(lags_kernel, out_shape=jax.ShapeDtypeStruct((N_Z * N_YH *...]
    ppermute x25 -> x24, starting transfers between devices: 36.2 us -> 39.2 us  [shift(): return lax.ppermute(x, axis, [(i, (i + step) % n) for i in range(n)])]
    unnamed x34 -> x40, local copies, waits for them, and re-layouts: 2.48 us -> 4.76 us
    squeeze x0 -> x2, local copies, waits for them, and re-layouts: none -> 1.98 us  [the longest x1 1.01 us: shards(): R[1, 1], R[-1, 1] = (both[0], both[1])]
  transfers between devices with their start and end apart: 25 -> 24, of which waited for: 7 -> 11; matrix products, arithmetic and copies ran while one was open for 1% -> 3% of each run, Pallas kernels for 33% -> 33%
where the time goes in v3:
time: 154 us; the launch traced here: 153 us
  Pallas kernels  59.2 us (38%)
  waiting for transfers between devices  43.1 us (28%)
  starting transfers between devices  39.2 us (25%)
  local copies, waits for them, and re-layouts  9.2 us (6%)
  other arithmetic  2.33 us (2%)
    ppermute x24, waiting for transfers between devices, shift(): return lax.ppermute(x, axis, [(i, (i + step) % n) for i in range(n)])  43.1 us
    ppermute x24, starting transfers between devices, shift(): return lax.ppermute(x, axis, [(i, (i + step) % n) for i in range(n)])  39.2 us
    pallas_call x3, Pallas kernels, cross(): pl.pallas_call(functools.partial(cross_kernel, n), out_shape=(shape, shap...  34.6 us
    pallas_call x3, Pallas kernels, lags(): pl.pallas_call(lags_kernel, out_shape=jax.ShapeDtypeStruct((N_Z * N_YH *...  19.3 us
    pallas_call x1, Pallas kernels, whiten(): pl.pallas_call(whiten_kernel, out_shape=(msg, msg), in_specs=[pl.BlockSpe...  5.35 us
    unnamed x40, local copies, waits for them, and re-layouts  4.76 us
  transfers between devices with their start and end apart: 24, of which 11 were waited for; matrix products, arithmetic and copies ran while one was open for 3% of the time, Pallas kernels for 33%

profile of v3, /device:TPU:1, one launch (start us, length us, event | category | flops | bytes accessed | tf_op | source)
XLA Modules:
  0.0 153.2 jit_solution(7113767487439563604)
XLA Ops:
  0.0 1.3 concatenate.3.scal
  1.3 5.4 %whiten.1 = (bf16[2,256,640]{2,1,0:T(8,128)(2,1)}, bf16[2,256,640]{2,1,0:T(8,128)(2,1)}) custom-call(s32[10]{0:T(128)} %concatenate.3.scal, f32[2560,128]{1,0:T(8,128)} %bitcast.37, s32[5,64]{1,0:T(8,128)} %valid.1), custom_call_target="tpu_custom_call" | custom-call | flops 1000000000 | bytes 3000000 | tf_op jit(solution)/shard_map/whiten/pallas_call | solution.py:93
  6.6 3.2 %collective-permute-start = (bf16[2,256,640]{2,1,0:T(8,128)(2,1)}, bf16[2,256,640]{2,1,0:T(8,128)(2,1)S(1)}, u32[]{:S(2)}, u32[]{:S(2)}) collective-permute-start(bf16[2,256,640]{2,1,0:T(8,128)(2,1)} %get-tuple-element.41), channel_id=1, source_target_pairs={{0,1},{1,0},{2,3},{3,2},{4,5},{5,4},{6,7},{7,6},{8,9},{9,8},{10,11... | collective-permute-start | bytes 1966088 | tf_op jit(solution)/shard_map/ppermute | solution.py:35
  12.8 3.8 %collective-permute-start.5 = (bf16[2,256,640]{2,1,0:T(8,128)(2,1)}, bf16[2,256,640]{2,1,0:T(8,128)(2,1)S(1)}, u32[]{:S(2)}, u32[]{:S(2)}) collective-permute-start(bf16[2,256,640]{2,1,0:T(8,128)(2,1)} %pad_maximum_fusion.2.refs_0_), channel_id=1, source_target_pairs={{0,28},{4,0},{8,4},{12,8},{16,12},{20,16},{24,20},{28,24},{1,29},{... | collective-permute-start | bytes 1966088 | tf_op jit(solution)/shard_map/ppermute | solution.py:35
  16.7 1.4 collective-permute-start.6
  18.1 1.2 collective-permute-start.8
  19.3 1.5 collective-permute-start.3
  20.8 9.9 %collective-permute-done.5.refs_2_ = bf16[2,256,640]{2,1,0:T(8,128)(2,1)S(1)} collective-permute-done((bf16[2,256,640]{2,1,0:T(8,128)(2,1)}, bf16[2,256,640]{2,1,0:T(8,128)(2,1)S(1)}, u32[]{:S(2)}, u32[]{:S(2)}) %collective-permute-start.5) | collective-permute-done | bytes 655392 | tf_op jit(solution)/shard_map/ppermute | solution.py:35
  30.7 3.0 %collective-permute-done.1.refs_1_ = bf16[2,256,640]{2,1,0:T(8,128)(2,1)S(1)} collective-permute-done((bf16[2,256,640]{2,1,0:T(8,128)(2,1)}, bf16[2,256,640]{2,1,0:T(8,128)(2,1)S(1)}, u32[]{:S(2)}, u32[]{:S(2)}) %collective-permute-start.1) | collective-permute-done | bytes 655392 | tf_op jit(solution)/shard_map/ppermute | solution.py:35
  33.9 3.0 %collective-permute-start.7 = (bf16[2,2,256,640]{3,2,1,0:T(8,128)(2,1)S(1)}, bf16[2,2,256,640]{3,2,1,0:T(8,128)(2,1)S(1)}, u32[]{:S(2)}, u32[]{:S(2)}) collective-permute-start(bf16[2,2,256,640]{3,2,1,0:T(8,128)(2,1)S(1)} %pad_maximum_fusion), channel_id=1, source_target_pairs={{0,2},{2,0},{1,3},{3,1},{4,6},{6,4},{5,7},{7,5},{8,10},{10,8},{9,1... | collective-permute-start | bytes 3932168 | tf_op jit(solution)/shard_map/ppermute | solution.py:35
  38.3 1.2 collective-permute-start.17
  39.5 1.5 collective-permute-start.9
  41.0 10.3 %collective-permute-done.12.refs_4_ = bf16[2,256,640]{2,1,0:T(8,128)(2,1)S(1)} collective-permute-done((bf16[2,256,640]{2,1,0:T(8,128)(2,1)S(1)}, bf16[2,256,640]{2,1,0:T(8,128)(2,1)S(1)}, u32[]{:S(2)}, u32[]{:S(2)}) %collective-permute-start.12) | collective-permute-done | bytes 655392 | tf_op jit(solution)/shard_map/ppermute | solution.py:35
  51.3 1.5 collective-permute-done.2.refs_3_
  54.2 1.2 collective-permute-start.18
  55.4 8.8 %collective-permute-done.7 = bf16[2,2,256,640]{3,2,1,0:T(8,128)(2,1)S(1)} collective-permute-done((bf16[2,2,256,640]{3,2,1,0:T(8,128)(2,1)S(1)}, bf16[2,2,256,640]{3,2,1,0:T(8,128)(2,1)S(1)}, u32[]{:S(2)}, u32[]{:S(2)}) %collective-permute-start.7) | collective-permute-done | bytes 1310752 | tf_op jit(solution)/shard_map/ppermute | solution.py:35
  65.6 1.6 %collective-permute-done.4.refs_5_ = bf16[2,256,640]{2,1,0:T(8,128)(2,1)S(1)} collective-permute-done((bf16[2,256,640]{2,1,0:T(8,128)(2,1)S(1)}, bf16[2,256,640]{2,1,0:T(8,128)(2,1)S(1)}, u32[]{:S(2)}, u32[]{:S(2)}) %collective-permute-start.4) | collective-permute-done | bytes 655392 | tf_op jit(solution)/shard_map/ppermute | solution.py:35
  67.6 2.5 %collective-permute-start.19 = (bf16[2,256,640]{2,1,0:T(8,128)(2,1)S(1)}, bf16[2,256,640]{2,1,0:T(8,128)(2,1)S(1)}, u32[]{:S(2)}, u32[]{:S(2)}) collective-permute-start(bf16[2,256,640]{2,1,0:T(8,128)(2,1)S(1)} %collective-permute-done.9.refs_7_.refs_10_.refs_14_), channel_id=1, source_target_pairs={{0,192},{64,0},{128,64},{192,128},{1,193},{65,1},{129,65},{193,129... | collective-permute-start | bytes 1966088 | tf_op jit(solution)/shard_map/ppermute | solution.py:35
  73.5 5.7 %collective-permute-done.14.refs_1_ = bf16[2,256,640]{2,1,0:T(8,128)(2,1)S(1)} collective-permute-done((bf16[2,256,640]{2,1,0:T(8,128)(2,1)S(1)}, bf16[2,256,640]{2,1,0:T(8,128)(2,1)S(1)}, u32[]{:S(2)}, u32[]{:S(2)}) %collective-permute-start.14) | collective-permute-done | bytes 655392 | tf_op jit(solution)/shard_map/ppermute | solution.py:35
  79.2 1.8 %collective-permute-start.15 = (bf16[2,256,640]{2,1,0:T(8,128)(2,1)S(1)}, bf16[2,256,640]{2,1,0:T(8,128)(2,1)}, u32[]{:S(2)}, u32[]{:S(2)}) collective-permute-start(bf16[2,256,640]{2,1,0:T(8,128)(2,1)S(1)} %collective-permute-done.14.refs_1_), channel_id=1, source_target_pairs={{0,28},{4,0},{8,4},{12,8},{16,12},{20,16},{24,20},{28,24},{1,29},{... | collective-permute-start | bytes 1966088 | tf_op jit(solution)/shard_map/ppermute | solution.py:35
  82.7 13.6 %cross.5 = (bf16[90,40,256]{2,1,0:T(8,128)(2,1)}, bf16[90,40,256]{2,1,0:T(8,128)(2,1)}) custom-call(s32[10]{0:T(128)} %concatenate.3.scal, bf16[2,256,640]{2,1,0:T(8,128)(2,1)} %pad_maximum_fusion.2.refs_0_, bf16[2,256,640]{2,1,0:T(8,128)(2,1)} %copy-done.3, bf16[2,256,640]{2,1,0:T(8,128)(2,1)} %copy-done.2, bf16[2,256,640]{2,1,0:T(8,128)(2,1)} %copy-done.16, ...), custom_call_target="tpu_custom_call" | custom-call | flops 10000000000 | bytes 10000000 | tf_op jit(solution)/shard_map/cross/pallas_call | solution.py:161
  96.3 5.8 %collective-permute-start.23 = (bf16[90,40,256]{2,1,0:T(8,128)(2,1)}, bf16[90,40,256]{2,1,0:T(8,128)(2,1)S(1)}, u32[]{:S(2)}, u32[]{:S(2)}) collective-permute-start(bf16[90,40,256]{2,1,0:T(8,128)(2,1)} %get-tuple-element.74), channel_id=1, source_target_pairs={{0,1},{1,0},{2,3},{3,2},{4,5},{5,4},{6,7},{7,6},{8,9},{9,8},{10,11... | collective-permute-start | bytes 5529608 | tf_op jit(solution)/shard_map/ppermute | solution.py:35
  103.1 1.5 collective-permute-start.11
  104.5 11.7 %cross.4 = (bf16[50,40,256]{2,1,0:T(8,128)(2,1)}, bf16[50,40,256]{2,1,0:T(8,128)(2,1)}) custom-call(s32[10]{0:T(128)} %concatenate.3.scal, bf16[2,256,640]{2,1,0:T(8,128)(2,1)} %collective-permute-done.21.refs_0_, bf16[2,256,640]{2,1,0:T(8,128)(2,1)} %copy-done.18, bf16[2,256,640]{2,1,0:T(8,128)(2,1)} %get-tuple-element.59.refs_2_, ...), custom_call_target="tpu_custom_call" | custom-call | flops 10000000000 | bytes 10000000 | tf_op jit(solution)/shard_map/cross/pallas_call | solution.py:161
  116.2 1.3 collective-permute-start.22
  117.5 1.2 collective-permute-done.16.refs_1_
  118.8 9.3 %cross.3 = (bf16[20,40,256]{2,1,0:T(8,128)(2,1)}, bf16[20,40,256]{2,1,0:T(8,128)(2,1)}) custom-call(s32[10]{0:T(128)} %concatenate.3.scal, bf16[2,256,640]{2,1,0:T(8,128)(2,1)} %collective-permute-done.11.refs_0_, bf16[2,256,640]{2,1,0:T(8,128)(2,1)} %collective-permute-done.16.refs_1_, bf16[2,256,640]{2,1,0:T(8,128)(2,1)} %copy-done.6, ...), custom_call_target="tpu_custom_call" | custom-call | flops 10000000000 | bytes 10000000 | tf_op jit(solution)/shard_map/cross/pallas_call | solution.py:161
  128.1 2.8 %collective-permute-start.20 = (bf16[20,40,256]{2,1,0:T(8,128)(2,1)}, bf16[20,40,256]{2,1,0:T(8,128)(2,1)S(1)}, u32[]{:S(2)}, u32[]{:S(2)}) collective-permute-start(bf16[20,40,256]{2,1,0:T(8,128)(2,1)} %get-tuple-element.55), channel_id=1, source_target_pairs={{0,1},{1,0},{2,3},{3,2},{4,5},{5,4},{6,7},{7,6},{8,9},{9,8},{10,11... | collective-permute-start | bytes 1228808 | tf_op jit(solution)/shard_map/ppermute | solution.py:35
  131.0 1.3 copy-done
  132.2 9.5 %lags.3.rest_0_ = bf16[6400,512]{1,0:T(8,128)(2,1)} custom-call(s32[10]{0:T(128)} %concatenate.3.scal, bf16[3600,256]{1,0:T(8,128)(2,1)} %bitcast.28, bf16[3600,256]{1,0:T(8,128)(2,1)} %bitcast.29, bf16[2,256,512]{2,1,0:T(8,128)(2,1)} %constant.28.near.far, bf16[2,256,512]{2,1,0:T(8,128)(2,1)} %constant.28.near.far), custom_call_target="tpu_custom_call" | custom-call | flops 2000000000 | bytes 3000000 | tf_op jit(solution)/shard_map/lags/pallas_call | solution.py:199
  142.7 6.3 %lags.4.rest_0_ = bf16[6400,512]{1,0:T(8,128)(2,1)} custom-call(s32[10]{0:T(128)} %concatenate.3.scal, bf16[2000,256]{1,0:T(8,128)(2,1)} %bitcast.30, bf16[2000,256]{1,0:T(8,128)(2,1)} %bitcast.31, bf16[2,256,512]{2,1,0:T(8,128)(2,1)} %constant.28.near.far, bf16[2,256,512]{2,1,0:T(8,128)(2,1)} %constant.28.near.far, ...), custom_call_target="tpu_custom_call", output_to_operand_aliasing={{}: (5, {})} | custom-call | flops 2000000000 | bytes 3000000 | tf_op jit(solution)/shard_map/lags/pallas_call | solution.py:199
  149.7 3.5 %lags.5 = bf16[6400,512]{1,0:T(8,128)(2,1)} custom-call(s32[10]{0:T(128)} %concatenate.3.scal, bf16[800,256]{1,0:T(8,128)(2,1)} %bitcast.35, bf16[800,256]{1,0:T(8,128)(2,1)} %bitcast.36, bf16[2,256,512]{2,1,0:T(8,128)(2,1)} %constant.28.near.far, bf16[2,256,512]{2,1,0:T(8,128)(2,1)} %constant.28.near.far, ...), custom_call_target="tpu_custom_call", output_to_operand_aliasing={{}: (5, {})} | custom-call | flops 2000000000 | bytes 3000000 | tf_op jit(solution)/shard_map/lags/pallas_call | solution.py:199
  (72 shorter events, 15.8 us)
Async XLA Ops:
  6.6 5.2 %collective-permute-start = (bf16[2,256,640]{2,1,0:T(8,128)(2,1)}, bf16[2,256,640]{2,1,0:T(8,128)(2,1)S(1)}, u32[]{:S(2)}, u32[]{:S(2)}) collective-permute-start(bf16[2,256,640]{2,1,0:T(8,128)(2,1)} %get-tuple-element.41), channel_id=1, source_target_pairs={{0,1},{1,0},{2,3},{3,2},{4,5},{5,4},{6,7},{7,6},{8,9},{9,8},{10,11... | collective-permute-start | bytes 1966088 | tf_op jit(solution)/shard_map/ppermute | solution.py:35
  12.8 17.9 %collective-permute-start.5 = (bf16[2,256,640]{2,1,0:T(8,128)(2,1)}, bf16[2,256,640]{2,1,0:T(8,128)(2,1)S(1)}, u32[]{:S(2)}, u32[]{:S(2)}) collective-permute-start(bf16[2,256,640]{2,1,0:T(8,128)(2,1)} %pad_maximum_fusion.2.refs_0_), channel_id=1, source_target_pairs={{0,28},{4,0},{8,4},{12,8},{16,12},{20,16},{24,20},{28,24},{1,29},{... | collective-permute-start | bytes 1966088 | tf_op jit(solution)/shard_map/ppermute | solution.py:35
  16.6 17.0 %collective-permute-start.1 = (bf16[2,256,640]{2,1,0:T(8,128)(2,1)}, bf16[2,256,640]{2,1,0:T(8,128)(2,1)S(1)}, u32[]{:S(2)}, u32[]{:S(2)}) collective-permute-start(bf16[2,256,640]{2,1,0:T(8,128)(2,1)} %pad_maximum_fusion.2.refs_0_), channel_id=1, source_target_pairs={{0,4},{4,8},{8,12},{12,16},{16,20},{20,24},{24,28},{28,0},{1,5},{5... | collective-permute-start | bytes 1966088 | tf_op jit(solution)/shard_map/ppermute | solution.py:35
  16.7 17.1 %copy-start.6 = (bf16[2,256,640]{2,1,0:T(8,128)(2,1)}, bf16[2,256,640]{2,1,0:T(8,128)(2,1)S(1)}, u32[]{:S(2)}) copy-start(bf16[2,256,640]{2,1,0:T(8,128)(2,1)S(1)} %pad_maximum_fusion.3.refs_2_.refs_5_.refs_9_) | copy-start | bytes 1966084
  16.7 17.1 %collective-permute-start.6 = (bf16[2,256,640]{2,1,0:T(8,128)(2,1)S(1)}, bf16[2,256,640]{2,1,0:T(8,128)(2,1)S(1)}, u32[]{:S(2)}, u32[]{:S(2)}) collective-permute-start(bf16[2,256,640]{2,1,0:T(8,128)(2,1)S(1)} %pad_maximum_fusion.3.refs_2_.refs_5_.refs_9_), channel_id=1, source_target_pairs={{0,32},{32,0},{1,33},{33,1},{2,34},{34,2},{3,35},{35,3},{4,36},{36... | collective-permute-start | bytes 1966088 | tf_op jit(solution)/shard_map/ppermute | solution.py:35
  18.1 20.2 %collective-permute-start.8 = (bf16[2,256,640]{2,1,0:T(8,128)(2,1)S(1)}, bf16[2,256,640]{2,1,0:T(8,128)(2,1)S(1)}, u32[]{:S(2)}, u32[]{:S(2)}) collective-permute-start(bf16[2,256,640]{2,1,0:T(8,128)(2,1)S(1)} %pad_maximum_fusion.3.refs_2_.refs_5_.refs_9_), channel_id=1, source_target_pairs={{0,64},{64,128},{128,192},{192,0},{1,65},{65,129},{129,193},{193,1... | collective-permute-start | bytes 1966088 | tf_op jit(solution)/shard_map/ppermute | solution.py:35
  19.3 20.2 %collective-permute-start.3 = (bf16[2,256,640]{2,1,0:T(8,128)(2,1)S(1)}, bf16[2,256,640]{2,1,0:T(8,128)(2,1)S(1)}, u32[]{:S(2)}, u32[]{:S(2)}) collective-permute-start(bf16[2,256,640]{2,1,0:T(8,128)(2,1)S(1)} %pad_maximum_fusion.3.refs_2_.refs_5_.refs_9_), channel_id=1, source_target_pairs={{0,192},{64,0},{128,64},{192,128},{1,193},{65,1},{129,65},{193,129... | collective-permute-start | bytes 1966088 | tf_op jit(solution)/shard_map/ppermute | solution.py:35
  33.8 31.4 %copy-start.9 = (bf16[2,256,640]{2,1,0:T(8,128)(2,1)}, bf16[2,256,640]{2,1,0:T(8,128)(2,1)S(1)}, u32[]{:S(2)}) copy-start(bf16[2,256,640]{2,1,0:T(8,128)(2,1)S(1)} %collective-permute-done.6.refs_3_.refs_6_.refs_10_) | copy-start | bytes 1966084
  33.9 30.3 %collective-permute-start.7 = (bf16[2,2,256,640]{3,2,1,0:T(8,128)(2,1)S(1)}, bf16[2,2,256,640]{3,2,1,0:T(8,128)(2,1)S(1)}, u32[]{:S(2)}, u32[]{:S(2)}) collective-permute-start(bf16[2,2,256,640]{3,2,1,0:T(8,128)(2,1)S(1)} %pad_maximum_fusion), channel_id=1, source_target_pairs={{0,2},{2,0},{1,3},{3,1},{4,6},{6,4},{5,7},{7,5},{8,10},{10,8},{9,1... | collective-permute-start | bytes 3932168 | tf_op jit(solution)/shard_map/ppermute | solution.py:35
  36.9 14.4 %collective-permute-start.12 = (bf16[2,256,640]{2,1,0:T(8,128)(2,1)S(1)}, bf16[2,256,640]{2,1,0:T(8,128)(2,1)S(1)}, u32[]{:S(2)}, u32[]{:S(2)}) collective-permute-start(bf16[2,256,640]{2,1,0:T(8,128)(2,1)S(1)} %collective-permute-done.5.refs_2_), channel_id=1, source_target_pairs={{0,28},{4,0},{8,4},{12,8},{16,12},{20,16},{24,20},{28,24},{1,29},{... | collective-permute-start | bytes 1966088 | tf_op jit(solution)/shard_map/ppermute | solution.py:35
  37.7 15.0 %collective-permute-start.2 = (bf16[2,256,640]{2,1,0:T(8,128)(2,1)S(1)}, bf16[2,256,640]{2,1,0:T(8,128)(2,1)S(1)}, u32[]{:S(2)}, u32[]{:S(2)}) collective-permute-start(bf16[2,256,640]{2,1,0:T(8,128)(2,1)S(1)} %collective-permute-done.1.refs_1_), channel_id=1, source_target_pairs={{0,4},{4,8},{8,12},{12,16},{16,20},{20,24},{24,28},{28,0},{1,5},{5... | collective-permute-start | bytes 1966088 | tf_op jit(solution)/shard_map/ppermute | solution.py:35
  38.3 26.9 %copy-start.10 = (bf16[2,256,640]{2,1,0:T(8,128)(2,1)}, bf16[2,256,640]{2,1,0:T(8,128)(2,1)S(1)}, u32[]{:S(2)}) copy-start(bf16[2,256,640]{2,1,0:T(8,128)(2,1)S(1)} %collective-permute-done.8.refs_4_.refs_7_.refs_11_) | copy-start | bytes 1966084
  38.3 15.9 %collective-permute-start.17 = (bf16[2,256,640]{2,1,0:T(8,128)(2,1)S(1)}, bf16[2,256,640]{2,1,0:T(8,128)(2,1)S(1)}, u32[]{:S(2)}, u32[]{:S(2)}) collective-permute-start(bf16[2,256,640]{2,1,0:T(8,128)(2,1)S(1)} %collective-permute-done.6.refs_3_.refs_6_.refs_10_), channel_id=1, source_target_pairs={{0,64},{64,128},{128,192},{192,0},{1,65},{65,129},{129,193},{193,1... | collective-permute-start | bytes 1966088 | tf_op jit(solution)/shard_map/ppermute | solution.py:35
  39.5 25.7 %copy-start.11 = (bf16[2,256,640]{2,1,0:T(8,128)(2,1)}, bf16[2,256,640]{2,1,0:T(8,128)(2,1)S(1)}, u32[]{:S(2)}) copy-start(bf16[2,256,640]{2,1,0:T(8,128)(2,1)S(1)} %collective-permute-done.3.refs_6_.refs_9_.refs_13_) | copy-start | bytes 1966084
  39.5 15.9 %collective-permute-start.9 = (bf16[2,256,640]{2,1,0:T(8,128)(2,1)S(1)}, bf16[2,256,640]{2,1,0:T(8,128)(2,1)S(1)}, u32[]{:S(2)}, u32[]{:S(2)}) collective-permute-start(bf16[2,256,640]{2,1,0:T(8,128)(2,1)S(1)} %collective-permute-done.6.refs_3_.refs_6_.refs_10_), channel_id=1, source_target_pairs={{0,192},{64,0},{128,64},{192,128},{1,193},{65,1},{129,65},{193,129... | collective-permute-start | bytes 1966088 | tf_op jit(solution)/shard_map/ppermute | solution.py:35
  51.3 18.8 %copy-start.15 = (bf16[2,256,640]{2,1,0:T(8,128)(2,1)}, bf16[2,256,640]{2,1,0:T(8,128)(2,1)S(1)}, u32[]{:S(2)}) copy-start(bf16[2,256,640]{2,1,0:T(8,128)(2,1)S(1)} %collective-permute-done.12.refs_4_) | copy-start | bytes 1966084
  52.7 28.3 %copy-start.16 = (bf16[2,256,640]{2,1,0:T(8,128)(2,1)}, bf16[2,256,640]{2,1,0:T(8,128)(2,1)S(1)}, u32[]{:S(2)}) copy-start(bf16[2,256,640]{2,1,0:T(8,128)(2,1)S(1)} %collective-permute-done.2.refs_3_) | copy-start | bytes 1966084
  52.7 12.9 %collective-permute-start.13 = (bf16[2,256,640]{2,1,0:T(8,128)(2,1)S(1)}, bf16[2,256,640]{2,1,0:T(8,128)(2,1)S(1)}, u32[]{:S(2)}, u32[]{:S(2)}) collective-permute-start(bf16[2,256,640]{2,1,0:T(8,128)(2,1)S(1)} %collective-permute-done.12.refs_4_), channel_id=1, source_target_pairs={{0,28},{4,0},{8,4},{12,8},{16,12},{20,16},{24,20},{28,24},{1,29},{... | collective-permute-start | bytes 1966088 | tf_op jit(solution)/shard_map/ppermute | solution.py:35
  53.1 14.1 %collective-permute-start.4 = (bf16[2,256,640]{2,1,0:T(8,128)(2,1)S(1)}, bf16[2,256,640]{2,1,0:T(8,128)(2,1)S(1)}, u32[]{:S(2)}, u32[]{:S(2)}) collective-permute-start(bf16[2,256,640]{2,1,0:T(8,128)(2,1)S(1)} %collective-permute-done.2.refs_3_), channel_id=1, source_target_pairs={{0,4},{4,8},{8,12},{12,16},{16,20},{20,24},{24,28},{28,0},{1,5},{5... | collective-permute-start | bytes 1966088 | tf_op jit(solution)/shard_map/ppermute | solution.py:35
  54.2 26.8 %collective-permute-start.18 = (bf16[2,256,640]{2,1,0:T(8,128)(2,1)S(1)}, bf16[2,256,640]{2,1,0:T(8,128)(2,1)S(1)}, u32[]{:S(2)}, u32[]{:S(2)}) collective-permute-start(bf16[2,256,640]{2,1,0:T(8,128)(2,1)S(1)} %collective-permute-done.8.refs_4_.refs_7_.refs_11_), channel_id=1, source_target_pairs={{0,64},{64,128},{128,192},{192,0},{1,65},{65,129},{129,193},{193,1... | collective-permute-start | bytes 1966088 | tf_op jit(solution)/shard_map/ppermute | solution.py:35
  55.4 12.1 %copy-start.13 = (bf16[2,256,640]{2,1,0:T(8,128)(2,1)}, bf16[2,256,640]{2,1,0:T(8,128)(2,1)S(1)}, u32[]{:S(2)}) copy-start(bf16[2,256,640]{2,1,0:T(8,128)(2,1)S(1)} %collective-permute-done.9.refs_7_.refs_10_.refs_14_) | copy-start | bytes 1966084
  67.2 12.0 %collective-permute-start.14 = (bf16[2,256,640]{2,1,0:T(8,128)(2,1)S(1)}, bf16[2,256,640]{2,1,0:T(8,128)(2,1)S(1)}, u32[]{:S(2)}, u32[]{:S(2)}) collective-permute-start(bf16[2,256,640]{2,1,0:T(8,128)(2,1)S(1)} %get-tuple-element.72.refs_8_), channel_id=1, source_target_pairs={{0,28},{4,0},{8,4},{12,8},{16,12},{20,16},{24,20},{28,24},{1,29},{... | collective-permute-start | bytes 1966088 | tf_op jit(solution)/shard_map/ppermute | solution.py:35
  67.6 14.3 %collective-permute-start.19 = (bf16[2,256,640]{2,1,0:T(8,128)(2,1)S(1)}, bf16[2,256,640]{2,1,0:T(8,128)(2,1)S(1)}, u32[]{:S(2)}, u32[]{:S(2)}) collective-permute-start(bf16[2,256,640]{2,1,0:T(8,128)(2,1)S(1)} %collective-permute-done.9.refs_7_.refs_10_.refs_14_), channel_id=1, source_target_pairs={{0,192},{64,0},{128,64},{192,128},{1,193},{65,1},{129,65},{193,129... | collective-permute-start | bytes 1966088 | tf_op jit(solution)/shard_map/ppermute | solution.py:35
  71.2 30.9 %collective-permute-start.10 = (bf16[2,2,256,640]{3,2,1,0:T(8,128)(2,1)}, bf16[2,2,256,640]{3,2,1,0:T(8,128)(2,1)S(1)}, u32[]{:S(2)}, u32[]{:S(2)}) collective-permute-start(bf16[2,2,256,640]{3,2,1,0:T(8,128)(2,1)} %pad_maximum_fusion.1), channel_id=1, source_target_pairs={{0,4},{4,8},{8,12},{12,16},{16,20},{20,24},{24,28},{28,0},{1,5},{5... | collective-permute-start | bytes 3932168 | tf_op jit(solution)/shard_map/ppermute | solution.py:35
  72.4 32.1 %collective-permute-start.21 = (bf16[2,256,640]{2,1,0:T(8,128)(2,1)}, bf16[2,256,640]{2,1,0:T(8,128)(2,1)}, u32[]{:S(2)}, u32[]{:S(2)}) collective-permute-start(bf16[2,256,640]{2,1,0:T(8,128)(2,1)} %pad_maximum_fusion.2.refs_0_), channel_id=1, source_target_pairs={{0,2},{2,0},{1,3},{3,1},{4,6},{6,4},{5,7},{7,5},{8,10},{10,8},{9,1... | collective-permute-start | bytes 1966088 | tf_op jit(solution)/shard_map/ppermute | solution.py:35
  79.2 17.1 %copy-start.18 = (bf16[2,256,640]{2,1,0:T(8,128)(2,1)}, bf16[2,256,640]{2,1,0:T(8,128)(2,1)S(1)}, u32[]{:S(2)}) copy-start(bf16[2,256,640]{2,1,0:T(8,128)(2,1)S(1)} %collective-permute-done.14.refs_1_) | copy-start | bytes 1966084
  79.2 22.9 %collective-permute-start.15 = (bf16[2,256,640]{2,1,0:T(8,128)(2,1)S(1)}, bf16[2,256,640]{2,1,0:T(8,128)(2,1)}, u32[]{:S(2)}, u32[]{:S(2)}) collective-permute-start(bf16[2,256,640]{2,1,0:T(8,128)(2,1)S(1)} %collective-permute-done.14.refs_1_), channel_id=1, source_target_pairs={{0,28},{4,0},{8,4},{12,8},{16,12},{20,16},{24,20},{28,24},{1,29},{... | collective-permute-start | bytes 1966088 | tf_op jit(solution)/shard_map/ppermute | solution.py:35
  96.3 34.6 %collective-permute-start.23 = (bf16[90,40,256]{2,1,0:T(8,128)(2,1)}, bf16[90,40,256]{2,1,0:T(8,128)(2,1)S(1)}, u32[]{:S(2)}, u32[]{:S(2)}) collective-permute-start(bf16[90,40,256]{2,1,0:T(8,128)(2,1)} %get-tuple-element.74), channel_id=1, source_target_pairs={{0,1},{1,0},{2,3},{3,2},{4,5},{5,4},{6,7},{7,6},{8,9},{9,8},{10,11... | collective-permute-start | bytes 5529608 | tf_op jit(solution)/shard_map/ppermute | solution.py:35
  102.1 16.6 %collective-permute-start.16 = (bf16[2,256,640]{2,1,0:T(8,128)(2,1)}, bf16[2,256,640]{2,1,0:T(8,128)(2,1)}, u32[]{:S(2)}, u32[]{:S(2)}) collective-permute-start(bf16[2,256,640]{2,1,0:T(8,128)(2,1)} %collective-permute-done.15.refs_4_), channel_id=1, source_target_pairs={{0,28},{4,0},{8,4},{12,8},{16,12},{20,16},{24,20},{28,24},{1,29},{... | collective-permute-start | bytes 1966088 | tf_op jit(solution)/shard_map/ppermute | solution.py:35
  103.1 15.7 %collective-permute-start.11 = (bf16[2,256,640]{2,1,0:T(8,128)(2,1)S(1)}, bf16[2,256,640]{2,1,0:T(8,128)(2,1)}, u32[]{:S(2)}, u32[]{:S(2)}) collective-permute-start(bf16[2,256,640]{2,1,0:T(8,128)(2,1)S(1)} %get-tuple-element.60.refs_3_), channel_id=1, source_target_pairs={{0,4},{4,8},{8,12},{12,16},{16,20},{20,24},{24,28},{28,0},{1,5},{5... | collective-permute-start | bytes 1966088 | tf_op jit(solution)/shard_map/ppermute | solution.py:35
  116.2 25.5 %collective-permute-start.22 = (bf16[50,40,256]{2,1,0:T(8,128)(2,1)}, bf16[50,40,256]{2,1,0:T(8,128)(2,1)S(1)}, u32[]{:S(2)}, u32[]{:S(2)}) collective-permute-start(bf16[50,40,256]{2,1,0:T(8,128)(2,1)} %get-tuple-element.63), channel_id=1, source_target_pairs={{0,1},{1,0},{2,3},{3,2},{4,5},{5,4},{6,7},{7,6},{8,9},{9,8},{10,11... | collective-permute-start | bytes 3072008 | tf_op jit(solution)/shard_map/ppermute | solution.py:35
  128.1 20.9 %collective-permute-start.20 = (bf16[20,40,256]{2,1,0:T(8,128)(2,1)}, bf16[20,40,256]{2,1,0:T(8,128)(2,1)S(1)}, u32[]{:S(2)}, u32[]{:S(2)}) collective-permute-start(bf16[20,40,256]{2,1,0:T(8,128)(2,1)} %get-tuple-element.55), channel_id=1, source_target_pairs={{0,1},{1,0},{2,3},{3,2},{4,5},{5,4},{6,7},{7,6},{8,9},{9,8},{10,11... | collective-permute-start | bytes 1228808 | tf_op jit(solution)/shard_map/ppermute | solution.py:35
  (12 other events, 43.1 us)

commit v4 on v3

--- a/solution.py
+++ b/solution.py
@@ -21,7 +21,7 @@
 COLS = 40
 BOTH = 2 * COLS
 FB = 128
-VMEM = 60 * 1024 * 1024
+VMEM = 24 * 1024 * 1024
 
 
 def lag_table():
@@ -108,24 +108,29 @@
 UNROLL = 16
 PITCH = FB + 8
 STEPS = (0, 1, -1, 2)
-
-
-def cross_kernel(n, scal, *refs):
+MIB = 1024 * 1024
+
+
+def cross_kernel(n, lead, scal, *refs):
     rows = 10 * n
-    pieces, cols = refs[:n], refs[n : n + 8]
-    keep, send, flat, side, acc = refs[n + 8 :]
+    pieces, rest = refs[:n], refs[n:]
     x, yl, c = scal[0], scal[1], scal[4]
+    if lead:
+        cols, (keep, send, packed, flat, acc, side) = rest[:8], rest[8:]
+    else:
+        packed, keep, send, flat, acc = rest
 
     def spread(piece, into, base):
         for k in range(CH):
             at = pl.multiple_of((base + k) * PITCH, 8)
             into[pl.ds(at, FB), :] = piece[:, k * K : (k + 1) * K].astype(jnp.float32)
 
-    for p in range(4):
-        for h in range(2):
-            r = lax.rem(x - STEPS[p] + N_X, N_X) * N_YL + (yl ^ h)
-            for q in range(2):
-                spread(cols[2 * p + h].at[q], side, q * COLS + r * CH)
+    if lead:
+        for p in range(4):
+            for h in range(2):
+                r = lax.rem(x - STEPS[p] + N_X, N_X) * N_YL + (yl ^ h)
+                for q in range(2):
+                    spread(cols[2 * p + h].at[q], side, q * COLS + r * CH)
     for p in range(n):
         for q in range(2):
             spread(pieces[p].at[q], flat, p * 10 + (c ^ q) * 5)
@@ -135,7 +140,11 @@
         pairs = []
         for f in at:
             first = flat[pl.ds(f, rows, stride=PITCH), :].astype(jnp.bfloat16)
-            second = side[pl.ds(f, BOTH, stride=PITCH), :].astype(jnp.bfloat16)
+            if lead:
+                second = side[pl.ds(f, BOTH, stride=PITCH), :].astype(jnp.bfloat16)
+                packed[f] = second
+            else:
+                second = packed[f]
             pairs.append(
                 lax.dot_general(
                     first, second, (((1,), (1,)), ((), ())), preferred_element_type=jnp.float32
@@ -152,70 +161,81 @@
         send[a] = tile[COLS:BOTH].astype(jnp.bfloat16)
 
 
-def cross(scal, pieces, cols):
+def cross(scal, pieces, cols, lead):
     n = len(pieces)
     rows = 10 * n
-    piece = pl.BlockSpec((2, FB, CH * K), lambda i, s: (0, i, 0))
+    specs, arrays = [], []
+    for piece in pieces:
+        if isinstance(piece, tuple):
+            piece, at = piece
+            specs.append(pl.BlockSpec((None, 2, FB, CH * K), lambda i, s, at=at: (at, 0, i, 0)))
+        else:
+            specs.append(pl.BlockSpec((2, FB, CH * K), lambda i, s: (0, i, 0)))
+        arrays.append(piece)
     part = pl.BlockSpec((rows, COLS, FB), lambda i, s: (0, 0, i))
     shape = jax.ShapeDtypeStruct((rows, COLS, HALF), jnp.bfloat16)
+    packed = pl.BlockSpec((FB, BOTH, K), lambda i, s: (i, 0, 0))
+    held = jax.ShapeDtypeStruct((HALF, BOTH, K), jnp.bfloat16)
+    scratch = [pltpu.VMEM((rows * PITCH, K), jnp.float32)] * 2
+    if lead:
+        specs += [pl.BlockSpec((2, FB, CH * K), lambda i, s: (0, i, 0))] * len(cols)
+        scratch.append(pltpu.VMEM((BOTH * PITCH, K), jnp.float32))
+    else:
+        specs.append(packed)
     return pl.pallas_call(
-        functools.partial(cross_kernel, n),
-        out_shape=(shape, shape),
+        functools.partial(cross_kernel, n, lead),
+        out_shape=(shape, shape, held) if lead else (shape, shape),
         grid_spec=pltpu.PrefetchScalarGridSpec(
             num_scalar_prefetch=1,
             grid=(HALF // FB,),
-            in_specs=[piece] * (n + 8),
-            out_specs=(part, part),
-            scratch_shapes=[
-                pltpu.VMEM((rows * PITCH, K), jnp.float32),
-                pltpu.VMEM((BOTH * PITCH, K), jnp.float32),
-                pltpu.VMEM((rows * PITCH, K), jnp.float32),
-            ],
+            in_specs=specs,
+            out_specs=(part, part, packed) if lead else (part, part),
+            scratch_shapes=scratch,
         ),
-        compiler_params=params(),
+        compiler_params=pltpu.CompilerParams(vmem_limit_bytes=(26 + 3 * n // 2) * MIB),
         cost_estimate=pl.CostEstimate(flops=10**10, bytes_accessed=10**7, transcendentals=0),
         name="cross",
-    )(scal, *pieces, *cols)
-
-
-def lags_kernel(scal, keep, recv, near, far, *rest):
-    both = jnp.concatenate([keep[...], recv[...]], axis=1)
-    table = jnp.concatenate([near[0], far[0]], axis=0)
-    total = jnp.dot(both, table, preferred_element_type=jnp.float32)
-    rest[-1][...] = total.astype(jnp.bfloat16)
+    )(scal, *arrays, *(cols if lead else [cols]))
+
+
+def lags_kernel(group, scal, keep, recv, table, *rest):
+    out, held, sem = rest[-3:]
+    rows = 10 * COLS
+    z, yh, c = scal[2], scal[3], scal[4]
+    copies = []
+    for g, (d, h) in enumerate(group):
+        at = slice(g * rows, (g + 1) * rows)
+        total = jnp.dot(keep[at, :], table[c], preferred_element_type=jnp.float32)
+        total += jnp.dot(recv[at, :], table[1 - c], preferred_element_type=jnp.float32)
+        held[at, :] = total.astype(jnp.bfloat16)
+        to = (lax.rem(z - d + N_Z, N_Z) * N_YH + (yh ^ h)) * rows
+        copy = pltpu.make_async_copy(
+            held.at[at, :], out.at[pl.ds(pl.multiple_of(to, rows), rows), :], sem.at[g]
+        )
+        copy.start()
+        copies.append(copy)
+    for copy in copies:
+        copy.wait()
 
 
 def lags(scal, group, keep, recv, table, prior):
     n = len(group)
     rows = 10 * COLS
-    half = pl.BlockSpec((rows, HALF), lambda i, s: (i, 0))
     extra = [] if prior is None else [prior]
-
-    def place(i, s):
-        back = sum(jnp.where(i == g, d, 0) for g, (d, _) in enumerate(group))
-        side = sum(jnp.where(i == g, h, 0) for g, (_, h) in enumerate(group))
-        return lax.rem(s[2] - back + N_Z, N_Z) * N_YH + (s[3] ^ side), 0
-
+    vmem = pl.BlockSpec(memory_space=pltpu.VMEM)
     return pl.pallas_call(
-        lags_kernel,
+        functools.partial(lags_kernel, group),
         out_shape=jax.ShapeDtypeStruct((N_Z * N_YH * rows, LAGS), jnp.bfloat16),
-        grid_spec=pltpu.PrefetchScalarGridSpec(
-            num_scalar_prefetch=1,
-            grid=(n,),
-            in_specs=[
-                half,
-                half,
-                pl.BlockSpec((1, HALF, LAGS), lambda i, s: (s[4], 0, 0)),
-                pl.BlockSpec((1, HALF, LAGS), lambda i, s: (1 - s[4], 0, 0)),
-            ]
-            + [pl.BlockSpec(memory_space=pl.ANY)] * len(extra),
-            out_specs=pl.BlockSpec((rows, LAGS), place),
-        ),
-        input_output_aliases={5: 0} if extra else {},
-        compiler_params=params(),
+        in_specs=[pl.BlockSpec(memory_space=pltpu.SMEM)]
+        + [vmem] * 3
+        + [pl.BlockSpec(memory_space=pl.ANY)] * len(extra),
+        out_specs=pl.BlockSpec(memory_space=pl.ANY),
+        scratch_shapes=[pltpu.VMEM((n * rows, LAGS), jnp.bfloat16), pltpu.SemaphoreType.DMA((n,))],
+        input_output_aliases={4: 0} if extra else {},
+        compiler_params=pltpu.CompilerParams(vmem_limit_bytes=16 * MIB),
         cost_estimate=pl.CostEstimate(flops=2 * 10**9, bytes_accessed=3 * 10**6, transcendentals=0),
         name="lags",
-    )(scal, keep.reshape(n * rows, HALF), recv.reshape(n * rows, HALF), table, table, *extra)
+    )(scal, keep.reshape(n * rows, HALF), recv.reshape(n * rows, HALF), table, *extra)
 
 
 OWN = tuple((d, 0) for d in (0, 1, -1, 2, -2, 3, -3))
@@ -228,6 +248,13 @@
 
 def after(value, *earlier):
     return lax.optimization_barrier((value, earlier))[0]
+
+
+def gate(pieces, *earlier):
+    arrays = [p[0] if isinstance(p, tuple) else p for p in pieces]
+    arrays, earlier = lax.optimization_barrier((arrays, earlier))
+    held = [(a, p[1]) if isinstance(p, tuple) else a for a, p in zip(arrays, pieces)]
+    return held, earlier
 
 
 def shards(raw_spectra, seg_valid, slot_order):
@@ -246,8 +273,8 @@
 
     R[2, 0] = shift(R[1, 0], "z", 1)
     R[-2, 0] = shift(after(R[-1, 0], R[1, 0]), "z", -1)
-    both = shift(after(jnp.stack([R[1, 0], R[-1, 0]]), C[0, 1]), "yh", 1)
-    R[1, 1], R[-1, 1] = both[0], both[1]
+    near = shift(after(jnp.stack([R[1, 0], R[-1, 0]]), C[0, 1]), "yh", 1)
+    R[1, 1], R[-1, 1] = (near, 0), (near, 1)
     C[1, 1] = shift(after(C[0, 1], R[-1, 0], C[1, 0]), "x", 1)
     C[-1, 1] = shift(after(C[0, 1], C[1, 0], C[-1, 0]), "x", -1)
 
@@ -255,22 +282,28 @@
     R[-3, 0] = shift(after(R[-2, 0], R[2, 0]), "z", -1)
     C[2, 0] = shift(after(C[1, 0], C[1, 1], R[-2, 0]), "x", 1)
     C[2, 1] = shift(after(C[-1, 1], C[1, 1]), "x", -1)
-    R[0, 1] = shift(after(row, both, C[-1, 1]), "yh", 1)
-
-    both = shift(after(jnp.stack([R[3, 0], R[1, 1]]), C[-1, 1]), "z", 1)
-    R[4, 0], R[2, 1] = both[0], both[1]
-    R[-2, 1] = shift(after(R[-1, 1], R[-3, 0], R[3, 0]), "z", -1)
-    R[-3, 1] = shift(R[-2, 1], "z", -1)
-    R[3, 1] = shift(R[2, 1], "z", 1)
+    R[0, 1] = shift(after(row, near, C[-1, 1]), "yh", 1)
+
+    far = shift(after(jnp.stack([R[3, 0], near[0]]), C[-1, 1]), "z", 1)
+    R[4, 0], R[2, 1] = (far, 0), (far, 1)
+    R[-2, 1] = shift(after(near[1], R[-3, 0], R[3, 0]), "z", -1)
+    R[-3, 1] = shift(after(R[-2, 1], C[2, 0], C[2, 1]), "z", -1)
+    R[3, 1] = shift(far[1], "z", 1)
     R[4, 1] = shift(R[-3, 1], "z", -1)
 
     cols = [C[dx, dy] for dx in STEPS for dy in (0, 1)]
-    gates = ((R[3, 0], R[-3, 0]), (R[4, 0], R[-3, 1]), ())
-    out = None
-    for group, gate in zip(GROUPS, gates):
-        pieces = after([R[p] for p in group], *gate)
-        keep, send = cross(scal, pieces, cols)
-        out = lags(scal, group, keep, shift(send, "c", 1), table, out)
+    own = [R[p] for p in GROUPS[0]]
+    keep, send, cols = cross(scal, gate(own, R[3, 0], R[-3, 0])[0], cols, True)
+    recv = shift(send, "c", 1)
+    own, _ = gate([R[p] for p in GROUPS[1]], far, R[-3, 1])
+    keep1, send1 = cross(scal, own, cols, False)
+    recv1 = shift(send1, "c", 1)
+    out = lags(scal, GROUPS[0], keep, recv, table, None)
+    own, (out,) = gate([R[p] for p in GROUPS[2]], out)
+    keep2, send2 = cross(scal, own, cols, False)
+    recv2 = shift(send2, "c", 1)
+    out = lags(scal, GROUPS[1], keep1, recv1, table, out)
+    out = lags(scal, GROUPS[2], keep2, recv2, table, out)
     return out.reshape(N_Z * 20, COLS, LAGS)
 
 

time: 154 us -> 128 us (0.83)
  Pallas kernels: 59.2 us -> 38.2 us
  waiting for transfers between devices: 43.1 us -> 48.5 us
  starting transfers between devices: 39.2 us -> 34.6 us
  local copies, waits for them, and re-layouts: 9.2 us -> 5.51 us
  other arithmetic: 2.33 us -> 0.42 us
    pallas_call x6, Pallas kernels: 53.8 us -> 34.7 us  [the longest x3 26.8 us: cross(): pl.pallas_call(functools.partial(cross_kernel, n, lead), out_shape=(shape...]
    ppermute x24, waiting for transfers between devices: 43.1 us -> 48.5 us  [shift(): return lax.ppermute(x, axis, [(i, (i + step) % n) for i in range(n)])]
    ppermute x24, starting transfers between devices: 39.2 us -> 34.6 us  [shift(): return lax.ppermute(x, axis, [(i, (i + step) % n) for i in range(n)])]
    pallas_call x1, Pallas kernels: 5.35 us -> 3.5 us  [whiten(): pl.pallas_call(whiten_kernel, out_shape=(msg, msg), in_specs=[pl.BlockSpe...]
    squeeze x2, local copies, waits for them, and re-layouts: 1.98 us -> 0.17 us  [the longest x1 0.11 us: shards(): R[-2, 1] = shift(after(near[1], R[-3, 0], R[3, 0]), 'z', -1)]
    unnamed x40 -> x10, local copies, waits for them, and re-layouts: 4.76 us -> 4.5 us
  transfers between devices with their start and end apart: 24 -> 24, of which waited for: 11 -> 13; matrix products, arithmetic and copies ran while one was open for 3% -> 0% of each run, Pallas kernels for 33% -> 26%
where the time goes in v4:
time: 128 us
  waiting for transfers between devices  48.5 us (38%)
  Pallas kernels  38.2 us (30%)
  starting transfers between devices  34.6 us (27%)
  local copies, waits for them, and re-layouts  5.51 us (4%)
    ppermute x24, waiting for transfers between devices, shift(): return lax.ppermute(x, axis, [(i, (i + step) % n) for i in range(n)])  48.5 us
    ppermute x24, starting transfers between devices, shift(): return lax.ppermute(x, axis, [(i, (i + step) % n) for i in range(n)])  34.6 us
    pallas_call x3, Pallas kernels, cross(): pl.pallas_call(functools.partial(cross_kernel, n, lead), out_shape=(shape...  26.8 us
    pallas_call x3, Pallas kernels, lags(): pl.pallas_call(functools.partial(lags_kernel, group), out_shape=jax.Shape...  7.92 us
    unnamed x10, local copies, waits for them, and re-layouts  4.5 us
    pallas_call x1, Pallas kernels, whiten(): pl.pallas_call(whiten_kernel, out_shape=(msg, msg), in_specs=[pl.BlockSpe...  3.5 us
  transfers between devices with their start and end apart: 24, of which 13 were waited for; matrix products, arithmetic and copies ran while one was open for 0% of the time, Pallas kernels for 26%

profile of v4, /device:TPU:1, one launch (start us, length us, event | category | flops | bytes accessed | tf_op | source)
XLA Modules:
  0.0 127.6 jit_solution(17538209715425813551)
XLA Ops:
  0.7 1.3 %copy-done.1 = f32[5,64,2,512]{3,2,1,0:T(2,128)S(1)} copy-done((f32[5,64,2,512]{3,2,1,0:T(2,128)S(1)}, f32[5,64,2,512]{3,2,1,0:T(2,128)}, u32[]{:S(2)}) %copy-start.1) | copy-done | bytes 1310744
  2.7 3.5 %whiten.1 = (bf16[2,256,640]{2,1,0:T(8,128)(2,1)S(1)}, bf16[2,256,640]{2,1,0:T(8,128)(2,1)S(1)}) custom-call(s32[10]{0:T(128)S(1)} %concatenate.3.scal, f32[2560,128]{1,0:T(8,128)S(1)} %bitcast.33, s32[5,64]{1,0:T(8,128)S(1)} %copy-done.2), custom_call_target="tpu_custom_call" | custom-call | flops 1000000000 | bytes 3000000 | tf_op jit(solution)/shard_map/whiten/pallas_call | solution.py:93
  6.2 3.3 %collective-permute-start = (bf16[2,256,640]{2,1,0:T(8,128)(2,1)S(1)}, bf16[2,256,640]{2,1,0:T(8,128)(2,1)S(1)}, u32[]{:S(2)}, u32[]{:S(2)}) collective-permute-start(bf16[2,256,640]{2,1,0:T(8,128)(2,1)S(1)} %get-tuple-element.44), channel_id=1, source_target_pairs={{0,1},{1,0},{2,3},{3,2},{4,5},{5,4},{6,7},{7,6},{8,9},{9,8},{10,11... | collective-permute-start | bytes 1966088 | tf_op jit(solution)/shard_map/ppermute | solution.py:35
  9.6 1.7 %collective-permute-done = bf16[2,256,640]{2,1,0:T(8,128)(2,1)S(1)} collective-permute-done((bf16[2,256,640]{2,1,0:T(8,128)(2,1)S(1)}, bf16[2,256,640]{2,1,0:T(8,128)(2,1)S(1)}, u32[]{:S(2)}, u32[]{:S(2)}) %collective-permute-start) | collective-permute-done | bytes 655392 | tf_op jit(solution)/shard_map/ppermute | solution.py:35
  11.4 3.9 %collective-permute-start.5 = (bf16[2,256,640]{2,1,0:T(8,128)(2,1)S(1)}, bf16[2,256,640]{2,1,0:T(8,128)(2,1)S(1)}, u32[]{:S(2)}, u32[]{:S(2)}) collective-permute-start(bf16[2,256,640]{2,1,0:T(8,128)(2,1)S(1)} %pad_maximum_fusion.2.refs_0_), channel_id=1, source_target_pairs={{0,28},{4,0},{8,4},{12,8},{16,12},{20,16},{24,20},{28,24},{1,29},{... | collective-permute-start | bytes 1966088 | tf_op jit(solution)/shard_map/ppermute | solution.py:35
  15.4 1.4 %collective-permute-start.6 = (bf16[2,256,640]{2,1,0:T(8,128)(2,1)S(1)}, bf16[2,256,640]{2,1,0:T(8,128)(2,1)S(1)}, u32[]{:S(2)}, u32[]{:S(2)}) collective-permute-start(bf16[2,256,640]{2,1,0:T(8,128)(2,1)S(1)} %pad_maximum_fusion.3.refs_9_), channel_id=1, source_target_pairs={{0,32},{32,0},{1,33},{33,1},{2,34},{34,2},{3,35},{35,3},{4,36},{36... | collective-permute-start | bytes 1966088 | tf_op jit(solution)/shard_map/ppermute | solution.py:35
  16.8 1.2 collective-permute-start.8
  18.0 1.5 %collective-permute-start.3 = (bf16[2,256,640]{2,1,0:T(8,128)(2,1)S(1)}, bf16[2,256,640]{2,1,0:T(8,128)(2,1)S(1)}, u32[]{:S(2)}, u32[]{:S(2)}) collective-permute-start(bf16[2,256,640]{2,1,0:T(8,128)(2,1)S(1)} %pad_maximum_fusion.3.refs_9_), channel_id=1, source_target_pairs={{0,192},{64,0},{128,64},{192,128},{1,193},{65,1},{129,65},{193,129... | collective-permute-start | bytes 1966088 | tf_op jit(solution)/shard_map/ppermute | solution.py:35
  19.5 9.6 %collective-permute-done.5.refs_2_ = bf16[2,256,640]{2,1,0:T(8,128)(2,1)S(1)} collective-permute-done((bf16[2,256,640]{2,1,0:T(8,128)(2,1)S(1)}, bf16[2,256,640]{2,1,0:T(8,128)(2,1)S(1)}, u32[]{:S(2)}, u32[]{:S(2)}) %collective-permute-start.5) | collective-permute-done | bytes 655392 | tf_op jit(solution)/shard_map/ppermute | solution.py:35
  29.1 3.1 %collective-permute-done.1.refs_1_ = bf16[2,256,640]{2,1,0:T(8,128)(2,1)S(1)} collective-permute-done((bf16[2,256,640]{2,1,0:T(8,128)(2,1)S(1)}, bf16[2,256,640]{2,1,0:T(8,128)(2,1)S(1)}, u32[]{:S(2)}, u32[]{:S(2)}) %collective-permute-start.1) | collective-permute-done | bytes 655392 | tf_op jit(solution)/shard_map/ppermute | solution.py:35
  32.3 3.0 %collective-permute-start.7 = (bf16[2,2,256,640]{3,2,1,0:T(8,128)(2,1)S(1)}, bf16[2,2,256,640]{3,2,1,0:T(8,128)(2,1)S(1)}, u32[]{:S(2)}, u32[]{:S(2)}) collective-permute-start(bf16[2,2,256,640]{3,2,1,0:T(8,128)(2,1)S(1)} %pad_maximum_fusion), channel_id=1, source_target_pairs={{0,2},{2,0},{1,3},{3,1},{4,6},{6,4},{5,7},{7,5},{8,10},{10,8},{9,1... | collective-permute-start | bytes 3932168 | tf_op jit(solution)/shard_map/ppermute | solution.py:35
  36.8 2.5 %collective-permute-start.9 = (bf16[2,256,640]{2,1,0:T(8,128)(2,1)S(1)}, bf16[2,256,640]{2,1,0:T(8,128)(2,1)S(1)}, u32[]{:S(2)}, u32[]{:S(2)}) collective-permute-start(bf16[2,256,640]{2,1,0:T(8,128)(2,1)S(1)} %collective-permute-done.6.refs_10_), channel_id=1, source_target_pairs={{0,192},{64,0},{128,64},{192,128},{1,193},{65,1},{129,65},{193,129... | collective-permute-start | bytes 1966088 | tf_op jit(solution)/shard_map/ppermute | solution.py:35
  39.3 10.5 %collective-permute-done.12.refs_4_ = bf16[2,256,640]{2,1,0:T(8,128)(2,1)S(1)} collective-permute-done((bf16[2,256,640]{2,1,0:T(8,128)(2,1)S(1)}, bf16[2,256,640]{2,1,0:T(8,128)(2,1)S(1)}, u32[]{:S(2)}, u32[]{:S(2)}) %collective-permute-start.12) | collective-permute-done | bytes 655392 | tf_op jit(solution)/shard_map/ppermute | solution.py:35
  49.8 1.7 %collective-permute-done.2.refs_3_ = bf16[2,256,640]{2,1,0:T(8,128)(2,1)S(1)} collective-permute-done((bf16[2,256,640]{2,1,0:T(8,128)(2,1)S(1)}, bf16[2,256,640]{2,1,0:T(8,128)(2,1)S(1)}, u32[]{:S(2)}, u32[]{:S(2)}) %collective-permute-start.2) | collective-permute-done | bytes 655392 | tf_op jit(solution)/shard_map/ppermute | solution.py:35
  51.7 1.2 collective-permute-start.4
  52.9 1.2 collective-permute-done.15.refs_12_
  54.1 1.3 %collective-permute-start.17 = (bf16[2,256,640]{2,1,0:T(8,128)(2,1)S(1)}, bf16[2,256,640]{2,1,0:T(8,128)(2,1)S(1)}, u32[]{:S(2)}, u32[]{:S(2)}) collective-permute-start(bf16[2,256,640]{2,1,0:T(8,128)(2,1)S(1)} %collective-permute-done.9.refs_14_), channel_id=1, source_target_pairs={{0,192},{64,0},{128,64},{192,128},{1,193},{65,1},{129,65},{193,129... | collective-permute-start | bytes 1966088 | tf_op jit(solution)/shard_map/ppermute | solution.py:35
  55.5 7.1 %collective-permute-done.7.refs_7_.refs_8_ = bf16[2,2,256,640]{3,2,1,0:T(8,128)(2,1)S(1)} collective-permute-done((bf16[2,2,256,640]{3,2,1,0:T(8,128)(2,1)S(1)}, bf16[2,2,256,640]{3,2,1,0:T(8,128)(2,1)S(1)}, u32[]{:S(2)}, u32[]{:S(2)}) %collective-permute-start.7) | collective-permute-done | bytes 1310752 | tf_op jit(solution)/shard_map/ppermute | solution.py:35
  62.8 1.5 %collective-permute-done.13.refs_6_ = bf16[2,256,640]{2,1,0:T(8,128)(2,1)S(1)} collective-permute-done((bf16[2,256,640]{2,1,0:T(8,128)(2,1)S(1)}, bf16[2,256,640]{2,1,0:T(8,128)(2,1)S(1)}, u32[]{:S(2)}, u32[]{:S(2)}) %collective-permute-start.13) | collective-permute-done | bytes 655392 | tf_op jit(solution)/shard_map/ppermute | solution.py:35
  64.3 1.5 %collective-permute-done.4.refs_5_ = bf16[2,256,640]{2,1,0:T(8,128)(2,1)S(1)} collective-permute-done((bf16[2,256,640]{2,1,0:T(8,128)(2,1)S(1)}, bf16[2,256,640]{2,1,0:T(8,128)(2,1)S(1)}, u32[]{:S(2)}, u32[]{:S(2)}) %collective-permute-start.4) | collective-permute-done | bytes 655392 | tf_op jit(solution)/shard_map/ppermute | solution.py:35
  68.7 9.1 %collective-permute-done.14.refs_1_ = bf16[2,256,640]{2,1,0:T(8,128)(2,1)S(1)} collective-permute-done((bf16[2,256,640]{2,1,0:T(8,128)(2,1)S(1)}, bf16[2,256,640]{2,1,0:T(8,128)(2,1)S(1)}, u32[]{:S(2)}, u32[]{:S(2)}) %collective-permute-start.14) | collective-permute-done | bytes 655392 | tf_op jit(solution)/shard_map/ppermute | solution.py:35
  77.8 1.8 %collective-permute-start.18 = (bf16[2,256,640]{2,1,0:T(8,128)(2,1)S(1)}, bf16[2,256,640]{2,1,0:T(8,128)(2,1)S(1)}, u32[]{:S(2)}, u32[]{:S(2)}) collective-permute-start(bf16[2,256,640]{2,1,0:T(8,128)(2,1)S(1)} %collective-permute-done.14.refs_1_), channel_id=1, source_target_pairs={{0,28},{4,0},{8,4},{12,8},{16,12},{20,16},{24,20},{28,24},{1,29},{... | collective-permute-start | bytes 1966088 | tf_op jit(solution)/shard_map/ppermute | solution.py:35
  79.6 13.0 %cross.3 = (bf16[90,40,256]{2,1,0:T(8,128)(2,1)S(1)}, bf16[90,40,256]{2,1,0:T(8,128)(2,1)S(1)}, bf16[256,80,128]{2,1,0:T(8,128)(2,1)}) custom-call(s32[10]{0:T(128)S(1)} %concatenate.3.scal, bf16[2,256,640]{2,1,0:T(8,128)(2,1)S(1)} %pad_maximum_fusion.2.refs_0_, bf16[2,256,640]{2,1,0:T(8,128)(2,1)S(1)} %collective-permute-done.1.refs_1_, ...), custom_call_target="tpu_custom_call" | custom-call | flops 10000000000 | bytes 10000000 | tf_op jit(solution)/shard_map/cross/pallas_call | solution.py:185
  92.5 5.7 %collective-permute-start.20 = (bf16[90,40,256]{2,1,0:T(8,128)(2,1)S(1)}, bf16[90,40,256]{2,1,0:T(8,128)(2,1)S(1)}, u32[]{:S(2)}, u32[]{:S(2)}) collective-permute-start(bf16[90,40,256]{2,1,0:T(8,128)(2,1)S(1)} %get-tuple-element.66), channel_id=1, source_target_pairs={{0,1},{1,0},{2,3},{3,2},{4,5},{5,4},{6,7},{7,6},{8,9},{9,8},{10,11... | collective-permute-start | bytes 5529608 | tf_op jit(solution)/shard_map/ppermute | solution.py:35
  98.3 1.6 %collective-permute-start.11 = (bf16[2,256,640]{2,1,0:T(8,128)(2,1)S(1)}, bf16[2,256,640]{2,1,0:T(8,128)(2,1)S(1)}, u32[]{:S(2)}, u32[]{:S(2)}) collective-permute-start(bf16[2,256,640]{2,1,0:T(8,128)(2,1)S(1)} %slice_bitcast_fusion.1), channel_id=1, source_target_pairs={{0,4},{4,8},{8,12},{12,16},{16,20},{20,24},{24,28},{28,0},{1,5},{5... | collective-permute-start | bytes 1966088 | tf_op jit(solution)/shard_map/ppermute | solution.py:35
  99.9 2.5 %copy-done.3 = bf16[256,80,128]{2,1,0:T(8,128)(2,1)S(1)} copy-done((bf16[256,80,128]{2,1,0:T(8,128)(2,1)S(1)}, bf16[256,80,128]{2,1,0:T(8,128)(2,1)}, u32[]{:S(2)}) %copy-start.3) | copy-done | bytes 5242904
  102.3 7.8 %cross.5 = (bf16[50,40,256]{2,1,0:T(8,128)(2,1)S(1)}, bf16[50,40,256]{2,1,0:T(8,128)(2,1)S(1)}) custom-call(s32[10]{0:T(128)S(1)} %concatenate.3.scal, bf16[2,256,640]{2,1,0:T(8,128)(2,1)S(1)} %collective-permute-done.22.refs_0_, bf16[2,256,640]{2,1,0:T(8,128)(2,1)S(1)} %collective-permute-done.14.refs_1_, ...), custom_call_target="tpu_custom_call" | custom-call | flops 10000000000 | bytes 10000000 | tf_op jit(solution)/shard_map/cross/pallas_call | solution.py:185
  111.0 3.5 %lags.3.rest_0_ = bf16[6400,512]{1,0:T(8,128)(2,1)} custom-call(s32[10]{0:T(128)S(1)} %concatenate.3.scal, bf16[3600,256]{1,0:T(8,128)(2,1)S(1)} %bitcast.24, bf16[3600,256]{1,0:T(8,128)(2,1)S(1)} %bitcast.25, bf16[2,256,512]{2,1,0:T(8,128)(2,1)S(1)} %copy-done), custom_call_target="tpu_custom_call" | custom-call | flops 2000000000 | bytes 3000000 | tf_op jit(solution)/shard_map/lags/pallas_call | solution.py:226
  114.9 6.0 %cross.4 = (bf16[20,40,256]{2,1,0:T(8,128)(2,1)S(1)}, bf16[20,40,256]{2,1,0:T(8,128)(2,1)S(1)}) custom-call(s32[10]{0:T(128)S(1)} %concatenate.3.scal, bf16[2,256,640]{2,1,0:T(8,128)(2,1)S(1)} %collective-permute-done.11.refs_0_, bf16[2,256,640]{2,1,0:T(8,128)(2,1)S(1)} %collective-permute-done.19.refs_1_, bf16[256,80,128]{2,1,0:T(8,128)(2,1)S(1)} %copy-done.4), custom_call_target="tpu_custom_call" | custom-call | flops 10000000000 | bytes 10000000 | tf_op jit(solution)/shard_map/cross/pallas_call | solution.py:185
  121.0 1.9 %collective-permute-start.21 = (bf16[20,40,256]{2,1,0:T(8,128)(2,1)S(1)}, bf16[20,40,256]{2,1,0:T(8,128)(2,1)S(1)}, u32[]{:S(2)}, u32[]{:S(2)}) collective-permute-start(bf16[20,40,256]{2,1,0:T(8,128)(2,1)S(1)} %get-tuple-element.71), channel_id=1, source_target_pairs={{0,1},{1,0},{2,3},{3,2},{4,5},{5,4},{6,7},{7,6},{8,9},{9,8},{10,11... | collective-permute-start | bytes 1228808 | tf_op jit(solution)/shard_map/ppermute | solution.py:35
  122.9 2.6 %lags.4.rest_0_ = bf16[6400,512]{1,0:T(8,128)(2,1)} custom-call(s32[10]{0:T(128)S(1)} %concatenate.3.scal, bf16[2000,256]{1,0:T(8,128)(2,1)S(1)} %bitcast.26, bf16[2000,256]{1,0:T(8,128)(2,1)S(1)} %bitcast.27, bf16[2,256,512]{2,1,0:T(8,128)(2,1)S(1)} %copy-done, bf16[6400,512]{1,0:T(8,128)(2,1)} %lags.3.rest_0_), custom_call_target="tpu_custom_call", output_to_operand_aliasing={{}: (4, {})} | custom-call | flops 2000000000 | bytes 3000000 | tf_op jit(solution)/shard_map/lags/pallas_call | solution.py:226
  125.5 1.9 %lags.5 = bf16[6400,512]{1,0:T(8,128)(2,1)} custom-call(s32[10]{0:T(128)S(1)} %concatenate.3.scal, bf16[800,256]{1,0:T(8,128)(2,1)S(1)} %bitcast.31, bf16[800,256]{1,0:T(8,128)(2,1)S(1)} %bitcast.32, bf16[2,256,512]{2,1,0:T(8,128)(2,1)S(1)} %copy-done, bf16[6400,512]{1,0:T(8,128)(2,1)} %lags.4.rest_0_), custom_call_target="tpu_custom_call", output_to_operand_aliasing={{}: (4, {})} | custom-call | flops 2000000000 | bytes 3000000 | tf_op jit(solution)/shard_map/lags/pallas_call | solution.py:226
  (42 shorter events, 8.1 us)
Async XLA Ops:
  0.7 1.3 %copy-start.1 = (f32[5,64,2,512]{3,2,1,0:T(2,128)S(1)}, f32[5,64,2,512]{3,2,1,0:T(2,128)}, u32[]{:S(2)}) copy-start(f32[5,64,2,512]{3,2,1,0:T(2,128)} %param.4) | copy-start | bytes 3932164
  2.1 0.7 copy-start.2
  6.2 5.0 %collective-permute-start = (bf16[2,256,640]{2,1,0:T(8,128)(2,1)S(1)}, bf16[2,256,640]{2,1,0:T(8,128)(2,1)S(1)}, u32[]{:S(2)}, u32[]{:S(2)}) collective-permute-start(bf16[2,256,640]{2,1,0:T(8,128)(2,1)S(1)} %get-tuple-element.44), channel_id=1, source_target_pairs={{0,1},{1,0},{2,3},{3,2},{4,5},{5,4},{6,7},{7,6},{8,9},{9,8},{10,11... | collective-permute-start | bytes 1966088 | tf_op jit(solution)/shard_map/ppermute | solution.py:35
  11.4 17.7 %collective-permute-start.5 = (bf16[2,256,640]{2,1,0:T(8,128)(2,1)S(1)}, bf16[2,256,640]{2,1,0:T(8,128)(2,1)S(1)}, u32[]{:S(2)}, u32[]{:S(2)}) collective-permute-start(bf16[2,256,640]{2,1,0:T(8,128)(2,1)S(1)} %pad_maximum_fusion.2.refs_0_), channel_id=1, source_target_pairs={{0,28},{4,0},{8,4},{12,8},{16,12},{20,16},{24,20},{28,24},{1,29},{... | collective-permute-start | bytes 1966088 | tf_op jit(solution)/shard_map/ppermute | solution.py:35
  15.3 16.8 %collective-permute-start.1 = (bf16[2,256,640]{2,1,0:T(8,128)(2,1)S(1)}, bf16[2,256,640]{2,1,0:T(8,128)(2,1)S(1)}, u32[]{:S(2)}, u32[]{:S(2)}) collective-permute-start(bf16[2,256,640]{2,1,0:T(8,128)(2,1)S(1)} %pad_maximum_fusion.2.refs_0_), channel_id=1, source_target_pairs={{0,4},{4,8},{8,12},{12,16},{16,20},{20,24},{24,28},{28,0},{1,5},{5... | collective-permute-start | bytes 1966088 | tf_op jit(solution)/shard_map/ppermute | solution.py:35
  15.4 16.9 %collective-permute-start.6 = (bf16[2,256,640]{2,1,0:T(8,128)(2,1)S(1)}, bf16[2,256,640]{2,1,0:T(8,128)(2,1)S(1)}, u32[]{:S(2)}, u32[]{:S(2)}) collective-permute-start(bf16[2,256,640]{2,1,0:T(8,128)(2,1)S(1)} %pad_maximum_fusion.3.refs_9_), channel_id=1, source_target_pairs={{0,32},{32,0},{1,33},{33,1},{2,34},{34,2},{3,35},{35,3},{4,36},{36... | collective-permute-start | bytes 1966088 | tf_op jit(solution)/shard_map/ppermute | solution.py:35
  16.8 20.0 %collective-permute-start.8 = (bf16[2,256,640]{2,1,0:T(8,128)(2,1)S(1)}, bf16[2,256,640]{2,1,0:T(8,128)(2,1)S(1)}, u32[]{:S(2)}, u32[]{:S(2)}) collective-permute-start(bf16[2,256,640]{2,1,0:T(8,128)(2,1)S(1)} %pad_maximum_fusion.3.refs_9_), channel_id=1, source_target_pairs={{0,64},{64,128},{128,192},{192,0},{1,65},{65,129},{129,193},{193,1... | collective-permute-start | bytes 1966088 | tf_op jit(solution)/shard_map/ppermute | solution.py:35
  18.0 18.8 %collective-permute-start.3 = (bf16[2,256,640]{2,1,0:T(8,128)(2,1)S(1)}, bf16[2,256,640]{2,1,0:T(8,128)(2,1)S(1)}, u32[]{:S(2)}, u32[]{:S(2)}) collective-permute-start(bf16[2,256,640]{2,1,0:T(8,128)(2,1)S(1)} %pad_maximum_fusion.3.refs_9_), channel_id=1, source_target_pairs={{0,192},{64,0},{128,64},{192,128},{1,193},{65,1},{129,65},{193,129... | collective-permute-start | bytes 1966088 | tf_op jit(solution)/shard_map/ppermute | solution.py:35
  32.3 30.3 %collective-permute-start.7 = (bf16[2,2,256,640]{3,2,1,0:T(8,128)(2,1)S(1)}, bf16[2,2,256,640]{3,2,1,0:T(8,128)(2,1)S(1)}, u32[]{:S(2)}, u32[]{:S(2)}) collective-permute-start(bf16[2,2,256,640]{3,2,1,0:T(8,128)(2,1)S(1)} %pad_maximum_fusion), channel_id=1, source_target_pairs={{0,2},{2,0},{1,3},{3,1},{4,6},{6,4},{5,7},{7,5},{8,10},{10,8},{9,1... | collective-permute-start | bytes 3932168 | tf_op jit(solution)/shard_map/ppermute | solution.py:35
  35.3 14.4 %collective-permute-start.12 = (bf16[2,256,640]{2,1,0:T(8,128)(2,1)S(1)}, bf16[2,256,640]{2,1,0:T(8,128)(2,1)S(1)}, u32[]{:S(2)}, u32[]{:S(2)}) collective-permute-start(bf16[2,256,640]{2,1,0:T(8,128)(2,1)S(1)} %collective-permute-done.5.refs_2_), channel_id=1, source_target_pairs={{0,28},{4,0},{8,4},{12,8},{16,12},{20,16},{24,20},{28,24},{1,29},{... | collective-permute-start | bytes 1966088 | tf_op jit(solution)/shard_map/ppermute | solution.py:35
  36.4 15.0 %collective-permute-start.2 = (bf16[2,256,640]{2,1,0:T(8,128)(2,1)S(1)}, bf16[2,256,640]{2,1,0:T(8,128)(2,1)S(1)}, u32[]{:S(2)}, u32[]{:S(2)}) collective-permute-start(bf16[2,256,640]{2,1,0:T(8,128)(2,1)S(1)} %collective-permute-done.1.refs_1_), channel_id=1, source_target_pairs={{0,4},{4,8},{8,12},{12,16},{16,20},{20,24},{24,28},{28,0},{1,5},{5... | collective-permute-start | bytes 1966088 | tf_op jit(solution)/shard_map/ppermute | solution.py:35
  36.8 16.1 %collective-permute-start.9 = (bf16[2,256,640]{2,1,0:T(8,128)(2,1)S(1)}, bf16[2,256,640]{2,1,0:T(8,128)(2,1)S(1)}, u32[]{:S(2)}, u32[]{:S(2)}) collective-permute-start(bf16[2,256,640]{2,1,0:T(8,128)(2,1)S(1)} %collective-permute-done.6.refs_10_), channel_id=1, source_target_pairs={{0,192},{64,0},{128,64},{192,128},{1,193},{65,1},{129,65},{193,129... | collective-permute-start | bytes 1966088 | tf_op jit(solution)/shard_map/ppermute | solution.py:35
  39.3 14.8 %collective-permute-start.15 = (bf16[2,256,640]{2,1,0:T(8,128)(2,1)S(1)}, bf16[2,256,640]{2,1,0:T(8,128)(2,1)S(1)}, u32[]{:S(2)}, u32[]{:S(2)}) collective-permute-start(bf16[2,256,640]{2,1,0:T(8,128)(2,1)S(1)} %collective-permute-done.6.refs_10_), channel_id=1, source_target_pairs={{0,64},{64,128},{128,192},{192,0},{1,65},{65,129},{129,193},{193,1... | collective-permute-start | bytes 1966088 | tf_op jit(solution)/shard_map/ppermute | solution.py:35
  51.4 12.9 %collective-permute-start.13 = (bf16[2,256,640]{2,1,0:T(8,128)(2,1)S(1)}, bf16[2,256,640]{2,1,0:T(8,128)(2,1)S(1)}, u32[]{:S(2)}, u32[]{:S(2)}) collective-permute-start(bf16[2,256,640]{2,1,0:T(8,128)(2,1)S(1)} %collective-permute-done.12.refs_4_), channel_id=1, source_target_pairs={{0,28},{4,0},{8,4},{12,8},{16,12},{20,16},{24,20},{28,24},{1,29},{... | collective-permute-start | bytes 1966088 | tf_op jit(solution)/shard_map/ppermute | solution.py:35
  51.7 14.1 %collective-permute-start.4 = (bf16[2,256,640]{2,1,0:T(8,128)(2,1)S(1)}, bf16[2,256,640]{2,1,0:T(8,128)(2,1)S(1)}, u32[]{:S(2)}, u32[]{:S(2)}) collective-permute-start(bf16[2,256,640]{2,1,0:T(8,128)(2,1)S(1)} %collective-permute-done.2.refs_3_), channel_id=1, source_target_pairs={{0,4},{4,8},{8,12},{12,16},{16,20},{20,24},{24,28},{28,0},{1,5},{5... | collective-permute-start | bytes 1966088 | tf_op jit(solution)/shard_map/ppermute | solution.py:35
  54.1 13.5 %collective-permute-start.17 = (bf16[2,256,640]{2,1,0:T(8,128)(2,1)S(1)}, bf16[2,256,640]{2,1,0:T(8,128)(2,1)S(1)}, u32[]{:S(2)}, u32[]{:S(2)}) collective-permute-start(bf16[2,256,640]{2,1,0:T(8,128)(2,1)S(1)} %collective-permute-done.9.refs_14_), channel_id=1, source_target_pairs={{0,192},{64,0},{128,64},{192,128},{1,193},{65,1},{129,65},{193,129... | collective-permute-start | bytes 1966088 | tf_op jit(solution)/shard_map/ppermute | solution.py:35
  55.4 13.3 %collective-permute-start.16 = (bf16[2,256,640]{2,1,0:T(8,128)(2,1)S(1)}, bf16[2,256,640]{2,1,0:T(8,128)(2,1)S(1)}, u32[]{:S(2)}, u32[]{:S(2)}) collective-permute-start(bf16[2,256,640]{2,1,0:T(8,128)(2,1)S(1)} %collective-permute-done.8.refs_11_), channel_id=1, source_target_pairs={{0,64},{64,128},{128,192},{192,0},{1,65},{65,129},{129,193},{193,1... | collective-permute-start | bytes 1966088 | tf_op jit(solution)/shard_map/ppermute | solution.py:35
  65.8 12.0 %collective-permute-start.14 = (bf16[2,256,640]{2,1,0:T(8,128)(2,1)S(1)}, bf16[2,256,640]{2,1,0:T(8,128)(2,1)S(1)}, u32[]{:S(2)}, u32[]{:S(2)}) collective-permute-start(bf16[2,256,640]{2,1,0:T(8,128)(2,1)S(1)} %get-tuple-element.51), channel_id=1, source_target_pairs={{0,28},{4,0},{8,4},{12,8},{16,12},{20,16},{24,20},{28,24},{1,29},{... | collective-permute-start | bytes 1966088 | tf_op jit(solution)/shard_map/ppermute | solution.py:35
  66.1 32.1 %collective-permute-start.22 = (bf16[2,256,640]{2,1,0:T(8,128)(2,1)S(1)}, bf16[2,256,640]{2,1,0:T(8,128)(2,1)S(1)}, u32[]{:S(2)}, u32[]{:S(2)}) collective-permute-start(bf16[2,256,640]{2,1,0:T(8,128)(2,1)S(1)} %pad_maximum_fusion.2.refs_0_), channel_id=1, source_target_pairs={{0,2},{2,0},{1,3},{3,1},{4,6},{6,4},{5,7},{7,5},{8,10},{10,8},{9,1... | collective-permute-start | bytes 1966088 | tf_op jit(solution)/shard_map/ppermute | solution.py:35
  66.7 31.5 %collective-permute-start.10 = (bf16[2,2,256,640]{3,2,1,0:T(8,128)(2,1)S(1)}, bf16[2,2,256,640]{3,2,1,0:T(8,128)(2,1)S(1)}, u32[]{:S(2)}, u32[]{:S(2)}) collective-permute-start(bf16[2,2,256,640]{3,2,1,0:T(8,128)(2,1)S(1)} %pad_maximum_fusion.1), channel_id=1, source_target_pairs={{0,4},{4,8},{8,12},{12,16},{16,20},{20,24},{24,28},{28,0},{1,5},{5... | collective-permute-start | bytes 3932168 | tf_op jit(solution)/shard_map/ppermute | solution.py:35
  77.8 20.4 %collective-permute-start.18 = (bf16[2,256,640]{2,1,0:T(8,128)(2,1)S(1)}, bf16[2,256,640]{2,1,0:T(8,128)(2,1)S(1)}, u32[]{:S(2)}, u32[]{:S(2)}) collective-permute-start(bf16[2,256,640]{2,1,0:T(8,128)(2,1)S(1)} %collective-permute-done.14.refs_1_), channel_id=1, source_target_pairs={{0,28},{4,0},{8,4},{12,8},{16,12},{20,16},{24,20},{28,24},{1,29},{... | collective-permute-start | bytes 1966088 | tf_op jit(solution)/shard_map/ppermute | solution.py:35
  92.5 18.5 %collective-permute-start.20 = (bf16[90,40,256]{2,1,0:T(8,128)(2,1)S(1)}, bf16[90,40,256]{2,1,0:T(8,128)(2,1)S(1)}, u32[]{:S(2)}, u32[]{:S(2)}) collective-permute-start(bf16[90,40,256]{2,1,0:T(8,128)(2,1)S(1)} %get-tuple-element.66), channel_id=1, source_target_pairs={{0,1},{1,0},{2,3},{3,2},{4,5},{5,4},{6,7},{7,6},{8,9},{9,8},{10,11... | collective-permute-start | bytes 5529608 | tf_op jit(solution)/shard_map/ppermute | solution.py:35
  98.2 16.4 %collective-permute-start.19 = (bf16[2,256,640]{2,1,0:T(8,128)(2,1)S(1)}, bf16[2,256,640]{2,1,0:T(8,128)(2,1)S(1)}, u32[]{:S(2)}, u32[]{:S(2)}) collective-permute-start(bf16[2,256,640]{2,1,0:T(8,128)(2,1)S(1)} %collective-permute-done.18.refs_4_), channel_id=1, source_target_pairs={{0,28},{4,0},{8,4},{12,8},{16,12},{20,16},{24,20},{28,24},{1,29},{... | collective-permute-start | bytes 1966088 | tf_op jit(solution)/shard_map/ppermute | solution.py:35
  98.3 16.6 %collective-permute-start.11 = (bf16[2,256,640]{2,1,0:T(8,128)(2,1)S(1)}, bf16[2,256,640]{2,1,0:T(8,128)(2,1)S(1)}, u32[]{:S(2)}, u32[]{:S(2)}) collective-permute-start(bf16[2,256,640]{2,1,0:T(8,128)(2,1)S(1)} %slice_bitcast_fusion.1), channel_id=1, source_target_pairs={{0,4},{4,8},{8,12},{12,16},{16,20},{20,24},{24,28},{28,0},{1,5},{5... | collective-permute-start | bytes 1966088 | tf_op jit(solution)/shard_map/ppermute | solution.py:35
  99.9 2.5 %copy-start.3 = (bf16[256,80,128]{2,1,0:T(8,128)(2,1)S(1)}, bf16[256,80,128]{2,1,0:T(8,128)(2,1)}, u32[]{:S(2)}) copy-start(bf16[256,80,128]{2,1,0:T(8,128)(2,1)} %get-tuple-element.69.refs_2_.refs_5_) | copy-start | bytes 15728644
  102.3 8.6 %copy-start = (bf16[2,256,512]{2,1,0:T(8,128)(2,1)S(1)}, bf16[2,256,512]{2,1,0:T(8,128)(2,1)}, u32[]{:S(2)}) copy-start(bf16[2,256,512]{2,1,0:T(8,128)(2,1)} %constant.28.table) | copy-start | bytes 1572868
  110.1 12.8 %collective-permute-start.23 = (bf16[50,40,256]{2,1,0:T(8,128)(2,1)S(1)}, bf16[50,40,256]{2,1,0:T(8,128)(2,1)S(1)}, u32[]{:S(2)}, u32[]{:S(2)}) collective-permute-start(bf16[50,40,256]{2,1,0:T(8,128)(2,1)S(1)} %get-tuple-element.79), channel_id=1, source_target_pairs={{0,1},{1,0},{2,3},{3,2},{4,5},{5,4},{6,7},{7,6},{8,9},{9,8},{10,11... | collective-permute-start | bytes 3072008 | tf_op jit(solution)/shard_map/ppermute | solution.py:35
  111.0 3.9 %copy-start.4 = (bf16[256,80,128]{2,1,0:T(8,128)(2,1)S(1)}, bf16[256,80,128]{2,1,0:T(8,128)(2,1)}, u32[]{:S(2)}) copy-start(bf16[256,80,128]{2,1,0:T(8,128)(2,1)} %get-tuple-element.69.refs_2_.refs_5_) | copy-start | bytes 15728644
  121.0 4.5 %collective-permute-start.21 = (bf16[20,40,256]{2,1,0:T(8,128)(2,1)S(1)}, bf16[20,40,256]{2,1,0:T(8,128)(2,1)S(1)}, u32[]{:S(2)}, u32[]{:S(2)}) collective-permute-start(bf16[20,40,256]{2,1,0:T(8,128)(2,1)S(1)} %get-tuple-element.71), channel_id=1, source_target_pairs={{0,1},{1,0},{2,3},{3,2},{4,5},{5,4},{6,7},{7,6},{8,9},{9,8},{10,11... | collective-permute-start | bytes 1228808 | tf_op jit(solution)/shard_map/ppermute | solution.py:35

commit v5 on v4

--- a/solution.py
+++ b/solution.py
@@ -105,13 +105,13 @@
     )(scal, view, valid)
 
 
-UNROLL = 16
+UNROLL = 32
 PITCH = FB + 8
 STEPS = (0, 1, -1, 2)
 MIB = 1024 * 1024
 
 
-def cross_kernel(n, lead, scal, *refs):
+def cross_kernel(n, lead, indices, scal, *refs):
     rows = 10 * n
     pieces, rest = refs[:n], refs[n:]
     x, yl, c = scal[0], scal[1], scal[4]
@@ -120,82 +120,80 @@
     else:
         packed, keep, send, flat, acc = rest
 
-    def spread(piece, into, base):
+    def spread(piece, q, start, into, base):
         for k in range(CH):
             at = pl.multiple_of((base + k) * PITCH, 8)
-            into[pl.ds(at, FB), :] = piece[:, k * K : (k + 1) * K].astype(jnp.float32)
-
-    if lead:
-        for p in range(4):
-            for h in range(2):
-                r = lax.rem(x - STEPS[p] + N_X, N_X) * N_YL + (yl ^ h)
-                for q in range(2):
-                    spread(cols[2 * p + h].at[q], side, q * COLS + r * CH)
-    for p in range(n):
-        for q in range(2):
-            spread(pieces[p].at[q], flat, p * 10 + (c ^ q) * 5)
-
-    def body(i, carry):
-        at = [i * UNROLL + u for u in range(UNROLL)]
-        pairs = []
-        for f in at:
-            first = flat[pl.ds(f, rows, stride=PITCH), :].astype(jnp.bfloat16)
-            if lead:
-                second = side[pl.ds(f, BOTH, stride=PITCH), :].astype(jnp.bfloat16)
-                packed[f] = second
-            else:
-                second = packed[f]
-            pairs.append(
-                lax.dot_general(
-                    first, second, (((1,), (1,)), ((), ())), preferred_element_type=jnp.float32
+            tile = piece[q, pl.ds(start, FB), k * K : (k + 1) * K]
+            into[pl.ds(at, FB), :] = tile.astype(jnp.float32)
+
+    def block(b, carry):
+        start = pl.multiple_of(b * FB, FB)
+        if lead:
+            for p in range(4):
+                for h in range(2):
+                    r = lax.rem(x - STEPS[p] + N_X, N_X) * N_YL + (yl ^ h)
+                    for q in range(2):
+                        spread(cols[2 * p + h], q, start, side, q * COLS + r * CH)
+        for p, index in enumerate(indices):
+            piece = pieces[p] if index is None else pieces[p].at[index]
+            for q in range(2):
+                spread(piece, q, start, flat, p * 10 + (c ^ q) * 5)
+
+        def body(i, carry):
+            at = [i * UNROLL + u for u in range(UNROLL)]
+            pairs = []
+            for f in at:
+                first = flat[pl.ds(f, rows, stride=PITCH), :].astype(jnp.bfloat16)
+                if lead:
+                    second = side[pl.ds(f, BOTH, stride=PITCH), :].astype(jnp.bfloat16)
+                    packed[start + f] = second
+                else:
+                    second = packed[start + f]
+                pairs.append(
+                    lax.dot_general(
+                        first,
+                        second,
+                        (((1,), (1,)), ((), ())),
+                        preferred_element_type=jnp.float32,
+                    )
                 )
-            )
-        for f, pair in zip(at, pairs):
-            acc[pl.ds(f, rows, stride=PITCH), 0:BOTH] = pair
+            for f, pair in zip(at, pairs):
+                acc[pl.ds(f, rows, stride=PITCH), 0:BOTH] = pair
+            return carry
+
+        lax.fori_loop(0, FB // UNROLL, body, 0)
+        for a in range(rows):
+            tile = acc[a * PITCH : a * PITCH + FB, :].T
+            keep[a, :, pl.ds(start, FB)] = tile[0:COLS].astype(jnp.bfloat16)
+            send[a, :, pl.ds(start, FB)] = tile[COLS:BOTH].astype(jnp.bfloat16)
         return carry
 
-    lax.fori_loop(0, FB // UNROLL, body, 0)
-    for a in range(rows):
-        tile = acc[a * PITCH : a * PITCH + FB, :].T
-        keep[a] = tile[0:COLS].astype(jnp.bfloat16)
-        send[a] = tile[COLS:BOTH].astype(jnp.bfloat16)
+    lax.fori_loop(0, HALF // FB, block, 0)
 
 
 def cross(scal, pieces, cols, lead):
     n = len(pieces)
     rows = 10 * n
-    specs, arrays = [], []
-    for piece in pieces:
-        if isinstance(piece, tuple):
-            piece, at = piece
-            specs.append(pl.BlockSpec((None, 2, FB, CH * K), lambda i, s, at=at: (at, 0, i, 0)))
-        else:
-            specs.append(pl.BlockSpec((2, FB, CH * K), lambda i, s: (0, i, 0)))
-        arrays.append(piece)
-    part = pl.BlockSpec((rows, COLS, FB), lambda i, s: (0, 0, i))
+    arrays = [p[0] if isinstance(p, tuple) else p for p in pieces]
+    indices = [p[1] if isinstance(p, tuple) else None for p in pieces]
+    arrays += list(cols) if lead else [cols]
     shape = jax.ShapeDtypeStruct((rows, COLS, HALF), jnp.bfloat16)
-    packed = pl.BlockSpec((FB, BOTH, K), lambda i, s: (i, 0, 0))
     held = jax.ShapeDtypeStruct((HALF, BOTH, K), jnp.bfloat16)
+    outs = (shape, shape, held) if lead else (shape, shape)
     scratch = [pltpu.VMEM((rows * PITCH, K), jnp.float32)] * 2
     if lead:
-        specs += [pl.BlockSpec((2, FB, CH * K), lambda i, s: (0, i, 0))] * len(cols)
         scratch.append(pltpu.VMEM((BOTH * PITCH, K), jnp.float32))
-    else:
-        specs.append(packed)
+    vmem = pl.BlockSpec(memory_space=pltpu.VMEM)
     return pl.pallas_call(
-        functools.partial(cross_kernel, n, lead),
-        out_shape=(shape, shape, held) if lead else (shape, shape),
-        grid_spec=pltpu.PrefetchScalarGridSpec(
-            num_scalar_prefetch=1,
-            grid=(HALF // FB,),
-            in_specs=specs,
-            out_specs=(part, part, packed) if lead else (part, part),
-            scratch_shapes=scratch,
-        ),
-        compiler_params=pltpu.CompilerParams(vmem_limit_bytes=(26 + 3 * n // 2) * MIB),
+        functools.partial(cross_kernel, n, lead, indices),
+        out_shape=outs,
+        in_specs=[pl.BlockSpec(memory_space=pltpu.SMEM)] + [vmem] * len(arrays),
+        out_specs=(vmem,) * len(outs),
+        scratch_shapes=scratch,
+        compiler_params=pltpu.CompilerParams(vmem_limit_bytes=(12 + 3 * n // 2) * MIB),
         cost_estimate=pl.CostEstimate(flops=10**10, bytes_accessed=10**7, transcendentals=0),
         name="cross",
-    )(scal, *arrays, *(cols if lead else [cols]))
+    )(scal, *arrays)
 
 
 def lags_kernel(group, scal, keep, recv, table, *rest):
@@ -273,7 +271,7 @@
 
     R[2, 0] = shift(R[1, 0], "z", 1)
     R[-2, 0] = shift(after(R[-1, 0], R[1, 0]), "z", -1)
-    near = shift(after(jnp.stack([R[1, 0], R[-1, 0]]), C[0, 1]), "yh", 1)
+    near = shift(after(jnp.stack([R[1, 0], R[-1, 0]]), C[0, 1], C[1, 0]), "yh", 1)
     R[1, 1], R[-1, 1] = (near, 0), (near, 1)
     C[1, 1] = shift(after(C[0, 1], R[-1, 0], C[1, 0]), "x", 1)
     C[-1, 1] = shift(after(C[0, 1], C[1, 0], C[-1, 0]), "x", -1)

time: 128 us -> 124 us (0.969)
  Pallas kernels: 38.2 us -> 31.5 us
  starting transfers between devices: 34.6 us -> 39.4 us
  local copies, waits for them, and re-layouts: 5.51 us -> 3.03 us
    pallas_call x3, Pallas kernels: 26.8 us -> 20.1 us  [cross(): pl.pallas_call(functools.partial(cross_kernel, n, lead, indices), out_sha...]
    ppermute x24, starting transfers between devices: 34.6 us -> 39.4 us  [shift(): return lax.ppermute(x, axis, [(i, (i + step) % n) for i in range(n)])]
    unnamed x10 -> x6, local copies, waits for them, and re-layouts: 4.5 us -> 2.01 us
  transfers between devices with their start and end apart: 24 -> 24, of which waited for: 13 -> 9; matrix products, arithmetic and copies ran while one was open for 0% -> 0% of each run, Pallas kernels for 26% -> 21%
where the time goes in v5:
time: 124 us
  waiting for transfers between devices  49.3 us (40%)
  starting transfers between devices  39.4 us (32%)
  Pallas kernels  31.5 us (25%)
  local copies, waits for them, and re-layouts  3.03 us (2%)
    ppermute x24, waiting for transfers between devices, shift(): return lax.ppermute(x, axis, [(i, (i + step) % n) for i in range(n)])  49.3 us
    ppermute x24, starting transfers between devices, shift(): return lax.ppermute(x, axis, [(i, (i + step) % n) for i in range(n)])  39.4 us
    pallas_call x3, Pallas kernels, cross(): pl.pallas_call(functools.partial(cross_kernel, n, lead, indices), out_sha...  20.1 us
    pallas_call x3, Pallas kernels, lags(): pl.pallas_call(functools.partial(lags_kernel, group), out_shape=jax.Shape...  7.92 us
    pallas_call x1, Pallas kernels, whiten(): pl.pallas_call(whiten_kernel, out_shape=(msg, msg), in_specs=[pl.BlockSpe...  3.5 us
  transfers between devices with their start and end apart: 24, of which 9 were waited for; matrix products, arithmetic and copies ran while one was open for 0% of the time, Pallas kernels for 21%

profile of v5, /device:TPU:1, one launch (start us, length us, event | category | flops | bytes accessed | tf_op | source)
XLA Modules:
  0.0 124.0 jit_solution(12229330418743946539)
XLA Ops:
  0.7 1.3 %copy-done.1 = f32[5,64,2,512]{3,2,1,0:T(2,128)S(1)} copy-done((f32[5,64,2,512]{3,2,1,0:T(2,128)S(1)}, f32[5,64,2,512]{3,2,1,0:T(2,128)}, u32[]{:S(2)}) %copy-start.1) | copy-done | bytes 1310744
  2.7 3.5 %whiten.1 = (bf16[2,256,640]{2,1,0:T(8,128)(2,1)S(1)}, bf16[2,256,640]{2,1,0:T(8,128)(2,1)S(1)}) custom-call(s32[10]{0:T(128)S(1)} %concatenate.3.scal, f32[2560,128]{1,0:T(8,128)S(1)} %bitcast.33, s32[5,64]{1,0:T(8,128)S(1)} %copy-done.2), custom_call_target="tpu_custom_call" | custom-call | flops 1000000000 | bytes 3000000 | tf_op jit(solution)/shard_map/whiten/pallas_call | solution.py:93
  6.2 3.3 %collective-permute-start = (bf16[2,256,640]{2,1,0:T(8,128)(2,1)S(1)}, bf16[2,256,640]{2,1,0:T(8,128)(2,1)S(1)}, u32[]{:S(2)}, u32[]{:S(2)}) collective-permute-start(bf16[2,256,640]{2,1,0:T(8,128)(2,1)S(1)} %get-tuple-element.44), channel_id=1, source_target_pairs={{0,1},{1,0},{2,3},{3,2},{4,5},{5,4},{6,7},{7,6},{8,9},{9,8},{10,11... | collective-permute-start | bytes 1966088 | tf_op jit(solution)/shard_map/ppermute | solution.py:35
  9.6 1.7 %collective-permute-done = bf16[2,256,640]{2,1,0:T(8,128)(2,1)S(1)} collective-permute-done((bf16[2,256,640]{2,1,0:T(8,128)(2,1)S(1)}, bf16[2,256,640]{2,1,0:T(8,128)(2,1)S(1)}, u32[]{:S(2)}, u32[]{:S(2)}) %collective-permute-start) | collective-permute-done | bytes 655392 | tf_op jit(solution)/shard_map/ppermute | solution.py:35
  11.4 3.9 %collective-permute-start.5 = (bf16[2,256,640]{2,1,0:T(8,128)(2,1)S(1)}, bf16[2,256,640]{2,1,0:T(8,128)(2,1)S(1)}, u32[]{:S(2)}, u32[]{:S(2)}) collective-permute-start(bf16[2,256,640]{2,1,0:T(8,128)(2,1)S(1)} %pad_maximum_fusion.2.refs_0_), channel_id=1, source_target_pairs={{0,28},{4,0},{8,4},{12,8},{16,12},{20,16},{24,20},{28,24},{1,29},{... | collective-permute-start | bytes 1966088 | tf_op jit(solution)/shard_map/ppermute | solution.py:35
  15.4 1.3 %collective-permute-start.7 = (bf16[2,256,640]{2,1,0:T(8,128)(2,1)S(1)}, bf16[2,256,640]{2,1,0:T(8,128)(2,1)S(1)}, u32[]{:S(2)}, u32[]{:S(2)}) collective-permute-start(bf16[2,256,640]{2,1,0:T(8,128)(2,1)S(1)} %pad_maximum_fusion.3.refs_9_), channel_id=1, source_target_pairs={{0,64},{64,128},{128,192},{192,0},{1,65},{65,129},{129,193},{193,1... | collective-permute-start | bytes 1966088 | tf_op jit(solution)/shard_map/ppermute | solution.py:35
  16.7 1.3 %collective-permute-start.6 = (bf16[2,256,640]{2,1,0:T(8,128)(2,1)S(1)}, bf16[2,256,640]{2,1,0:T(8,128)(2,1)S(1)}, u32[]{:S(2)}, u32[]{:S(2)}) collective-permute-start(bf16[2,256,640]{2,1,0:T(8,128)(2,1)S(1)} %pad_maximum_fusion.3.refs_9_), channel_id=1, source_target_pairs={{0,32},{32,0},{1,33},{33,1},{2,34},{34,2},{3,35},{35,3},{4,36},{36... | collective-permute-start | bytes 1966088 | tf_op jit(solution)/shard_map/ppermute | solution.py:35
  18.0 1.5 %collective-permute-start.3 = (bf16[2,256,640]{2,1,0:T(8,128)(2,1)S(1)}, bf16[2,256,640]{2,1,0:T(8,128)(2,1)S(1)}, u32[]{:S(2)}, u32[]{:S(2)}) collective-permute-start(bf16[2,256,640]{2,1,0:T(8,128)(2,1)S(1)} %pad_maximum_fusion.3.refs_9_), channel_id=1, source_target_pairs={{0,192},{64,0},{128,64},{192,128},{1,193},{65,1},{129,65},{193,129... | collective-permute-start | bytes 1966088 | tf_op jit(solution)/shard_map/ppermute | solution.py:35
  19.5 9.6 %collective-permute-done.5.refs_2_ = bf16[2,256,640]{2,1,0:T(8,128)(2,1)S(1)} collective-permute-done((bf16[2,256,640]{2,1,0:T(8,128)(2,1)S(1)}, bf16[2,256,640]{2,1,0:T(8,128)(2,1)S(1)}, u32[]{:S(2)}, u32[]{:S(2)}) %collective-permute-start.5) | collective-permute-done | bytes 655392 | tf_op jit(solution)/shard_map/ppermute | solution.py:35
  29.1 3.1 %collective-permute-done.1.refs_1_ = bf16[2,256,640]{2,1,0:T(8,128)(2,1)S(1)} collective-permute-done((bf16[2,256,640]{2,1,0:T(8,128)(2,1)S(1)}, bf16[2,256,640]{2,1,0:T(8,128)(2,1)S(1)}, u32[]{:S(2)}, u32[]{:S(2)}) %collective-permute-start.1) | collective-permute-done | bytes 655392 | tf_op jit(solution)/shard_map/ppermute | solution.py:35
  32.3 3.0 %collective-permute-start.8 = (bf16[2,2,256,640]{3,2,1,0:T(8,128)(2,1)S(1)}, bf16[2,2,256,640]{3,2,1,0:T(8,128)(2,1)S(1)}, u32[]{:S(2)}, u32[]{:S(2)}) collective-permute-start(bf16[2,2,256,640]{3,2,1,0:T(8,128)(2,1)S(1)} %pad_maximum_fusion), channel_id=1, source_target_pairs={{0,2},{2,0},{1,3},{3,1},{4,6},{6,4},{5,7},{7,5},{8,10},{10,8},{9,1... | collective-permute-start | bytes 3932168 | tf_op jit(solution)/shard_map/ppermute | solution.py:35
  35.3 2.3 %collective-permute-start.12 = (bf16[2,256,640]{2,1,0:T(8,128)(2,1)S(1)}, bf16[2,256,640]{2,1,0:T(8,128)(2,1)S(1)}, u32[]{:S(2)}, u32[]{:S(2)}) collective-permute-start(bf16[2,256,640]{2,1,0:T(8,128)(2,1)S(1)} %collective-permute-done.5.refs_2_), channel_id=1, source_target_pairs={{0,28},{4,0},{8,4},{12,8},{16,12},{20,16},{24,20},{28,24},{1,29},{... | collective-permute-start | bytes 1966088 | tf_op jit(solution)/shard_map/ppermute | solution.py:35
  37.6 1.7 %collective-permute-start.9 = (bf16[2,256,640]{2,1,0:T(8,128)(2,1)S(1)}, bf16[2,256,640]{2,1,0:T(8,128)(2,1)S(1)}, u32[]{:S(2)}, u32[]{:S(2)}) collective-permute-start(bf16[2,256,640]{2,1,0:T(8,128)(2,1)S(1)} %collective-permute-done.6.refs_10_), channel_id=1, source_target_pairs={{0,192},{64,0},{128,64},{192,128},{1,193},{65,1},{129,65},{193,129... | collective-permute-start | bytes 1966088 | tf_op jit(solution)/shard_map/ppermute | solution.py:35
  39.3 10.5 %collective-permute-done.12.refs_4_ = bf16[2,256,640]{2,1,0:T(8,128)(2,1)S(1)} collective-permute-done((bf16[2,256,640]{2,1,0:T(8,128)(2,1)S(1)}, bf16[2,256,640]{2,1,0:T(8,128)(2,1)S(1)}, u32[]{:S(2)}, u32[]{:S(2)}) %collective-permute-start.12) | collective-permute-done | bytes 655392 | tf_op jit(solution)/shard_map/ppermute | solution.py:35
  49.8 2.9 %collective-permute-done.2.refs_3_ = bf16[2,256,640]{2,1,0:T(8,128)(2,1)S(1)} collective-permute-done((bf16[2,256,640]{2,1,0:T(8,128)(2,1)S(1)}, bf16[2,256,640]{2,1,0:T(8,128)(2,1)S(1)}, u32[]{:S(2)}, u32[]{:S(2)}) %collective-permute-start.2) | collective-permute-done | bytes 655392 | tf_op jit(solution)/shard_map/ppermute | solution.py:35
  52.9 1.2 collective-permute-start.4
  54.1 1.1 collective-permute-start.17
  55.6 7.1 %collective-permute-done.8.refs_7_.refs_8_ = bf16[2,2,256,640]{3,2,1,0:T(8,128)(2,1)S(1)} collective-permute-done((bf16[2,2,256,640]{3,2,1,0:T(8,128)(2,1)S(1)}, bf16[2,2,256,640]{3,2,1,0:T(8,128)(2,1)S(1)}, u32[]{:S(2)}, u32[]{:S(2)}) %collective-permute-start.8) | collective-permute-done | bytes 1310752 | tf_op jit(solution)/shard_map/ppermute | solution.py:35
  62.8 2.7 %collective-permute-done.13.refs_6_ = bf16[2,256,640]{2,1,0:T(8,128)(2,1)S(1)} collective-permute-done((bf16[2,256,640]{2,1,0:T(8,128)(2,1)S(1)}, bf16[2,256,640]{2,1,0:T(8,128)(2,1)S(1)}, u32[]{:S(2)}, u32[]{:S(2)}) %collective-permute-start.13) | collective-permute-done | bytes 655392 | tf_op jit(solution)/shard_map/ppermute | solution.py:35
  65.5 1.5 %collective-permute-done.4.refs_5_ = bf16[2,256,640]{2,1,0:T(8,128)(2,1)S(1)} collective-permute-done((bf16[2,256,640]{2,1,0:T(8,128)(2,1)S(1)}, bf16[2,256,640]{2,1,0:T(8,128)(2,1)S(1)}, u32[]{:S(2)}, u32[]{:S(2)}) %collective-permute-start.4) | collective-permute-done | bytes 655392 | tf_op jit(solution)/shard_map/ppermute | solution.py:35
  68.8 10.2 %collective-permute-done.14.refs_1_ = bf16[2,256,640]{2,1,0:T(8,128)(2,1)S(1)} collective-permute-done((bf16[2,256,640]{2,1,0:T(8,128)(2,1)S(1)}, bf16[2,256,640]{2,1,0:T(8,128)(2,1)S(1)}, u32[]{:S(2)}, u32[]{:S(2)}) %collective-permute-start.14) | collective-permute-done | bytes 655392 | tf_op jit(solution)/shard_map/ppermute | solution.py:35
  79.0 1.8 %collective-permute-start.18 = (bf16[2,256,640]{2,1,0:T(8,128)(2,1)S(1)}, bf16[2,256,640]{2,1,0:T(8,128)(2,1)S(1)}, u32[]{:S(2)}, u32[]{:S(2)}) collective-permute-start(bf16[2,256,640]{2,1,0:T(8,128)(2,1)S(1)} %collective-permute-done.14.refs_1_), channel_id=1, source_target_pairs={{0,28},{4,0},{8,4},{12,8},{16,12},{20,16},{24,20},{28,24},{1,29},{... | collective-permute-start | bytes 1966088 | tf_op jit(solution)/shard_map/ppermute | solution.py:35
  80.8 9.4 %cross.3 = (bf16[90,40,256]{2,1,0:T(8,128)(2,1)S(1)}, bf16[90,40,256]{2,1,0:T(8,128)(2,1)S(1)}, bf16[256,80,128]{2,1,0:T(8,128)(2,1)S(1)}) custom-call(s32[10]{0:T(128)S(1)} %concatenate.3.scal, bf16[2,256,640]{2,1,0:T(8,128)(2,1)S(1)} %pad_maximum_fusion.2.refs_0_, bf16[2,256,640]{2,1,0:T(8,128)(2,1)S(1)} %collective-permute-done.1.refs_1_, ...), custom_call_target="tpu_custom_call" | custom-call | flops 10000000000 | bytes 10000000 | tf_op jit(solution)/shard_map/cross/pallas_call | solution.py:187
  90.2 5.8 %collective-permute-start.20 = (bf16[90,40,256]{2,1,0:T(8,128)(2,1)S(1)}, bf16[90,40,256]{2,1,0:T(8,128)(2,1)S(1)}, u32[]{:S(2)}, u32[]{:S(2)}) collective-permute-start(bf16[90,40,256]{2,1,0:T(8,128)(2,1)S(1)} %get-tuple-element.66), channel_id=1, source_target_pairs={{0,1},{1,0},{2,3},{3,2},{4,5},{5,4},{6,7},{7,6},{8,9},{9,8},{10,11... | collective-permute-start | bytes 5529608 | tf_op jit(solution)/shard_map/ppermute | solution.py:35
  96.0 1.5 %collective-permute-start.11 = (bf16[2,256,640]{2,1,0:T(8,128)(2,1)S(1)}, bf16[2,256,640]{2,1,0:T(8,128)(2,1)S(1)}, u32[]{:S(2)}, u32[]{:S(2)}) collective-permute-start(bf16[2,256,640]{2,1,0:T(8,128)(2,1)S(1)} %slice_bitcast_fusion.1), channel_id=1, source_target_pairs={{0,4},{4,8},{8,12},{12,16},{16,20},{20,24},{24,28},{28,0},{1,5},{5... | collective-permute-start | bytes 1966088 | tf_op jit(solution)/shard_map/ppermute | solution.py:35
  97.6 5.9 %cross.5 = (bf16[50,40,256]{2,1,0:T(8,128)(2,1)S(1)}, bf16[50,40,256]{2,1,0:T(8,128)(2,1)S(1)}) custom-call(s32[10]{0:T(128)S(1)} %concatenate.3.scal, bf16[2,256,640]{2,1,0:T(8,128)(2,1)S(1)} %collective-permute-done.22.refs_0_, bf16[2,256,640]{2,1,0:T(8,128)(2,1)S(1)} %collective-permute-done.14.refs_1_, ...), custom_call_target="tpu_custom_call" | custom-call | flops 10000000000 | bytes 10000000 | tf_op jit(solution)/shard_map/cross/pallas_call | solution.py:187
  103.5 3.1 %collective-permute-start.23 = (bf16[50,40,256]{2,1,0:T(8,128)(2,1)S(1)}, bf16[50,40,256]{2,1,0:T(8,128)(2,1)S(1)}, u32[]{:S(2)}, u32[]{:S(2)}) collective-permute-start(bf16[50,40,256]{2,1,0:T(8,128)(2,1)S(1)} %get-tuple-element.79), channel_id=1, source_target_pairs={{0,1},{1,0},{2,3},{3,2},{4,5},{5,4},{6,7},{7,6},{8,9},{9,8},{10,11... | collective-permute-start | bytes 3072008 | tf_op jit(solution)/shard_map/ppermute | solution.py:35
  106.5 3.5 %lags.3.rest_0_ = bf16[6400,512]{1,0:T(8,128)(2,1)} custom-call(s32[10]{0:T(128)S(1)} %concatenate.3.scal, bf16[3600,256]{1,0:T(8,128)(2,1)S(1)} %bitcast.24, bf16[3600,256]{1,0:T(8,128)(2,1)S(1)} %bitcast.25, bf16[2,256,512]{2,1,0:T(8,128)(2,1)S(1)} %copy-done), custom_call_target="tpu_custom_call" | custom-call | flops 2000000000 | bytes 3000000 | tf_op jit(solution)/shard_map/lags/pallas_call | solution.py:224
  110.0 4.8 %cross.4 = (bf16[20,40,256]{2,1,0:T(8,128)(2,1)S(1)}, bf16[20,40,256]{2,1,0:T(8,128)(2,1)S(1)}) custom-call(s32[10]{0:T(128)S(1)} %concatenate.3.scal, bf16[2,256,640]{2,1,0:T(8,128)(2,1)S(1)} %collective-permute-done.11.refs_0_, bf16[2,256,640]{2,1,0:T(8,128)(2,1)S(1)} %collective-permute-done.19.refs_1_, ...), custom_call_target="tpu_custom_call" | custom-call | flops 10000000000 | bytes 10000000 | tf_op jit(solution)/shard_map/cross/pallas_call | solution.py:187
  114.8 4.5 %collective-permute-start.21 = (bf16[20,40,256]{2,1,0:T(8,128)(2,1)S(1)}, bf16[20,40,256]{2,1,0:T(8,128)(2,1)S(1)}, u32[]{:S(2)}, u32[]{:S(2)}) collective-permute-start(bf16[20,40,256]{2,1,0:T(8,128)(2,1)S(1)} %get-tuple-element.71), channel_id=1, source_target_pairs={{0,1},{1,0},{2,3},{3,2},{4,5},{5,4},{6,7},{7,6},{8,9},{9,8},{10,11... | collective-permute-start | bytes 1228808 | tf_op jit(solution)/shard_map/ppermute | solution.py:35
  119.4 2.6 %lags.4.rest_0_ = bf16[6400,512]{1,0:T(8,128)(2,1)} custom-call(s32[10]{0:T(128)S(1)} %concatenate.3.scal, bf16[2000,256]{1,0:T(8,128)(2,1)S(1)} %bitcast.26, bf16[2000,256]{1,0:T(8,128)(2,1)S(1)} %bitcast.27, bf16[2,256,512]{2,1,0:T(8,128)(2,1)S(1)} %copy-done, bf16[6400,512]{1,0:T(8,128)(2,1)} %lags.3.rest_0_), custom_call_target="tpu_custom_call", output_to_operand_aliasing={{}: (4, {})} | custom-call | flops 2000000000 | bytes 3000000 | tf_op jit(solution)/shard_map/lags/pallas_call | solution.py:224
  122.0 1.9 %lags.5 = bf16[6400,512]{1,0:T(8,128)(2,1)} custom-call(s32[10]{0:T(128)S(1)} %concatenate.3.scal, bf16[800,256]{1,0:T(8,128)(2,1)S(1)} %bitcast.31, bf16[800,256]{1,0:T(8,128)(2,1)S(1)} %bitcast.32, bf16[2,256,512]{2,1,0:T(8,128)(2,1)S(1)} %copy-done, bf16[6400,512]{1,0:T(8,128)(2,1)} %lags.4.rest_0_), custom_call_target="tpu_custom_call", output_to_operand_aliasing={{}: (4, {})} | custom-call | flops 2000000000 | bytes 3000000 | tf_op jit(solution)/shard_map/lags/pallas_call | solution.py:224
  (38 shorter events, 4.5 us)
Async XLA Ops:
  0.7 1.3 %copy-start.1 = (f32[5,64,2,512]{3,2,1,0:T(2,128)S(1)}, f32[5,64,2,512]{3,2,1,0:T(2,128)}, u32[]{:S(2)}) copy-start(f32[5,64,2,512]{3,2,1,0:T(2,128)} %param.4) | copy-start | bytes 3932164
  2.1 0.7 copy-start.2
  6.2 5.0 %collective-permute-start = (bf16[2,256,640]{2,1,0:T(8,128)(2,1)S(1)}, bf16[2,256,640]{2,1,0:T(8,128)(2,1)S(1)}, u32[]{:S(2)}, u32[]{:S(2)}) collective-permute-start(bf16[2,256,640]{2,1,0:T(8,128)(2,1)S(1)} %get-tuple-element.44), channel_id=1, source_target_pairs={{0,1},{1,0},{2,3},{3,2},{4,5},{5,4},{6,7},{7,6},{8,9},{9,8},{10,11... | collective-permute-start | bytes 1966088 | tf_op jit(solution)/shard_map/ppermute | solution.py:35
  11.4 17.7 %collective-permute-start.5 = (bf16[2,256,640]{2,1,0:T(8,128)(2,1)S(1)}, bf16[2,256,640]{2,1,0:T(8,128)(2,1)S(1)}, u32[]{:S(2)}, u32[]{:S(2)}) collective-permute-start(bf16[2,256,640]{2,1,0:T(8,128)(2,1)S(1)} %pad_maximum_fusion.2.refs_0_), channel_id=1, source_target_pairs={{0,28},{4,0},{8,4},{12,8},{16,12},{20,16},{24,20},{28,24},{1,29},{... | collective-permute-start | bytes 1966088 | tf_op jit(solution)/shard_map/ppermute | solution.py:35
  15.3 16.8 %collective-permute-start.1 = (bf16[2,256,640]{2,1,0:T(8,128)(2,1)S(1)}, bf16[2,256,640]{2,1,0:T(8,128)(2,1)S(1)}, u32[]{:S(2)}, u32[]{:S(2)}) collective-permute-start(bf16[2,256,640]{2,1,0:T(8,128)(2,1)S(1)} %pad_maximum_fusion.2.refs_0_), channel_id=1, source_target_pairs={{0,4},{4,8},{8,12},{12,16},{16,20},{20,24},{24,28},{28,0},{1,5},{5... | collective-permute-start | bytes 1966088 | tf_op jit(solution)/shard_map/ppermute | solution.py:35
  15.4 16.9 %collective-permute-start.7 = (bf16[2,256,640]{2,1,0:T(8,128)(2,1)S(1)}, bf16[2,256,640]{2,1,0:T(8,128)(2,1)S(1)}, u32[]{:S(2)}, u32[]{:S(2)}) collective-permute-start(bf16[2,256,640]{2,1,0:T(8,128)(2,1)S(1)} %pad_maximum_fusion.3.refs_9_), channel_id=1, source_target_pairs={{0,64},{64,128},{128,192},{192,0},{1,65},{65,129},{129,193},{193,1... | collective-permute-start | bytes 1966088 | tf_op jit(solution)/shard_map/ppermute | solution.py:35
  16.7 15.6 %collective-permute-start.6 = (bf16[2,256,640]{2,1,0:T(8,128)(2,1)S(1)}, bf16[2,256,640]{2,1,0:T(8,128)(2,1)S(1)}, u32[]{:S(2)}, u32[]{:S(2)}) collective-permute-start(bf16[2,256,640]{2,1,0:T(8,128)(2,1)S(1)} %pad_maximum_fusion.3.refs_9_), channel_id=1, source_target_pairs={{0,32},{32,0},{1,33},{33,1},{2,34},{34,2},{3,35},{35,3},{4,36},{36... | collective-permute-start | bytes 1966088 | tf_op jit(solution)/shard_map/ppermute | solution.py:35
  18.0 19.6 %collective-permute-start.3 = (bf16[2,256,640]{2,1,0:T(8,128)(2,1)S(1)}, bf16[2,256,640]{2,1,0:T(8,128)(2,1)S(1)}, u32[]{:S(2)}, u32[]{:S(2)}) collective-permute-start(bf16[2,256,640]{2,1,0:T(8,128)(2,1)S(1)} %pad_maximum_fusion.3.refs_9_), channel_id=1, source_target_pairs={{0,192},{64,0},{128,64},{192,128},{1,193},{65,1},{129,65},{193,129... | collective-permute-start | bytes 1966088 | tf_op jit(solution)/shard_map/ppermute | solution.py:35
  32.3 30.3 %collective-permute-start.8 = (bf16[2,2,256,640]{3,2,1,0:T(8,128)(2,1)S(1)}, bf16[2,2,256,640]{3,2,1,0:T(8,128)(2,1)S(1)}, u32[]{:S(2)}, u32[]{:S(2)}) collective-permute-start(bf16[2,2,256,640]{3,2,1,0:T(8,128)(2,1)S(1)} %pad_maximum_fusion), channel_id=1, source_target_pairs={{0,2},{2,0},{1,3},{3,1},{4,6},{6,4},{5,7},{7,5},{8,10},{10,8},{9,1... | collective-permute-start | bytes 3932168 | tf_op jit(solution)/shard_map/ppermute | solution.py:35
  35.3 14.4 %collective-permute-start.12 = (bf16[2,256,640]{2,1,0:T(8,128)(2,1)S(1)}, bf16[2,256,640]{2,1,0:T(8,128)(2,1)S(1)}, u32[]{:S(2)}, u32[]{:S(2)}) collective-permute-start(bf16[2,256,640]{2,1,0:T(8,128)(2,1)S(1)} %collective-permute-done.5.refs_2_), channel_id=1, source_target_pairs={{0,28},{4,0},{8,4},{12,8},{16,12},{20,16},{24,20},{28,24},{1,29},{... | collective-permute-start | bytes 1966088 | tf_op jit(solution)/shard_map/ppermute | solution.py:35
  37.6 15.0 %collective-permute-start.2 = (bf16[2,256,640]{2,1,0:T(8,128)(2,1)S(1)}, bf16[2,256,640]{2,1,0:T(8,128)(2,1)S(1)}, u32[]{:S(2)}, u32[]{:S(2)}) collective-permute-start(bf16[2,256,640]{2,1,0:T(8,128)(2,1)S(1)} %collective-permute-done.1.refs_1_), channel_id=1, source_target_pairs={{0,4},{4,8},{8,12},{12,16},{16,20},{20,24},{24,28},{28,0},{1,5},{5... | collective-permute-start | bytes 1966088 | tf_op jit(solution)/shard_map/ppermute | solution.py:35
  37.6 16.5 %collective-permute-start.9 = (bf16[2,256,640]{2,1,0:T(8,128)(2,1)S(1)}, bf16[2,256,640]{2,1,0:T(8,128)(2,1)S(1)}, u32[]{:S(2)}, u32[]{:S(2)}) collective-permute-start(bf16[2,256,640]{2,1,0:T(8,128)(2,1)S(1)} %collective-permute-done.6.refs_10_), channel_id=1, source_target_pairs={{0,192},{64,0},{128,64},{192,128},{1,193},{65,1},{129,65},{193,129... | collective-permute-start | bytes 1966088 | tf_op jit(solution)/shard_map/ppermute | solution.py:35
  39.3 14.8 %collective-permute-start.15 = (bf16[2,256,640]{2,1,0:T(8,128)(2,1)S(1)}, bf16[2,256,640]{2,1,0:T(8,128)(2,1)S(1)}, u32[]{:S(2)}, u32[]{:S(2)}) collective-permute-start(bf16[2,256,640]{2,1,0:T(8,128)(2,1)S(1)} %collective-permute-done.6.refs_10_), channel_id=1, source_target_pairs={{0,64},{64,128},{128,192},{192,0},{1,65},{65,129},{129,193},{193,1... | collective-permute-start | bytes 1966088 | tf_op jit(solution)/shard_map/ppermute | solution.py:35
  52.6 12.9 %collective-permute-start.13 = (bf16[2,256,640]{2,1,0:T(8,128)(2,1)S(1)}, bf16[2,256,640]{2,1,0:T(8,128)(2,1)S(1)}, u32[]{:S(2)}, u32[]{:S(2)}) collective-permute-start(bf16[2,256,640]{2,1,0:T(8,128)(2,1)S(1)} %collective-permute-done.12.refs_4_), channel_id=1, source_target_pairs={{0,28},{4,0},{8,4},{12,8},{16,12},{20,16},{24,20},{28,24},{1,29},{... | collective-permute-start | bytes 1966088 | tf_op jit(solution)/shard_map/ppermute | solution.py:35
  52.9 14.1 %collective-permute-start.4 = (bf16[2,256,640]{2,1,0:T(8,128)(2,1)S(1)}, bf16[2,256,640]{2,1,0:T(8,128)(2,1)S(1)}, u32[]{:S(2)}, u32[]{:S(2)}) collective-permute-start(bf16[2,256,640]{2,1,0:T(8,128)(2,1)S(1)} %collective-permute-done.2.refs_3_), channel_id=1, source_target_pairs={{0,4},{4,8},{8,12},{12,16},{16,20},{20,24},{24,28},{28,0},{1,5},{5... | collective-permute-start | bytes 1966088 | tf_op jit(solution)/shard_map/ppermute | solution.py:35
  54.1 14.7 %collective-permute-start.17 = (bf16[2,256,640]{2,1,0:T(8,128)(2,1)S(1)}, bf16[2,256,640]{2,1,0:T(8,128)(2,1)S(1)}, u32[]{:S(2)}, u32[]{:S(2)}) collective-permute-start(bf16[2,256,640]{2,1,0:T(8,128)(2,1)S(1)} %collective-permute-done.9.refs_14_), channel_id=1, source_target_pairs={{0,192},{64,0},{128,64},{192,128},{1,193},{65,1},{129,65},{193,129... | collective-permute-start | bytes 1966088 | tf_op jit(solution)/shard_map/ppermute | solution.py:35
  55.2 13.6 %collective-permute-start.16 = (bf16[2,256,640]{2,1,0:T(8,128)(2,1)S(1)}, bf16[2,256,640]{2,1,0:T(8,128)(2,1)S(1)}, u32[]{:S(2)}, u32[]{:S(2)}) collective-permute-start(bf16[2,256,640]{2,1,0:T(8,128)(2,1)S(1)} %collective-permute-done.7.refs_11_), channel_id=1, source_target_pairs={{0,64},{64,128},{128,192},{192,0},{1,65},{65,129},{129,193},{193,1... | collective-permute-start | bytes 1966088 | tf_op jit(solution)/shard_map/ppermute | solution.py:35
  67.0 12.0 %collective-permute-start.14 = (bf16[2,256,640]{2,1,0:T(8,128)(2,1)S(1)}, bf16[2,256,640]{2,1,0:T(8,128)(2,1)S(1)}, u32[]{:S(2)}, u32[]{:S(2)}) collective-permute-start(bf16[2,256,640]{2,1,0:T(8,128)(2,1)S(1)} %get-tuple-element.51), channel_id=1, source_target_pairs={{0,28},{4,0},{8,4},{12,8},{16,12},{20,16},{24,20},{28,24},{1,29},{... | collective-permute-start | bytes 1966088 | tf_op jit(solution)/shard_map/ppermute | solution.py:35
  67.3 28.6 %collective-permute-start.22 = (bf16[2,256,640]{2,1,0:T(8,128)(2,1)S(1)}, bf16[2,256,640]{2,1,0:T(8,128)(2,1)S(1)}, u32[]{:S(2)}, u32[]{:S(2)}) collective-permute-start(bf16[2,256,640]{2,1,0:T(8,128)(2,1)S(1)} %pad_maximum_fusion.2.refs_0_), channel_id=1, source_target_pairs={{0,2},{2,0},{1,3},{3,1},{4,6},{6,4},{5,7},{7,5},{8,10},{10,8},{9,1... | collective-permute-start | bytes 1966088 | tf_op jit(solution)/shard_map/ppermute | solution.py:35
  67.9 28.1 %collective-permute-start.10 = (bf16[2,2,256,640]{3,2,1,0:T(8,128)(2,1)S(1)}, bf16[2,2,256,640]{3,2,1,0:T(8,128)(2,1)S(1)}, u32[]{:S(2)}, u32[]{:S(2)}) collective-permute-start(bf16[2,2,256,640]{3,2,1,0:T(8,128)(2,1)S(1)} %pad_maximum_fusion.1), channel_id=1, source_target_pairs={{0,4},{4,8},{8,12},{12,16},{16,20},{20,24},{24,28},{28,0},{1,5},{5... | collective-permute-start | bytes 3932168 | tf_op jit(solution)/shard_map/ppermute | solution.py:35
  79.0 16.9 %collective-permute-start.18 = (bf16[2,256,640]{2,1,0:T(8,128)(2,1)S(1)}, bf16[2,256,640]{2,1,0:T(8,128)(2,1)S(1)}, u32[]{:S(2)}, u32[]{:S(2)}) collective-permute-start(bf16[2,256,640]{2,1,0:T(8,128)(2,1)S(1)} %collective-permute-done.14.refs_1_), channel_id=1, source_target_pairs={{0,28},{4,0},{8,4},{12,8},{16,12},{20,16},{24,20},{28,24},{1,29},{... | collective-permute-start | bytes 1966088 | tf_op jit(solution)/shard_map/ppermute | solution.py:35
  90.2 16.4 %collective-permute-start.20 = (bf16[90,40,256]{2,1,0:T(8,128)(2,1)S(1)}, bf16[90,40,256]{2,1,0:T(8,128)(2,1)S(1)}, u32[]{:S(2)}, u32[]{:S(2)}) collective-permute-start(bf16[90,40,256]{2,1,0:T(8,128)(2,1)S(1)} %get-tuple-element.66), channel_id=1, source_target_pairs={{0,1},{1,0},{2,3},{3,2},{4,5},{5,4},{6,7},{7,6},{8,9},{9,8},{10,11... | collective-permute-start | bytes 5529608 | tf_op jit(solution)/shard_map/ppermute | solution.py:35
  95.9 14.1 %collective-permute-start.19 = (bf16[2,256,640]{2,1,0:T(8,128)(2,1)S(1)}, bf16[2,256,640]{2,1,0:T(8,128)(2,1)S(1)}, u32[]{:S(2)}, u32[]{:S(2)}) collective-permute-start(bf16[2,256,640]{2,1,0:T(8,128)(2,1)S(1)} %collective-permute-done.18.refs_4_), channel_id=1, source_target_pairs={{0,28},{4,0},{8,4},{12,8},{16,12},{20,16},{24,20},{28,24},{1,29},{... | collective-permute-start | bytes 1966088 | tf_op jit(solution)/shard_map/ppermute | solution.py:35
  96.0 14.0 %collective-permute-start.11 = (bf16[2,256,640]{2,1,0:T(8,128)(2,1)S(1)}, bf16[2,256,640]{2,1,0:T(8,128)(2,1)S(1)}, u32[]{:S(2)}, u32[]{:S(2)}) collective-permute-start(bf16[2,256,640]{2,1,0:T(8,128)(2,1)S(1)} %slice_bitcast_fusion.1), channel_id=1, source_target_pairs={{0,4},{4,8},{8,12},{12,16},{16,20},{20,24},{24,28},{28,0},{1,5},{5... | collective-permute-start | bytes 1966088 | tf_op jit(solution)/shard_map/ppermute | solution.py:35
  97.6 9.0 %copy-start = (bf16[2,256,512]{2,1,0:T(8,128)(2,1)S(1)}, bf16[2,256,512]{2,1,0:T(8,128)(2,1)}, u32[]{:S(2)}) copy-start(bf16[2,256,512]{2,1,0:T(8,128)(2,1)} %constant.28.table) | copy-start | bytes 1572868
  103.5 15.9 %collective-permute-start.23 = (bf16[50,40,256]{2,1,0:T(8,128)(2,1)S(1)}, bf16[50,40,256]{2,1,0:T(8,128)(2,1)S(1)}, u32[]{:S(2)}, u32[]{:S(2)}) collective-permute-start(bf16[50,40,256]{2,1,0:T(8,128)(2,1)S(1)} %get-tuple-element.79), channel_id=1, source_target_pairs={{0,1},{1,0},{2,3},{3,2},{4,5},{5,4},{6,7},{7,6},{8,9},{9,8},{10,11... | collective-permute-start | bytes 3072008 | tf_op jit(solution)/shard_map/ppermute | solution.py:35
  114.8 7.1 %collective-permute-start.21 = (bf16[20,40,256]{2,1,0:T(8,128)(2,1)S(1)}, bf16[20,40,256]{2,1,0:T(8,128)(2,1)S(1)}, u32[]{:S(2)}, u32[]{:S(2)}) collective-permute-start(bf16[20,40,256]{2,1,0:T(8,128)(2,1)S(1)} %get-tuple-element.71), channel_id=1, source_target_pairs={{0,1},{1,0},{2,3},{3,2},{4,5},{5,4},{6,7},{7,6},{8,9},{9,8},{10,11... | collective-permute-start | bytes 1228808 | tf_op jit(solution)/shard_map/ppermute | solution.py:35

commit v6 on v5

--- a/solution.py
+++ b/solution.py
@@ -239,8 +239,8 @@
 OWN = tuple((d, 0) for d in (0, 1, -1, 2, -2, 3, -3))
 GROUPS = (
     OWN + ((1, 1), (-1, 1)),
-    ((0, 1), (-2, 1), (4, 0), (2, 1), (-3, 1)),
-    ((3, 1), (4, 1)),
+    ((-2, 1), (4, 0), (2, 1), (-3, 1)),
+    ((0, 1), (3, 1), (4, 1)),
 )
 
 
@@ -271,8 +271,8 @@
 
     R[2, 0] = shift(R[1, 0], "z", 1)
     R[-2, 0] = shift(after(R[-1, 0], R[1, 0]), "z", -1)
-    near = shift(after(jnp.stack([R[1, 0], R[-1, 0]]), C[0, 1], C[1, 0]), "yh", 1)
-    R[1, 1], R[-1, 1] = (near, 0), (near, 1)
+    R[-1, 1] = shift(after(R[-1, 0], C[0, 1], C[1, 0]), "yh", 1)
+    R[1, 1] = shift(after(R[1, 0], R[-1, 1]), "yh", 1)
     C[1, 1] = shift(after(C[0, 1], R[-1, 0], C[1, 0]), "x", 1)
     C[-1, 1] = shift(after(C[0, 1], C[1, 0], C[-1, 0]), "x", -1)
 
@@ -280,11 +280,10 @@
     R[-3, 0] = shift(after(R[-2, 0], R[2, 0]), "z", -1)
     C[2, 0] = shift(after(C[1, 0], C[1, 1], R[-2, 0]), "x", 1)
     C[2, 1] = shift(after(C[-1, 1], C[1, 1]), "x", -1)
-    R[0, 1] = shift(after(row, near, C[-1, 1]), "yh", 1)
-
-    far = shift(after(jnp.stack([R[3, 0], near[0]]), C[-1, 1]), "z", 1)
+
+    far = shift(after(jnp.stack([R[3, 0], R[1, 1]]), C[-1, 1]), "z", 1)
     R[4, 0], R[2, 1] = (far, 0), (far, 1)
-    R[-2, 1] = shift(after(near[1], R[-3, 0], R[3, 0]), "z", -1)
+    R[-2, 1] = shift(after(R[-1, 1], R[-3, 0], R[3, 0]), "z", -1)
     R[-3, 1] = shift(after(R[-2, 1], C[2, 0], C[2, 1]), "z", -1)
     R[3, 1] = shift(far[1], "z", 1)
     R[4, 1] = shift(R[-3, 1], "z", -1)
@@ -292,6 +291,7 @@
     cols = [C[dx, dy] for dx in STEPS for dy in (0, 1)]
     own = [R[p] for p in GROUPS[0]]
     keep, send, cols = cross(scal, gate(own, R[3, 0], R[-3, 0])[0], cols, True)
+    R[0, 1] = shift(after(row, keep), "yh", 1)
     recv = shift(send, "c", 1)
     own, _ = gate([R[p] for p in GROUPS[1]], far, R[-3, 1])
     keep1, send1 = cross(scal, own, cols, False)

time: 124 us -> 124 us (level)
  starting transfers between devices: 39.4 us -> 45.8 us
  waiting for transfers between devices: 49.3 us -> 43.5 us
    ppermute x24 -> x25, starting transfers between devices: 39.4 us -> 45.8 us  [shift(): return lax.ppermute(x, axis, [(i, (i + step) % n) for i in range(n)])]
    ppermute x24 -> x25, waiting for transfers between devices: 49.3 us -> 43.5 us  [shift(): return lax.ppermute(x, axis, [(i, (i + step) % n) for i in range(n)])]
  transfers between devices with their start and end apart: 24 -> 25, of which waited for: 9 -> 9; matrix products, arithmetic and copies ran while one was open for 0% -> 0% of each run, Pallas kernels for 21% -> 21%
where the time goes in v6:
time: 124 us
  starting transfers between devices  45.8 us (37%)
  waiting for transfers between devices  43.5 us (35%)
  Pallas kernels  31.4 us (25%)
  local copies, waits for them, and re-layouts  2.91 us (2%)
    ppermute x25, starting transfers between devices, shift(): return lax.ppermute(x, axis, [(i, (i + step) % n) for i in range(n)])  45.8 us
    ppermute x25, waiting for transfers between devices, shift(): return lax.ppermute(x, axis, [(i, (i + step) % n) for i in range(n)])  43.5 us
    pallas_call x3, Pallas kernels, cross(): pl.pallas_call(functools.partial(cross_kernel, n, lead, indices), out_sha...  20 us
    pallas_call x3, Pallas kernels, lags(): pl.pallas_call(functools.partial(lags_kernel, group), out_shape=jax.Shape...  7.92 us
    pallas_call x1, Pallas kernels, whiten(): pl.pallas_call(whiten_kernel, out_shape=(msg, msg), in_specs=[pl.BlockSpe...  3.5 us
  transfers between devices with their start and end apart: 25, of which 9 were waited for; matrix products, arithmetic and copies ran while one was open for 0% of the time, Pallas kernels for 21%

profile of v6, /device:TPU:1, one launch (start us, length us, event | category | flops | bytes accessed | tf_op | source)
XLA Modules:
  0.0 124.2 jit_solution(4870289155718817590)
XLA Ops:
  0.7 1.3 %copy-done.1 = f32[5,64,2,512]{3,2,1,0:T(2,128)S(1)} copy-done((f32[5,64,2,512]{3,2,1,0:T(2,128)S(1)}, f32[5,64,2,512]{3,2,1,0:T(2,128)}, u32[]{:S(2)}) %copy-start.1) | copy-done | bytes 1310744
  2.7 3.5 %whiten.1 = (bf16[2,256,640]{2,1,0:T(8,128)(2,1)S(1)}, bf16[2,256,640]{2,1,0:T(8,128)(2,1)S(1)}) custom-call(s32[10]{0:T(128)S(1)} %concatenate.3.scal, f32[2560,128]{1,0:T(8,128)S(1)} %bitcast.29, s32[5,64]{1,0:T(8,128)S(1)} %copy-done.2), custom_call_target="tpu_custom_call" | custom-call | flops 1000000000 | bytes 3000000 | tf_op jit(solution)/shard_map/whiten/pallas_call | solution.py:93
  6.2 3.3 %collective-permute-start = (bf16[2,256,640]{2,1,0:T(8,128)(2,1)S(1)}, bf16[2,256,640]{2,1,0:T(8,128)(2,1)S(1)}, u32[]{:S(2)}, u32[]{:S(2)}) collective-permute-start(bf16[2,256,640]{2,1,0:T(8,128)(2,1)S(1)} %get-tuple-element.45), channel_id=1, source_target_pairs={{0,1},{1,0},{2,3},{3,2},{4,5},{5,4},{6,7},{7,6},{8,9},{9,8},{10,11... | collective-permute-start | bytes 1966088 | tf_op jit(solution)/shard_map/ppermute | solution.py:35
  9.6 1.7 %collective-permute-done = bf16[2,256,640]{2,1,0:T(8,128)(2,1)S(1)} collective-permute-done((bf16[2,256,640]{2,1,0:T(8,128)(2,1)S(1)}, bf16[2,256,640]{2,1,0:T(8,128)(2,1)S(1)}, u32[]{:S(2)}, u32[]{:S(2)}) %collective-permute-start) | collective-permute-done | bytes 655392 | tf_op jit(solution)/shard_map/ppermute | solution.py:35
  11.5 3.9 %collective-permute-start.2 = (bf16[2,256,640]{2,1,0:T(8,128)(2,1)S(1)}, bf16[2,256,640]{2,1,0:T(8,128)(2,1)S(1)}, u32[]{:S(2)}, u32[]{:S(2)}) collective-permute-start(bf16[2,256,640]{2,1,0:T(8,128)(2,1)S(1)} %pad_maximum_fusion.1.refs_0_), channel_id=1, source_target_pairs={{0,28},{4,0},{8,4},{12,8},{16,12},{20,16},{24,20},{28,24},{1,29},{... | collective-permute-start | bytes 1966088 | tf_op jit(solution)/shard_map/ppermute | solution.py:35
  15.5 1.4 %collective-permute-start.8 = (bf16[2,256,640]{2,1,0:T(8,128)(2,1)S(1)}, bf16[2,256,640]{2,1,0:T(8,128)(2,1)S(1)}, u32[]{:S(2)}, u32[]{:S(2)}) collective-permute-start(bf16[2,256,640]{2,1,0:T(8,128)(2,1)S(1)} %pad_maximum_fusion.2.refs_9_), channel_id=1, source_target_pairs={{0,32},{32,0},{1,33},{33,1},{2,34},{34,2},{3,35},{35,3},{4,36},{36... | collective-permute-start | bytes 1966088 | tf_op jit(solution)/shard_map/ppermute | solution.py:35
  18.1 1.5 %collective-permute-start.5 = (bf16[2,256,640]{2,1,0:T(8,128)(2,1)S(1)}, bf16[2,256,640]{2,1,0:T(8,128)(2,1)S(1)}, u32[]{:S(2)}, u32[]{:S(2)}) collective-permute-start(bf16[2,256,640]{2,1,0:T(8,128)(2,1)S(1)} %pad_maximum_fusion.2.refs_9_), channel_id=1, source_target_pairs={{0,192},{64,0},{128,64},{192,128},{1,193},{65,1},{129,65},{193,129... | collective-permute-start | bytes 1966088 | tf_op jit(solution)/shard_map/ppermute | solution.py:35
  19.6 10.6 %collective-permute-done.1.refs_1_ = bf16[2,256,640]{2,1,0:T(8,128)(2,1)S(1)} collective-permute-done((bf16[2,256,640]{2,1,0:T(8,128)(2,1)S(1)}, bf16[2,256,640]{2,1,0:T(8,128)(2,1)S(1)}, u32[]{:S(2)}, u32[]{:S(2)}) %collective-permute-start.1) | collective-permute-done | bytes 655392 | tf_op jit(solution)/shard_map/ppermute | solution.py:35
  30.2 2.7 %collective-permute-start.4 = (bf16[2,256,640]{2,1,0:T(8,128)(2,1)S(1)}, bf16[2,256,640]{2,1,0:T(8,128)(2,1)S(1)}, u32[]{:S(2)}, u32[]{:S(2)}) collective-permute-start(bf16[2,256,640]{2,1,0:T(8,128)(2,1)S(1)} %collective-permute-done.2.refs_2_), channel_id=1, source_target_pairs={{0,28},{4,0},{8,4},{12,8},{16,12},{20,16},{24,20},{28,24},{1,29},{... | collective-permute-start | bytes 1966088 | tf_op jit(solution)/shard_map/ppermute | solution.py:35
  33.4 2.6 %collective-permute-start.10 = (bf16[2,256,640]{2,1,0:T(8,128)(2,1)S(1)}, bf16[2,256,640]{2,1,0:T(8,128)(2,1)S(1)}, u32[]{:S(2)}, u32[]{:S(2)}) collective-permute-start(bf16[2,256,640]{2,1,0:T(8,128)(2,1)S(1)} %collective-permute-done.2.refs_2_), channel_id=1, source_target_pairs={{0,2},{2,0},{1,3},{3,1},{4,6},{6,4},{5,7},{7,5},{8,10},{10,8},{9,1... | collective-permute-start | bytes 1966088 | tf_op jit(solution)/shard_map/ppermute | solution.py:35
  37.0 1.7 %collective-permute-start.13 = (bf16[2,256,640]{2,1,0:T(8,128)(2,1)S(1)}, bf16[2,256,640]{2,1,0:T(8,128)(2,1)S(1)}, u32[]{:S(2)}, u32[]{:S(2)}) collective-permute-start(bf16[2,256,640]{2,1,0:T(8,128)(2,1)S(1)} %collective-permute-done.8.refs_10_), channel_id=1, source_target_pairs={{0,192},{64,0},{128,64},{192,128},{1,193},{65,1},{129,65},{193,129... | collective-permute-start | bytes 1966088 | tf_op jit(solution)/shard_map/ppermute | solution.py:35
  38.7 8.0 %collective-permute-done.3.refs_3_ = bf16[2,256,640]{2,1,0:T(8,128)(2,1)S(1)} collective-permute-done((bf16[2,256,640]{2,1,0:T(8,128)(2,1)S(1)}, bf16[2,256,640]{2,1,0:T(8,128)(2,1)S(1)}, u32[]{:S(2)}, u32[]{:S(2)}) %collective-permute-start.3) | collective-permute-done | bytes 655392 | tf_op jit(solution)/shard_map/ppermute | solution.py:35
  46.7 2.7 %collective-permute-start.7 = (bf16[2,256,640]{2,1,0:T(8,128)(2,1)S(1)}, bf16[2,256,640]{2,1,0:T(8,128)(2,1)S(1)}, u32[]{:S(2)}, u32[]{:S(2)}) collective-permute-start(bf16[2,256,640]{2,1,0:T(8,128)(2,1)S(1)} %collective-permute-done.4.refs_4_), channel_id=1, source_target_pairs={{0,28},{4,0},{8,4},{12,8},{16,12},{20,16},{24,20},{28,24},{1,29},{... | collective-permute-start | bytes 1966088 | tf_op jit(solution)/shard_map/ppermute | solution.py:35
  49.4 2.9 %collective-permute-start.11 = (bf16[2,256,640]{2,1,0:T(8,128)(2,1)S(1)}, bf16[2,256,640]{2,1,0:T(8,128)(2,1)S(1)}, u32[]{:S(2)}, u32[]{:S(2)}) collective-permute-start(bf16[2,256,640]{2,1,0:T(8,128)(2,1)S(1)} %collective-permute-done.1.refs_1_), channel_id=1, source_target_pairs={{0,2},{2,0},{1,3},{3,1},{4,6},{6,4},{5,7},{7,5},{8,10},{10,8},{9,1... | collective-permute-start | bytes 1966088 | tf_op jit(solution)/shard_map/ppermute | solution.py:35
  52.3 1.2 collective-permute-start.14
  53.5 1.5 %collective-permute-start.15 = (bf16[2,256,640]{2,1,0:T(8,128)(2,1)S(1)}, bf16[2,256,640]{2,1,0:T(8,128)(2,1)S(1)}, u32[]{:S(2)}, u32[]{:S(2)}) collective-permute-start(bf16[2,256,640]{2,1,0:T(8,128)(2,1)S(1)} %collective-permute-done.13.refs_14_), channel_id=1, source_target_pairs={{0,192},{64,0},{128,64},{192,128},{1,193},{65,1},{129,65},{193,129... | collective-permute-start | bytes 1966088 | tf_op jit(solution)/shard_map/ppermute | solution.py:35
  55.0 7.4 %collective-permute-done.6.refs_5_ = bf16[2,256,640]{2,1,0:T(8,128)(2,1)S(1)} collective-permute-done((bf16[2,256,640]{2,1,0:T(8,128)(2,1)S(1)}, bf16[2,256,640]{2,1,0:T(8,128)(2,1)S(1)}, u32[]{:S(2)}, u32[]{:S(2)}) %collective-permute-start.6) | collective-permute-done | bytes 655392 | tf_op jit(solution)/shard_map/ppermute | solution.py:35
  62.4 2.4 %collective-permute-start.19 = (bf16[2,256,640]{2,1,0:T(8,128)(2,1)S(1)}, bf16[2,256,640]{2,1,0:T(8,128)(2,1)S(1)}, u32[]{:S(2)}, u32[]{:S(2)}) collective-permute-start(bf16[2,256,640]{2,1,0:T(8,128)(2,1)S(1)} %collective-permute-done.10.refs_8_), channel_id=1, source_target_pairs={{0,28},{4,0},{8,4},{12,8},{16,12},{20,16},{24,20},{28,24},{1,29},{... | collective-permute-start | bytes 1966088 | tf_op jit(solution)/shard_map/ppermute | solution.py:35
  65.0 2.1 %collective-permute-done.14.refs_15_ = bf16[2,256,640]{2,1,0:T(8,128)(2,1)S(1)} collective-permute-done((bf16[2,256,640]{2,1,0:T(8,128)(2,1)S(1)}, bf16[2,256,640]{2,1,0:T(8,128)(2,1)S(1)}, u32[]{:S(2)}, u32[]{:S(2)}) %collective-permute-start.14) | collective-permute-done | bytes 655392 | tf_op jit(solution)/shard_map/ppermute | solution.py:35
  67.1 8.8 %collective-permute-done.19.refs_0_ = bf16[2,256,640]{2,1,0:T(8,128)(2,1)S(1)} collective-permute-done((bf16[2,256,640]{2,1,0:T(8,128)(2,1)S(1)}, bf16[2,256,640]{2,1,0:T(8,128)(2,1)S(1)}, u32[]{:S(2)}, u32[]{:S(2)}) %collective-permute-start.19) | collective-permute-done | bytes 655392 | tf_op jit(solution)/shard_map/ppermute | solution.py:35
  75.9 3.3 %collective-permute-start.20 = (bf16[2,256,640]{2,1,0:T(8,128)(2,1)S(1)}, bf16[2,256,640]{2,1,0:T(8,128)(2,1)S(1)}, u32[]{:S(2)}, u32[]{:S(2)}) collective-permute-start(bf16[2,256,640]{2,1,0:T(8,128)(2,1)S(1)} %collective-permute-done.19.refs_0_), channel_id=1, source_target_pairs={{0,28},{4,0},{8,4},{12,8},{16,12},{20,16},{24,20},{28,24},{1,29},{... | collective-permute-start | bytes 1966088 | tf_op jit(solution)/shard_map/ppermute | solution.py:35
  79.2 9.4 %cross.3 = (bf16[90,40,256]{2,1,0:T(8,128)(2,1)S(1)}, bf16[90,40,256]{2,1,0:T(8,128)(2,1)S(1)}, bf16[256,80,128]{2,1,0:T(8,128)(2,1)S(1)}) custom-call(s32[10]{0:T(128)S(1)} %concatenate.3.scal, bf16[2,256,640]{2,1,0:T(8,128)(2,1)S(1)} %pad_maximum_fusion.1.refs_0_, bf16[2,256,640]{2,1,0:T(8,128)(2,1)S(1)} %collective-permute-done.1.refs_1_, ...), custom_call_target="tpu_custom_call" | custom-call | flops 10000000000 | bytes 10000000 | tf_op jit(solution)/shard_map/cross/pallas_call | solution.py:187
  88.6 4.3 %collective-permute-start.22 = (bf16[90,40,256]{2,1,0:T(8,128)(2,1)S(1)}, bf16[90,40,256]{2,1,0:T(8,128)(2,1)S(1)}, u32[]{:S(2)}, u32[]{:S(2)}) collective-permute-start(bf16[90,40,256]{2,1,0:T(8,128)(2,1)S(1)} %get-tuple-element.69), channel_id=1, source_target_pairs={{0,1},{1,0},{2,3},{3,2},{4,5},{5,4},{6,7},{7,6},{8,9},{9,8},{10,11... | collective-permute-start | bytes 5529608 | tf_op jit(solution)/shard_map/ppermute | solution.py:35
  92.9 2.9 %collective-permute-start.16 = (bf16[2,256,640]{2,1,0:T(8,128)(2,1)S(1)}, bf16[2,256,640]{2,1,0:T(8,128)(2,1)S(1)}, u32[]{:S(2)}, u32[]{:S(2)}) collective-permute-start(bf16[2,256,640]{2,1,0:T(8,128)(2,1)S(1)} %pad_maximum_fusion.1.refs_0_), channel_id=1, source_target_pairs={{0,2},{2,0},{1,3},{3,1},{4,6},{6,4},{5,7},{7,5},{8,10},{10,8},{9,1... | collective-permute-start | bytes 1966088 | tf_op jit(solution)/shard_map/ppermute | solution.py:35
  95.9 1.5 %collective-permute-start.18 = (bf16[2,256,640]{2,1,0:T(8,128)(2,1)S(1)}, bf16[2,256,640]{2,1,0:T(8,128)(2,1)S(1)}, u32[]{:S(2)}, u32[]{:S(2)}) collective-permute-start(bf16[2,256,640]{2,1,0:T(8,128)(2,1)S(1)} %slice_bitcast_fusion), channel_id=1, source_target_pairs={{0,4},{4,8},{8,12},{12,16},{16,20},{20,24},{24,28},{28,0},{1,5},{5... | collective-permute-start | bytes 1966088 | tf_op jit(solution)/shard_map/ppermute | solution.py:35
  97.5 5.5 %cross.5 = (bf16[40,40,256]{2,1,0:T(8,128)(2,1)S(1)}, bf16[40,40,256]{2,1,0:T(8,128)(2,1)S(1)}) custom-call(s32[10]{0:T(128)S(1)} %concatenate.3.scal, bf16[2,256,640]{2,1,0:T(8,128)(2,1)S(1)} %collective-permute-done.19.refs_0_, bf16[2,2,256,640]{3,2,1,0:T(8,128)(2,1)S(1)} %collective-permute-done.17.refs_1_.refs_2_, ...), custom_call_target="tpu_custom_call" | custom-call | flops 10000000000 | bytes 10000000 | tf_op jit(solution)/shard_map/cross/pallas_call | solution.py:187
  104.0 3.5 %lags.3.rest_0_ = bf16[6400,512]{1,0:T(8,128)(2,1)} custom-call(s32[10]{0:T(128)S(1)} %concatenate.3.scal, bf16[3600,256]{1,0:T(8,128)(2,1)S(1)} %bitcast.21, bf16[3600,256]{1,0:T(8,128)(2,1)S(1)} %bitcast.22, bf16[2,256,512]{2,1,0:T(8,128)(2,1)S(1)} %copy-done), custom_call_target="tpu_custom_call" | custom-call | flops 2000000000 | bytes 3000000 | tf_op jit(solution)/shard_map/lags/pallas_call | solution.py:224
  107.5 3.2 %collective-permute-done.16.refs_0_ = bf16[2,256,640]{2,1,0:T(8,128)(2,1)S(1)} collective-permute-done((bf16[2,256,640]{2,1,0:T(8,128)(2,1)S(1)}, bf16[2,256,640]{2,1,0:T(8,128)(2,1)S(1)}, u32[]{:S(2)}, u32[]{:S(2)}) %collective-permute-start.16) | collective-permute-done | bytes 655392 | tf_op jit(solution)/shard_map/ppermute | solution.py:35
  111.8 5.1 %cross.4 = (bf16[30,40,256]{2,1,0:T(8,128)(2,1)S(1)}, bf16[30,40,256]{2,1,0:T(8,128)(2,1)S(1)}) custom-call(s32[10]{0:T(128)S(1)} %concatenate.3.scal, bf16[2,256,640]{2,1,0:T(8,128)(2,1)S(1)} %collective-permute-done.16.refs_0_, bf16[2,256,640]{2,1,0:T(8,128)(2,1)S(1)} %collective-permute-done.18.refs_1_, ...), custom_call_target="tpu_custom_call" | custom-call | flops 10000000000 | bytes 10000000 | tf_op jit(solution)/shard_map/cross/pallas_call | solution.py:187
  116.9 2.6 %collective-permute-start.23 = (bf16[30,40,256]{2,1,0:T(8,128)(2,1)S(1)}, bf16[30,40,256]{2,1,0:T(8,128)(2,1)S(1)}, u32[]{:S(2)}, u32[]{:S(2)}) collective-permute-start(bf16[30,40,256]{2,1,0:T(8,128)(2,1)S(1)} %get-tuple-element.75), channel_id=1, source_target_pairs={{0,1},{1,0},{2,3},{3,2},{4,5},{5,4},{6,7},{7,6},{8,9},{9,8},{10,11... | collective-permute-start | bytes 1843208 | tf_op jit(solution)/shard_map/ppermute | solution.py:35
  119.6 2.3 %lags.4.rest_0_ = bf16[6400,512]{1,0:T(8,128)(2,1)} custom-call(s32[10]{0:T(128)S(1)} %concatenate.3.scal, bf16[1600,256]{1,0:T(8,128)(2,1)S(1)} %bitcast.23, bf16[1600,256]{1,0:T(8,128)(2,1)S(1)} %bitcast.24, bf16[2,256,512]{2,1,0:T(8,128)(2,1)S(1)} %copy-done, bf16[6400,512]{1,0:T(8,128)(2,1)} %lags.3.rest_0_), custom_call_target="tpu_custom_call", output_to_operand_aliasing={{}: (4, {})} | custom-call | flops 2000000000 | bytes 3000000 | tf_op jit(solution)/shard_map/lags/pallas_call | solution.py:224
  121.9 2.1 %lags.5 = bf16[6400,512]{1,0:T(8,128)(2,1)} custom-call(s32[10]{0:T(128)S(1)} %concatenate.3.scal, bf16[1200,256]{1,0:T(8,128)(2,1)S(1)} %bitcast.27, bf16[1200,256]{1,0:T(8,128)(2,1)S(1)} %bitcast.28, bf16[2,256,512]{2,1,0:T(8,128)(2,1)S(1)} %copy-done, bf16[6400,512]{1,0:T(8,128)(2,1)} %lags.4.rest_0_), custom_call_target="tpu_custom_call", output_to_operand_aliasing={{}: (4, {})} | custom-call | flops 2000000000 | bytes 3000000 | tf_op jit(solution)/shard_map/lags/pallas_call | solution.py:224
  (38 shorter events, 6.9 us)
Async XLA Ops:
  0.7 1.3 %copy-start.1 = (f32[5,64,2,512]{3,2,1,0:T(2,128)S(1)}, f32[5,64,2,512]{3,2,1,0:T(2,128)}, u32[]{:S(2)}) copy-start(f32[5,64,2,512]{3,2,1,0:T(2,128)} %param.4) | copy-start | bytes 3932164
  2.1 0.7 copy-start.2
  6.2 5.0 %collective-permute-start = (bf16[2,256,640]{2,1,0:T(8,128)(2,1)S(1)}, bf16[2,256,640]{2,1,0:T(8,128)(2,1)S(1)}, u32[]{:S(2)}, u32[]{:S(2)}) collective-permute-start(bf16[2,256,640]{2,1,0:T(8,128)(2,1)S(1)} %get-tuple-element.45), channel_id=1, source_target_pairs={{0,1},{1,0},{2,3},{3,2},{4,5},{5,4},{6,7},{7,6},{8,9},{9,8},{10,11... | collective-permute-start | bytes 1966088 | tf_op jit(solution)/shard_map/ppermute | solution.py:35
  11.4 18.7 %collective-permute-start.1 = (bf16[2,256,640]{2,1,0:T(8,128)(2,1)S(1)}, bf16[2,256,640]{2,1,0:T(8,128)(2,1)S(1)}, u32[]{:S(2)}, u32[]{:S(2)}) collective-permute-start(bf16[2,256,640]{2,1,0:T(8,128)(2,1)S(1)} %pad_maximum_fusion.1.refs_0_), channel_id=1, source_target_pairs={{0,4},{4,8},{8,12},{12,16},{16,20},{20,24},{24,28},{28,0},{1,5},{5... | collective-permute-start | bytes 1966088 | tf_op jit(solution)/shard_map/ppermute | solution.py:35
  11.5 18.6 %collective-permute-start.2 = (bf16[2,256,640]{2,1,0:T(8,128)(2,1)S(1)}, bf16[2,256,640]{2,1,0:T(8,128)(2,1)S(1)}, u32[]{:S(2)}, u32[]{:S(2)}) collective-permute-start(bf16[2,256,640]{2,1,0:T(8,128)(2,1)S(1)} %pad_maximum_fusion.1.refs_0_), channel_id=1, source_target_pairs={{0,28},{4,0},{8,4},{12,8},{16,12},{20,16},{24,20},{28,24},{1,29},{... | collective-permute-start | bytes 1966088 | tf_op jit(solution)/shard_map/ppermute | solution.py:35
  15.5 17.3 %collective-permute-start.8 = (bf16[2,256,640]{2,1,0:T(8,128)(2,1)S(1)}, bf16[2,256,640]{2,1,0:T(8,128)(2,1)S(1)}, u32[]{:S(2)}, u32[]{:S(2)}) collective-permute-start(bf16[2,256,640]{2,1,0:T(8,128)(2,1)S(1)} %pad_maximum_fusion.2.refs_9_), channel_id=1, source_target_pairs={{0,32},{32,0},{1,33},{33,1},{2,34},{34,2},{3,35},{35,3},{4,36},{36... | collective-permute-start | bytes 1966088 | tf_op jit(solution)/shard_map/ppermute | solution.py:35
  16.9 16.5 %collective-permute-start.9 = (bf16[2,256,640]{2,1,0:T(8,128)(2,1)S(1)}, bf16[2,256,640]{2,1,0:T(8,128)(2,1)S(1)}, u32[]{:S(2)}, u32[]{:S(2)}) collective-permute-start(bf16[2,256,640]{2,1,0:T(8,128)(2,1)S(1)} %pad_maximum_fusion.2.refs_9_), channel_id=1, source_target_pairs={{0,64},{64,128},{128,192},{192,0},{1,65},{65,129},{129,193},{193,1... | collective-permute-start | bytes 1966088 | tf_op jit(solution)/shard_map/ppermute | solution.py:35
  18.1 18.9 %collective-permute-start.5 = (bf16[2,256,640]{2,1,0:T(8,128)(2,1)S(1)}, bf16[2,256,640]{2,1,0:T(8,128)(2,1)S(1)}, u32[]{:S(2)}, u32[]{:S(2)}) collective-permute-start(bf16[2,256,640]{2,1,0:T(8,128)(2,1)S(1)} %pad_maximum_fusion.2.refs_9_), channel_id=1, source_target_pairs={{0,192},{64,0},{128,64},{192,128},{1,193},{65,1},{129,65},{193,129... | collective-permute-start | bytes 1966088 | tf_op jit(solution)/shard_map/ppermute | solution.py:35
  30.2 16.6 %collective-permute-start.3 = (bf16[2,256,640]{2,1,0:T(8,128)(2,1)S(1)}, bf16[2,256,640]{2,1,0:T(8,128)(2,1)S(1)}, u32[]{:S(2)}, u32[]{:S(2)}) collective-permute-start(bf16[2,256,640]{2,1,0:T(8,128)(2,1)S(1)} %collective-permute-done.1.refs_1_), channel_id=1, source_target_pairs={{0,4},{4,8},{8,12},{12,16},{16,20},{20,24},{24,28},{28,0},{1,5},{5... | collective-permute-start | bytes 1966088 | tf_op jit(solution)/shard_map/ppermute | solution.py:35
  30.2 16.6 %collective-permute-start.4 = (bf16[2,256,640]{2,1,0:T(8,128)(2,1)S(1)}, bf16[2,256,640]{2,1,0:T(8,128)(2,1)S(1)}, u32[]{:S(2)}, u32[]{:S(2)}) collective-permute-start(bf16[2,256,640]{2,1,0:T(8,128)(2,1)S(1)} %collective-permute-done.2.refs_2_), channel_id=1, source_target_pairs={{0,28},{4,0},{8,4},{12,8},{16,12},{20,16},{24,20},{28,24},{1,29},{... | collective-permute-start | bytes 1966088 | tf_op jit(solution)/shard_map/ppermute | solution.py:35
  33.4 16.0 %collective-permute-start.10 = (bf16[2,256,640]{2,1,0:T(8,128)(2,1)S(1)}, bf16[2,256,640]{2,1,0:T(8,128)(2,1)S(1)}, u32[]{:S(2)}, u32[]{:S(2)}) collective-permute-start(bf16[2,256,640]{2,1,0:T(8,128)(2,1)S(1)} %collective-permute-done.2.refs_2_), channel_id=1, source_target_pairs={{0,2},{2,0},{1,3},{3,1},{4,6},{6,4},{5,7},{7,5},{8,10},{10,8},{9,1... | collective-permute-start | bytes 1966088 | tf_op jit(solution)/shard_map/ppermute | solution.py:35
  36.0 16.3 %collective-permute-start.12 = (bf16[2,256,640]{2,1,0:T(8,128)(2,1)S(1)}, bf16[2,256,640]{2,1,0:T(8,128)(2,1)S(1)}, u32[]{:S(2)}, u32[]{:S(2)}) collective-permute-start(bf16[2,256,640]{2,1,0:T(8,128)(2,1)S(1)} %collective-permute-done.8.refs_10_), channel_id=1, source_target_pairs={{0,64},{64,128},{128,192},{192,0},{1,65},{65,129},{129,193},{193,1... | collective-permute-start | bytes 1966088 | tf_op jit(solution)/shard_map/ppermute | solution.py:35
  37.0 16.6 %collective-permute-start.13 = (bf16[2,256,640]{2,1,0:T(8,128)(2,1)S(1)}, bf16[2,256,640]{2,1,0:T(8,128)(2,1)S(1)}, u32[]{:S(2)}, u32[]{:S(2)}) collective-permute-start(bf16[2,256,640]{2,1,0:T(8,128)(2,1)S(1)} %collective-permute-done.8.refs_10_), channel_id=1, source_target_pairs={{0,192},{64,0},{128,64},{192,128},{1,193},{65,1},{129,65},{193,129... | collective-permute-start | bytes 1966088 | tf_op jit(solution)/shard_map/ppermute | solution.py:35
  46.7 15.7 %collective-permute-start.6 = (bf16[2,256,640]{2,1,0:T(8,128)(2,1)S(1)}, bf16[2,256,640]{2,1,0:T(8,128)(2,1)S(1)}, u32[]{:S(2)}, u32[]{:S(2)}) collective-permute-start(bf16[2,256,640]{2,1,0:T(8,128)(2,1)S(1)} %collective-permute-done.3.refs_3_), channel_id=1, source_target_pairs={{0,4},{4,8},{8,12},{12,16},{16,20},{20,24},{24,28},{28,0},{1,5},{5... | collective-permute-start | bytes 1966088 | tf_op jit(solution)/shard_map/ppermute | solution.py:35
  46.7 15.7 %collective-permute-start.7 = (bf16[2,256,640]{2,1,0:T(8,128)(2,1)S(1)}, bf16[2,256,640]{2,1,0:T(8,128)(2,1)S(1)}, u32[]{:S(2)}, u32[]{:S(2)}) collective-permute-start(bf16[2,256,640]{2,1,0:T(8,128)(2,1)S(1)} %collective-permute-done.4.refs_4_), channel_id=1, source_target_pairs={{0,28},{4,0},{8,4},{12,8},{16,12},{20,16},{24,20},{28,24},{1,29},{... | collective-permute-start | bytes 1966088 | tf_op jit(solution)/shard_map/ppermute | solution.py:35
  49.4 15.4 %collective-permute-start.11 = (bf16[2,256,640]{2,1,0:T(8,128)(2,1)S(1)}, bf16[2,256,640]{2,1,0:T(8,128)(2,1)S(1)}, u32[]{:S(2)}, u32[]{:S(2)}) collective-permute-start(bf16[2,256,640]{2,1,0:T(8,128)(2,1)S(1)} %collective-permute-done.1.refs_1_), channel_id=1, source_target_pairs={{0,2},{2,0},{1,3},{3,1},{4,6},{6,4},{5,7},{7,5},{8,10},{10,8},{9,1... | collective-permute-start | bytes 1966088 | tf_op jit(solution)/shard_map/ppermute | solution.py:35
  52.3 14.8 %collective-permute-start.14 = (bf16[2,256,640]{2,1,0:T(8,128)(2,1)S(1)}, bf16[2,256,640]{2,1,0:T(8,128)(2,1)S(1)}, u32[]{:S(2)}, u32[]{:S(2)}) collective-permute-start(bf16[2,256,640]{2,1,0:T(8,128)(2,1)S(1)} %collective-permute-done.9.refs_11_), channel_id=1, source_target_pairs={{0,64},{64,128},{128,192},{192,0},{1,65},{65,129},{129,193},{193,1... | collective-permute-start | bytes 1966088 | tf_op jit(solution)/shard_map/ppermute | solution.py:35
  53.5 13.6 %collective-permute-start.15 = (bf16[2,256,640]{2,1,0:T(8,128)(2,1)S(1)}, bf16[2,256,640]{2,1,0:T(8,128)(2,1)S(1)}, u32[]{:S(2)}, u32[]{:S(2)}) collective-permute-start(bf16[2,256,640]{2,1,0:T(8,128)(2,1)S(1)} %collective-permute-done.13.refs_14_), channel_id=1, source_target_pairs={{0,192},{64,0},{128,64},{192,128},{1,193},{65,1},{129,65},{193,129... | collective-permute-start | bytes 1966088 | tf_op jit(solution)/shard_map/ppermute | solution.py:35
  62.4 13.5 %collective-permute-start.19 = (bf16[2,256,640]{2,1,0:T(8,128)(2,1)S(1)}, bf16[2,256,640]{2,1,0:T(8,128)(2,1)S(1)}, u32[]{:S(2)}, u32[]{:S(2)}) collective-permute-start(bf16[2,256,640]{2,1,0:T(8,128)(2,1)S(1)} %collective-permute-done.10.refs_8_), channel_id=1, source_target_pairs={{0,28},{4,0},{8,4},{12,8},{16,12},{20,16},{24,20},{28,24},{1,29},{... | collective-permute-start | bytes 1966088 | tf_op jit(solution)/shard_map/ppermute | solution.py:35
  64.9 30.9 %collective-permute-start.17 = (bf16[2,2,256,640]{3,2,1,0:T(8,128)(2,1)S(1)}, bf16[2,2,256,640]{3,2,1,0:T(8,128)(2,1)S(1)}, u32[]{:S(2)}, u32[]{:S(2)}) collective-permute-start(bf16[2,2,256,640]{3,2,1,0:T(8,128)(2,1)S(1)} %pad_maximum_fusion), channel_id=1, source_target_pairs={{0,4},{4,8},{8,12},{12,16},{16,20},{20,24},{24,28},{28,0},{1,5},{5... | collective-permute-start | bytes 3932168 | tf_op jit(solution)/shard_map/ppermute | solution.py:35
  75.9 19.9 %collective-permute-start.20 = (bf16[2,256,640]{2,1,0:T(8,128)(2,1)S(1)}, bf16[2,256,640]{2,1,0:T(8,128)(2,1)S(1)}, u32[]{:S(2)}, u32[]{:S(2)}) collective-permute-start(bf16[2,256,640]{2,1,0:T(8,128)(2,1)S(1)} %collective-permute-done.19.refs_0_), channel_id=1, source_target_pairs={{0,28},{4,0},{8,4},{12,8},{16,12},{20,16},{24,20},{28,24},{1,29},{... | collective-permute-start | bytes 1966088 | tf_op jit(solution)/shard_map/ppermute | solution.py:35
  88.6 15.4 %collective-permute-start.22 = (bf16[90,40,256]{2,1,0:T(8,128)(2,1)S(1)}, bf16[90,40,256]{2,1,0:T(8,128)(2,1)S(1)}, u32[]{:S(2)}, u32[]{:S(2)}) collective-permute-start(bf16[90,40,256]{2,1,0:T(8,128)(2,1)S(1)} %get-tuple-element.69), channel_id=1, source_target_pairs={{0,1},{1,0},{2,3},{3,2},{4,5},{5,4},{6,7},{7,6},{8,9},{9,8},{10,11... | collective-permute-start | bytes 5529608 | tf_op jit(solution)/shard_map/ppermute | solution.py:35
  92.9 17.8 %collective-permute-start.16 = (bf16[2,256,640]{2,1,0:T(8,128)(2,1)S(1)}, bf16[2,256,640]{2,1,0:T(8,128)(2,1)S(1)}, u32[]{:S(2)}, u32[]{:S(2)}) collective-permute-start(bf16[2,256,640]{2,1,0:T(8,128)(2,1)S(1)} %pad_maximum_fusion.1.refs_0_), channel_id=1, source_target_pairs={{0,2},{2,0},{1,3},{3,1},{4,6},{6,4},{5,7},{7,5},{8,10},{10,8},{9,1... | collective-permute-start | bytes 1966088 | tf_op jit(solution)/shard_map/ppermute | solution.py:35
  95.8 16.0 %collective-permute-start.21 = (bf16[2,256,640]{2,1,0:T(8,128)(2,1)S(1)}, bf16[2,256,640]{2,1,0:T(8,128)(2,1)S(1)}, u32[]{:S(2)}, u32[]{:S(2)}) collective-permute-start(bf16[2,256,640]{2,1,0:T(8,128)(2,1)S(1)} %collective-permute-done.20.refs_3_), channel_id=1, source_target_pairs={{0,28},{4,0},{8,4},{12,8},{16,12},{20,16},{24,20},{28,24},{1,29},{... | collective-permute-start | bytes 1966088 | tf_op jit(solution)/shard_map/ppermute | solution.py:35
  95.9 15.9 %collective-permute-start.18 = (bf16[2,256,640]{2,1,0:T(8,128)(2,1)S(1)}, bf16[2,256,640]{2,1,0:T(8,128)(2,1)S(1)}, u32[]{:S(2)}, u32[]{:S(2)}) collective-permute-start(bf16[2,256,640]{2,1,0:T(8,128)(2,1)S(1)} %slice_bitcast_fusion), channel_id=1, source_target_pairs={{0,4},{4,8},{8,12},{12,16},{16,20},{20,24},{24,28},{28,0},{1,5},{5... | collective-permute-start | bytes 1966088 | tf_op jit(solution)/shard_map/ppermute | solution.py:35
  97.5 6.5 %copy-start = (bf16[2,256,512]{2,1,0:T(8,128)(2,1)S(1)}, bf16[2,256,512]{2,1,0:T(8,128)(2,1)}, u32[]{:S(2)}) copy-start(bf16[2,256,512]{2,1,0:T(8,128)(2,1)} %constant.28.table) | copy-start | bytes 1572868
  103.0 16.6 %collective-permute-start.24 = (bf16[40,40,256]{2,1,0:T(8,128)(2,1)S(1)}, bf16[40,40,256]{2,1,0:T(8,128)(2,1)S(1)}, u32[]{:S(2)}, u32[]{:S(2)}) collective-permute-start(bf16[40,40,256]{2,1,0:T(8,128)(2,1)S(1)} %get-tuple-element.81), channel_id=1, source_target_pairs={{0,1},{1,0},{2,3},{3,2},{4,5},{5,4},{6,7},{7,6},{8,9},{9,8},{10,11... | collective-permute-start | bytes 2457608 | tf_op jit(solution)/shard_map/ppermute | solution.py:35
  116.9 5.0 %collective-permute-start.23 = (bf16[30,40,256]{2,1,0:T(8,128)(2,1)S(1)}, bf16[30,40,256]{2,1,0:T(8,128)(2,1)S(1)}, u32[]{:S(2)}, u32[]{:S(2)}) collective-permute-start(bf16[30,40,256]{2,1,0:T(8,128)(2,1)S(1)} %get-tuple-element.75), channel_id=1, source_target_pairs={{0,1},{1,0},{2,3},{3,2},{4,5},{5,4},{6,7},{7,6},{8,9},{9,8},{10,11... | collective-permute-start | bytes 1843208 | tf_op jit(solution)/shard_map/ppermute | solution.py:35

commit v7 on v6

--- a/solution.py
+++ b/solution.py
@@ -291,7 +291,7 @@
     cols = [C[dx, dy] for dx in STEPS for dy in (0, 1)]
     own = [R[p] for p in GROUPS[0]]
     keep, send, cols = cross(scal, gate(own, R[3, 0], R[-3, 0])[0], cols, True)
-    R[0, 1] = shift(after(row, keep), "yh", 1)
+    R[0, 1] = shift(after(row, keep, R[-3, 1]), "yh", 1)
     recv = shift(send, "c", 1)
     own, _ = gate([R[p] for p in GROUPS[1]], far, R[-3, 1])
     keep1, send1 = cross(scal, own, cols, False)

time: 124 us -> 124 us (level)
  waiting for transfers between devices: 43.5 us -> 39.1 us
  starting transfers between devices: 45.8 us -> 50.1 us
    ppermute x25, waiting for transfers between devices: 43.5 us -> 39.1 us  [shift(): return lax.ppermute(x, axis, [(i, (i + step) % n) for i in range(n)])]
    ppermute x25, starting transfers between devices: 45.8 us -> 50.1 us  [shift(): return lax.ppermute(x, axis, [(i, (i + step) % n) for i in range(n)])]
  transfers between devices with their start and end apart: 25 -> 25, of which waited for: 9 -> 7; matrix products, arithmetic and copies ran while one was open for 0% -> 0% of each run, Pallas kernels for 21% -> 21%
where the time goes in v7:
time: 124 us
  starting transfers between devices  50.1 us (40%)
  waiting for transfers between devices  39.1 us (32%)
  Pallas kernels  31.4 us (25%)
  local copies, waits for them, and re-layouts  2.91 us (2%)
    ppermute x25, starting transfers between devices, shift(): return lax.ppermute(x, axis, [(i, (i + step) % n) for i in range(n)])  50.1 us
    ppermute x25, waiting for transfers between devices, shift(): return lax.ppermute(x, axis, [(i, (i + step) % n) for i in range(n)])  39.1 us
    pallas_call x3, Pallas kernels, cross(): pl.pallas_call(functools.partial(cross_kernel, n, lead, indices), out_sha...  20 us
    pallas_call x3, Pallas kernels, lags(): pl.pallas_call(functools.partial(lags_kernel, group), out_shape=jax.Shape...  7.92 us
    pallas_call x1, Pallas kernels, whiten(): pl.pallas_call(whiten_kernel, out_shape=(msg, msg), in_specs=[pl.BlockSpe...  3.5 us
  transfers between devices with their start and end apart: 25, of which 7 were waited for; matrix products, arithmetic and copies ran while one was open for 0% of the time, Pallas kernels for 21%

profile of v7, /device:TPU:1, one launch (start us, length us, event | category | flops | bytes accessed | tf_op | source)
XLA Modules:
  0.0 124.2 jit_solution(10922404724674226291)
XLA Ops:
  0.7 1.3 %copy-done.1 = f32[5,64,2,512]{3,2,1,0:T(2,128)S(1)} copy-done((f32[5,64,2,512]{3,2,1,0:T(2,128)S(1)}, f32[5,64,2,512]{3,2,1,0:T(2,128)}, u32[]{:S(2)}) %copy-start.1) | copy-done | bytes 1310744
  2.7 3.5 %whiten.1 = (bf16[2,256,640]{2,1,0:T(8,128)(2,1)S(1)}, bf16[2,256,640]{2,1,0:T(8,128)(2,1)S(1)}) custom-call(s32[10]{0:T(128)S(1)} %concatenate.3.scal, f32[2560,128]{1,0:T(8,128)S(1)} %bitcast.29, s32[5,64]{1,0:T(8,128)S(1)} %copy-done.2), custom_call_target="tpu_custom_call" | custom-call | flops 1000000000 | bytes 3000000 | tf_op jit(solution)/shard_map/whiten/pallas_call | solution.py:93
  6.2 3.3 %collective-permute-start = (bf16[2,256,640]{2,1,0:T(8,128)(2,1)S(1)}, bf16[2,256,640]{2,1,0:T(8,128)(2,1)S(1)}, u32[]{:S(2)}, u32[]{:S(2)}) collective-permute-start(bf16[2,256,640]{2,1,0:T(8,128)(2,1)S(1)} %get-tuple-element.45), channel_id=1, source_target_pairs={{0,1},{1,0},{2,3},{3,2},{4,5},{5,4},{6,7},{7,6},{8,9},{9,8},{10,11... | collective-permute-start | bytes 1966088 | tf_op jit(solution)/shard_map/ppermute | solution.py:35
  9.6 1.7 %collective-permute-done = bf16[2,256,640]{2,1,0:T(8,128)(2,1)S(1)} collective-permute-done((bf16[2,256,640]{2,1,0:T(8,128)(2,1)S(1)}, bf16[2,256,640]{2,1,0:T(8,128)(2,1)S(1)}, u32[]{:S(2)}, u32[]{:S(2)}) %collective-permute-start) | collective-permute-done | bytes 655392 | tf_op jit(solution)/shard_map/ppermute | solution.py:35
  11.5 3.9 %collective-permute-start.2 = (bf16[2,256,640]{2,1,0:T(8,128)(2,1)S(1)}, bf16[2,256,640]{2,1,0:T(8,128)(2,1)S(1)}, u32[]{:S(2)}, u32[]{:S(2)}) collective-permute-start(bf16[2,256,640]{2,1,0:T(8,128)(2,1)S(1)} %pad_maximum_fusion.1.refs_0_), channel_id=1, source_target_pairs={{0,28},{4,0},{8,4},{12,8},{16,12},{20,16},{24,20},{28,24},{1,29},{... | collective-permute-start | bytes 1966088 | tf_op jit(solution)/shard_map/ppermute | solution.py:35
  15.5 1.4 %collective-permute-start.8 = (bf16[2,256,640]{2,1,0:T(8,128)(2,1)S(1)}, bf16[2,256,640]{2,1,0:T(8,128)(2,1)S(1)}, u32[]{:S(2)}, u32[]{:S(2)}) collective-permute-start(bf16[2,256,640]{2,1,0:T(8,128)(2,1)S(1)} %pad_maximum_fusion.2.refs_9_), channel_id=1, source_target_pairs={{0,32},{32,0},{1,33},{33,1},{2,34},{34,2},{3,35},{35,3},{4,36},{36... | collective-permute-start | bytes 1966088 | tf_op jit(solution)/shard_map/ppermute | solution.py:35
  18.1 1.5 %collective-permute-start.5 = (bf16[2,256,640]{2,1,0:T(8,128)(2,1)S(1)}, bf16[2,256,640]{2,1,0:T(8,128)(2,1)S(1)}, u32[]{:S(2)}, u32[]{:S(2)}) collective-permute-start(bf16[2,256,640]{2,1,0:T(8,128)(2,1)S(1)} %pad_maximum_fusion.2.refs_9_), channel_id=1, source_target_pairs={{0,192},{64,0},{128,64},{192,128},{1,193},{65,1},{129,65},{193,129... | collective-permute-start | bytes 1966088 | tf_op jit(solution)/shard_map/ppermute | solution.py:35
  19.6 10.6 %collective-permute-done.1.refs_1_ = bf16[2,256,640]{2,1,0:T(8,128)(2,1)S(1)} collective-permute-done((bf16[2,256,640]{2,1,0:T(8,128)(2,1)S(1)}, bf16[2,256,640]{2,1,0:T(8,128)(2,1)S(1)}, u32[]{:S(2)}, u32[]{:S(2)}) %collective-permute-start.1) | collective-permute-done | bytes 655392 | tf_op jit(solution)/shard_map/ppermute | solution.py:35
  30.2 2.7 %collective-permute-start.4 = (bf16[2,256,640]{2,1,0:T(8,128)(2,1)S(1)}, bf16[2,256,640]{2,1,0:T(8,128)(2,1)S(1)}, u32[]{:S(2)}, u32[]{:S(2)}) collective-permute-start(bf16[2,256,640]{2,1,0:T(8,128)(2,1)S(1)} %collective-permute-done.2.refs_2_), channel_id=1, source_target_pairs={{0,28},{4,0},{8,4},{12,8},{16,12},{20,16},{24,20},{28,24},{1,29},{... | collective-permute-start | bytes 1966088 | tf_op jit(solution)/shard_map/ppermute | solution.py:35
  33.4 2.6 %collective-permute-start.10 = (bf16[2,256,640]{2,1,0:T(8,128)(2,1)S(1)}, bf16[2,256,640]{2,1,0:T(8,128)(2,1)S(1)}, u32[]{:S(2)}, u32[]{:S(2)}) collective-permute-start(bf16[2,256,640]{2,1,0:T(8,128)(2,1)S(1)} %collective-permute-done.2.refs_2_), channel_id=1, source_target_pairs={{0,2},{2,0},{1,3},{3,1},{4,6},{6,4},{5,7},{7,5},{8,10},{10,8},{9,1... | collective-permute-start | bytes 1966088 | tf_op jit(solution)/shard_map/ppermute | solution.py:35
  37.0 1.7 %collective-permute-start.13 = (bf16[2,256,640]{2,1,0:T(8,128)(2,1)S(1)}, bf16[2,256,640]{2,1,0:T(8,128)(2,1)S(1)}, u32[]{:S(2)}, u32[]{:S(2)}) collective-permute-start(bf16[2,256,640]{2,1,0:T(8,128)(2,1)S(1)} %collective-permute-done.8.refs_10_), channel_id=1, source_target_pairs={{0,192},{64,0},{128,64},{192,128},{1,193},{65,1},{129,65},{193,129... | collective-permute-start | bytes 1966088 | tf_op jit(solution)/shard_map/ppermute | solution.py:35
  38.7 8.0 %collective-permute-done.3.refs_3_ = bf16[2,256,640]{2,1,0:T(8,128)(2,1)S(1)} collective-permute-done((bf16[2,256,640]{2,1,0:T(8,128)(2,1)S(1)}, bf16[2,256,640]{2,1,0:T(8,128)(2,1)S(1)}, u32[]{:S(2)}, u32[]{:S(2)}) %collective-permute-start.3) | collective-permute-done | bytes 655392 | tf_op jit(solution)/shard_map/ppermute | solution.py:35
  46.7 2.7 %collective-permute-start.7 = (bf16[2,256,640]{2,1,0:T(8,128)(2,1)S(1)}, bf16[2,256,640]{2,1,0:T(8,128)(2,1)S(1)}, u32[]{:S(2)}, u32[]{:S(2)}) collective-permute-start(bf16[2,256,640]{2,1,0:T(8,128)(2,1)S(1)} %collective-permute-done.4.refs_4_), channel_id=1, source_target_pairs={{0,28},{4,0},{8,4},{12,8},{16,12},{20,16},{24,20},{28,24},{1,29},{... | collective-permute-start | bytes 1966088 | tf_op jit(solution)/shard_map/ppermute | solution.py:35
  49.4 2.9 %collective-permute-start.11 = (bf16[2,256,640]{2,1,0:T(8,128)(2,1)S(1)}, bf16[2,256,640]{2,1,0:T(8,128)(2,1)S(1)}, u32[]{:S(2)}, u32[]{:S(2)}) collective-permute-start(bf16[2,256,640]{2,1,0:T(8,128)(2,1)S(1)} %collective-permute-done.1.refs_1_), channel_id=1, source_target_pairs={{0,2},{2,0},{1,3},{3,1},{4,6},{6,4},{5,7},{7,5},{8,10},{10,8},{9,1... | collective-permute-start | bytes 1966088 | tf_op jit(solution)/shard_map/ppermute | solution.py:35
  52.3 1.2 collective-permute-start.14
  53.5 1.5 %collective-permute-start.15 = (bf16[2,256,640]{2,1,0:T(8,128)(2,1)S(1)}, bf16[2,256,640]{2,1,0:T(8,128)(2,1)S(1)}, u32[]{:S(2)}, u32[]{:S(2)}) collective-permute-start(bf16[2,256,640]{2,1,0:T(8,128)(2,1)S(1)} %collective-permute-done.13.refs_14_), channel_id=1, source_target_pairs={{0,192},{64,0},{128,64},{192,128},{1,193},{65,1},{129,65},{193,129... | collective-permute-start | bytes 1966088 | tf_op jit(solution)/shard_map/ppermute | solution.py:35
  55.0 7.4 %collective-permute-done.6.refs_5_ = bf16[2,256,640]{2,1,0:T(8,128)(2,1)S(1)} collective-permute-done((bf16[2,256,640]{2,1,0:T(8,128)(2,1)S(1)}, bf16[2,256,640]{2,1,0:T(8,128)(2,1)S(1)}, u32[]{:S(2)}, u32[]{:S(2)}) %collective-permute-start.6) | collective-permute-done | bytes 655392 | tf_op jit(solution)/shard_map/ppermute | solution.py:35
  62.4 2.4 %collective-permute-start.16 = (bf16[2,256,640]{2,1,0:T(8,128)(2,1)S(1)}, bf16[2,256,640]{2,1,0:T(8,128)(2,1)S(1)}, u32[]{:S(2)}, u32[]{:S(2)}) collective-permute-start(bf16[2,256,640]{2,1,0:T(8,128)(2,1)S(1)} %collective-permute-done.10.refs_8_), channel_id=1, source_target_pairs={{0,28},{4,0},{8,4},{12,8},{16,12},{20,16},{24,20},{28,24},{1,29},{... | collective-permute-start | bytes 1966088 | tf_op jit(solution)/shard_map/ppermute | solution.py:35
  65.0 2.1 %collective-permute-done.14.refs_15_ = bf16[2,256,640]{2,1,0:T(8,128)(2,1)S(1)} collective-permute-done((bf16[2,256,640]{2,1,0:T(8,128)(2,1)S(1)}, bf16[2,256,640]{2,1,0:T(8,128)(2,1)S(1)}, u32[]{:S(2)}, u32[]{:S(2)}) %collective-permute-start.14) | collective-permute-done | bytes 655392 | tf_op jit(solution)/shard_map/ppermute | solution.py:35
  67.1 8.8 %collective-permute-done.16.refs_0_ = bf16[2,256,640]{2,1,0:T(8,128)(2,1)S(1)} collective-permute-done((bf16[2,256,640]{2,1,0:T(8,128)(2,1)S(1)}, bf16[2,256,640]{2,1,0:T(8,128)(2,1)S(1)}, u32[]{:S(2)}, u32[]{:S(2)}) %collective-permute-start.16) | collective-permute-done | bytes 655392 | tf_op jit(solution)/shard_map/ppermute | solution.py:35
  75.9 3.3 %collective-permute-start.17 = (bf16[2,256,640]{2,1,0:T(8,128)(2,1)S(1)}, bf16[2,256,640]{2,1,0:T(8,128)(2,1)S(1)}, u32[]{:S(2)}, u32[]{:S(2)}) collective-permute-start(bf16[2,256,640]{2,1,0:T(8,128)(2,1)S(1)} %collective-permute-done.16.refs_0_), channel_id=1, source_target_pairs={{0,28},{4,0},{8,4},{12,8},{16,12},{20,16},{24,20},{28,24},{1,29},{... | collective-permute-start | bytes 1966088 | tf_op jit(solution)/shard_map/ppermute | solution.py:35
  79.2 9.4 %cross.3 = (bf16[90,40,256]{2,1,0:T(8,128)(2,1)S(1)}, bf16[90,40,256]{2,1,0:T(8,128)(2,1)S(1)}, bf16[256,80,128]{2,1,0:T(8,128)(2,1)S(1)}) custom-call(s32[10]{0:T(128)S(1)} %concatenate.3.scal, bf16[2,256,640]{2,1,0:T(8,128)(2,1)S(1)} %pad_maximum_fusion.1.refs_0_, bf16[2,256,640]{2,1,0:T(8,128)(2,1)S(1)} %collective-permute-done.1.refs_1_, ...), custom_call_target="tpu_custom_call" | custom-call | flops 10000000000 | bytes 10000000 | tf_op jit(solution)/shard_map/cross/pallas_call | solution.py:187
  88.6 4.3 %collective-permute-start.22 = (bf16[90,40,256]{2,1,0:T(8,128)(2,1)S(1)}, bf16[90,40,256]{2,1,0:T(8,128)(2,1)S(1)}, u32[]{:S(2)}, u32[]{:S(2)}) collective-permute-start(bf16[90,40,256]{2,1,0:T(8,128)(2,1)S(1)} %get-tuple-element.69), channel_id=1, source_target_pairs={{0,1},{1,0},{2,3},{3,2},{4,5},{5,4},{6,7},{7,6},{8,9},{9,8},{10,11... | collective-permute-start | bytes 5529608 | tf_op jit(solution)/shard_map/ppermute | solution.py:35
  92.9 2.9 %collective-permute-start.18 = (bf16[2,256,640]{2,1,0:T(8,128)(2,1)S(1)}, bf16[2,256,640]{2,1,0:T(8,128)(2,1)S(1)}, u32[]{:S(2)}, u32[]{:S(2)}) collective-permute-start(bf16[2,256,640]{2,1,0:T(8,128)(2,1)S(1)} %pad_maximum_fusion.1.refs_0_), channel_id=1, source_target_pairs={{0,2},{2,0},{1,3},{3,1},{4,6},{6,4},{5,7},{7,5},{8,10},{10,8},{9,1... | collective-permute-start | bytes 1966088 | tf_op jit(solution)/shard_map/ppermute | solution.py:35
  95.9 1.5 %collective-permute-start.20 = (bf16[2,256,640]{2,1,0:T(8,128)(2,1)S(1)}, bf16[2,256,640]{2,1,0:T(8,128)(2,1)S(1)}, u32[]{:S(2)}, u32[]{:S(2)}) collective-permute-start(bf16[2,256,640]{2,1,0:T(8,128)(2,1)S(1)} %slice_bitcast_fusion), channel_id=1, source_target_pairs={{0,4},{4,8},{8,12},{12,16},{16,20},{20,24},{24,28},{28,0},{1,5},{5... | collective-permute-start | bytes 1966088 | tf_op jit(solution)/shard_map/ppermute | solution.py:35
  97.4 5.5 %cross.5 = (bf16[40,40,256]{2,1,0:T(8,128)(2,1)S(1)}, bf16[40,40,256]{2,1,0:T(8,128)(2,1)S(1)}) custom-call(s32[10]{0:T(128)S(1)} %concatenate.3.scal, bf16[2,256,640]{2,1,0:T(8,128)(2,1)S(1)} %collective-permute-done.16.refs_0_, bf16[2,2,256,640]{3,2,1,0:T(8,128)(2,1)S(1)} %collective-permute-done.19.refs_1_.refs_2_, ...), custom_call_target="tpu_custom_call" | custom-call | flops 10000000000 | bytes 10000000 | tf_op jit(solution)/shard_map/cross/pallas_call | solution.py:187
  103.0 4.2 %collective-permute-start.24 = (bf16[40,40,256]{2,1,0:T(8,128)(2,1)S(1)}, bf16[40,40,256]{2,1,0:T(8,128)(2,1)S(1)}, u32[]{:S(2)}, u32[]{:S(2)}) collective-permute-start(bf16[40,40,256]{2,1,0:T(8,128)(2,1)S(1)} %get-tuple-element.81), channel_id=1, source_target_pairs={{0,1},{1,0},{2,3},{3,2},{4,5},{5,4},{6,7},{7,6},{8,9},{9,8},{10,11... | collective-permute-start | bytes 2457608 | tf_op jit(solution)/shard_map/ppermute | solution.py:35
  107.1 3.5 %lags.3.rest_0_ = bf16[6400,512]{1,0:T(8,128)(2,1)} custom-call(s32[10]{0:T(128)S(1)} %concatenate.3.scal, bf16[3600,256]{1,0:T(8,128)(2,1)S(1)} %bitcast.21, bf16[3600,256]{1,0:T(8,128)(2,1)S(1)} %bitcast.22, bf16[2,256,512]{2,1,0:T(8,128)(2,1)S(1)} %copy-done), custom_call_target="tpu_custom_call" | custom-call | flops 2000000000 | bytes 3000000 | tf_op jit(solution)/shard_map/lags/pallas_call | solution.py:224
  110.6 5.1 %cross.4 = (bf16[30,40,256]{2,1,0:T(8,128)(2,1)S(1)}, bf16[30,40,256]{2,1,0:T(8,128)(2,1)S(1)}) custom-call(s32[10]{0:T(128)S(1)} %concatenate.3.scal, bf16[2,256,640]{2,1,0:T(8,128)(2,1)S(1)} %collective-permute-done.18.refs_0_, bf16[2,256,640]{2,1,0:T(8,128)(2,1)S(1)} %collective-permute-done.20.refs_1_, ...), custom_call_target="tpu_custom_call" | custom-call | flops 10000000000 | bytes 10000000 | tf_op jit(solution)/shard_map/cross/pallas_call | solution.py:187
  115.7 3.8 %collective-permute-start.23 = (bf16[30,40,256]{2,1,0:T(8,128)(2,1)S(1)}, bf16[30,40,256]{2,1,0:T(8,128)(2,1)S(1)}, u32[]{:S(2)}, u32[]{:S(2)}) collective-permute-start(bf16[30,40,256]{2,1,0:T(8,128)(2,1)S(1)} %get-tuple-element.75), channel_id=1, source_target_pairs={{0,1},{1,0},{2,3},{3,2},{4,5},{5,4},{6,7},{7,6},{8,9},{9,8},{10,11... | collective-permute-start | bytes 1843208 | tf_op jit(solution)/shard_map/ppermute | solution.py:35
  119.5 2.3 %lags.4.rest_0_ = bf16[6400,512]{1,0:T(8,128)(2,1)} custom-call(s32[10]{0:T(128)S(1)} %concatenate.3.scal, bf16[1600,256]{1,0:T(8,128)(2,1)S(1)} %bitcast.23, bf16[1600,256]{1,0:T(8,128)(2,1)S(1)} %bitcast.24, bf16[2,256,512]{2,1,0:T(8,128)(2,1)S(1)} %copy-done, bf16[6400,512]{1,0:T(8,128)(2,1)} %lags.3.rest_0_), custom_call_target="tpu_custom_call", output_to_operand_aliasing={{}: (4, {})} | custom-call | flops 2000000000 | bytes 3000000 | tf_op jit(solution)/shard_map/lags/pallas_call | solution.py:224
  121.9 2.1 %lags.5 = bf16[6400,512]{1,0:T(8,128)(2,1)} custom-call(s32[10]{0:T(128)S(1)} %concatenate.3.scal, bf16[1200,256]{1,0:T(8,128)(2,1)S(1)} %bitcast.27, bf16[1200,256]{1,0:T(8,128)(2,1)S(1)} %bitcast.28, bf16[2,256,512]{2,1,0:T(8,128)(2,1)S(1)} %copy-done, bf16[6400,512]{1,0:T(8,128)(2,1)} %lags.4.rest_0_), custom_call_target="tpu_custom_call", output_to_operand_aliasing={{}: (4, {})} | custom-call | flops 2000000000 | bytes 3000000 | tf_op jit(solution)/shard_map/lags/pallas_call | solution.py:224
  (38 shorter events, 4.8 us)
Async XLA Ops:
  0.7 1.3 %copy-start.1 = (f32[5,64,2,512]{3,2,1,0:T(2,128)S(1)}, f32[5,64,2,512]{3,2,1,0:T(2,128)}, u32[]{:S(2)}) copy-start(f32[5,64,2,512]{3,2,1,0:T(2,128)} %param.4) | copy-start | bytes 3932164
  2.1 0.7 copy-start.2
  6.2 5.0 %collective-permute-start = (bf16[2,256,640]{2,1,0:T(8,128)(2,1)S(1)}, bf16[2,256,640]{2,1,0:T(8,128)(2,1)S(1)}, u32[]{:S(2)}, u32[]{:S(2)}) collective-permute-start(bf16[2,256,640]{2,1,0:T(8,128)(2,1)S(1)} %get-tuple-element.45), channel_id=1, source_target_pairs={{0,1},{1,0},{2,3},{3,2},{4,5},{5,4},{6,7},{7,6},{8,9},{9,8},{10,11... | collective-permute-start | bytes 1966088 | tf_op jit(solution)/shard_map/ppermute | solution.py:35
  11.4 18.7 %collective-permute-start.1 = (bf16[2,256,640]{2,1,0:T(8,128)(2,1)S(1)}, bf16[2,256,640]{2,1,0:T(8,128)(2,1)S(1)}, u32[]{:S(2)}, u32[]{:S(2)}) collective-permute-start(bf16[2,256,640]{2,1,0:T(8,128)(2,1)S(1)} %pad_maximum_fusion.1.refs_0_), channel_id=1, source_target_pairs={{0,4},{4,8},{8,12},{12,16},{16,20},{20,24},{24,28},{28,0},{1,5},{5... | collective-permute-start | bytes 1966088 | tf_op jit(solution)/shard_map/ppermute | solution.py:35
  11.5 18.6 %collective-permute-start.2 = (bf16[2,256,640]{2,1,0:T(8,128)(2,1)S(1)}, bf16[2,256,640]{2,1,0:T(8,128)(2,1)S(1)}, u32[]{:S(2)}, u32[]{:S(2)}) collective-permute-start(bf16[2,256,640]{2,1,0:T(8,128)(2,1)S(1)} %pad_maximum_fusion.1.refs_0_), channel_id=1, source_target_pairs={{0,28},{4,0},{8,4},{12,8},{16,12},{20,16},{24,20},{28,24},{1,29},{... | collective-permute-start | bytes 1966088 | tf_op jit(solution)/shard_map/ppermute | solution.py:35
  15.5 17.3 %collective-permute-start.8 = (bf16[2,256,640]{2,1,0:T(8,128)(2,1)S(1)}, bf16[2,256,640]{2,1,0:T(8,128)(2,1)S(1)}, u32[]{:S(2)}, u32[]{:S(2)}) collective-permute-start(bf16[2,256,640]{2,1,0:T(8,128)(2,1)S(1)} %pad_maximum_fusion.2.refs_9_), channel_id=1, source_target_pairs={{0,32},{32,0},{1,33},{33,1},{2,34},{34,2},{3,35},{35,3},{4,36},{36... | collective-permute-start | bytes 1966088 | tf_op jit(solution)/shard_map/ppermute | solution.py:35
  16.9 16.5 %collective-permute-start.9 = (bf16[2,256,640]{2,1,0:T(8,128)(2,1)S(1)}, bf16[2,256,640]{2,1,0:T(8,128)(2,1)S(1)}, u32[]{:S(2)}, u32[]{:S(2)}) collective-permute-start(bf16[2,256,640]{2,1,0:T(8,128)(2,1)S(1)} %pad_maximum_fusion.2.refs_9_), channel_id=1, source_target_pairs={{0,64},{64,128},{128,192},{192,0},{1,65},{65,129},{129,193},{193,1... | collective-permute-start | bytes 1966088 | tf_op jit(solution)/shard_map/ppermute | solution.py:35
  18.1 18.9 %collective-permute-start.5 = (bf16[2,256,640]{2,1,0:T(8,128)(2,1)S(1)}, bf16[2,256,640]{2,1,0:T(8,128)(2,1)S(1)}, u32[]{:S(2)}, u32[]{:S(2)}) collective-permute-start(bf16[2,256,640]{2,1,0:T(8,128)(2,1)S(1)} %pad_maximum_fusion.2.refs_9_), channel_id=1, source_target_pairs={{0,192},{64,0},{128,64},{192,128},{1,193},{65,1},{129,65},{193,129... | collective-permute-start | bytes 1966088 | tf_op jit(solution)/shard_map/ppermute | solution.py:35
  30.2 16.6 %collective-permute-start.3 = (bf16[2,256,640]{2,1,0:T(8,128)(2,1)S(1)}, bf16[2,256,640]{2,1,0:T(8,128)(2,1)S(1)}, u32[]{:S(2)}, u32[]{:S(2)}) collective-permute-start(bf16[2,256,640]{2,1,0:T(8,128)(2,1)S(1)} %collective-permute-done.1.refs_1_), channel_id=1, source_target_pairs={{0,4},{4,8},{8,12},{12,16},{16,20},{20,24},{24,28},{28,0},{1,5},{5... | collective-permute-start | bytes 1966088 | tf_op jit(solution)/shard_map/ppermute | solution.py:35
  30.2 16.6 %collective-permute-start.4 = (bf16[2,256,640]{2,1,0:T(8,128)(2,1)S(1)}, bf16[2,256,640]{2,1,0:T(8,128)(2,1)S(1)}, u32[]{:S(2)}, u32[]{:S(2)}) collective-permute-start(bf16[2,256,640]{2,1,0:T(8,128)(2,1)S(1)} %collective-permute-done.2.refs_2_), channel_id=1, source_target_pairs={{0,28},{4,0},{8,4},{12,8},{16,12},{20,16},{24,20},{28,24},{1,29},{... | collective-permute-start | bytes 1966088 | tf_op jit(solution)/shard_map/ppermute | solution.py:35
  33.4 16.0 %collective-permute-start.10 = (bf16[2,256,640]{2,1,0:T(8,128)(2,1)S(1)}, bf16[2,256,640]{2,1,0:T(8,128)(2,1)S(1)}, u32[]{:S(2)}, u32[]{:S(2)}) collective-permute-start(bf16[2,256,640]{2,1,0:T(8,128)(2,1)S(1)} %collective-permute-done.2.refs_2_), channel_id=1, source_target_pairs={{0,2},{2,0},{1,3},{3,1},{4,6},{6,4},{5,7},{7,5},{8,10},{10,8},{9,1... | collective-permute-start | bytes 1966088 | tf_op jit(solution)/shard_map/ppermute | solution.py:35
  36.0 16.3 %collective-permute-start.12 = (bf16[2,256,640]{2,1,0:T(8,128)(2,1)S(1)}, bf16[2,256,640]{2,1,0:T(8,128)(2,1)S(1)}, u32[]{:S(2)}, u32[]{:S(2)}) collective-permute-start(bf16[2,256,640]{2,1,0:T(8,128)(2,1)S(1)} %collective-permute-done.8.refs_10_), channel_id=1, source_target_pairs={{0,64},{64,128},{128,192},{192,0},{1,65},{65,129},{129,193},{193,1... | collective-permute-start | bytes 1966088 | tf_op jit(solution)/shard_map/ppermute | solution.py:35
  37.0 16.6 %collective-permute-start.13 = (bf16[2,256,640]{2,1,0:T(8,128)(2,1)S(1)}, bf16[2,256,640]{2,1,0:T(8,128)(2,1)S(1)}, u32[]{:S(2)}, u32[]{:S(2)}) collective-permute-start(bf16[2,256,640]{2,1,0:T(8,128)(2,1)S(1)} %collective-permute-done.8.refs_10_), channel_id=1, source_target_pairs={{0,192},{64,0},{128,64},{192,128},{1,193},{65,1},{129,65},{193,129... | collective-permute-start | bytes 1966088 | tf_op jit(solution)/shard_map/ppermute | solution.py:35
  46.7 15.7 %collective-permute-start.6 = (bf16[2,256,640]{2,1,0:T(8,128)(2,1)S(1)}, bf16[2,256,640]{2,1,0:T(8,128)(2,1)S(1)}, u32[]{:S(2)}, u32[]{:S(2)}) collective-permute-start(bf16[2,256,640]{2,1,0:T(8,128)(2,1)S(1)} %collective-permute-done.3.refs_3_), channel_id=1, source_target_pairs={{0,4},{4,8},{8,12},{12,16},{16,20},{20,24},{24,28},{28,0},{1,5},{5... | collective-permute-start | bytes 1966088 | tf_op jit(solution)/shard_map/ppermute | solution.py:35
  46.7 15.7 %collective-permute-start.7 = (bf16[2,256,640]{2,1,0:T(8,128)(2,1)S(1)}, bf16[2,256,640]{2,1,0:T(8,128)(2,1)S(1)}, u32[]{:S(2)}, u32[]{:S(2)}) collective-permute-start(bf16[2,256,640]{2,1,0:T(8,128)(2,1)S(1)} %collective-permute-done.4.refs_4_), channel_id=1, source_target_pairs={{0,28},{4,0},{8,4},{12,8},{16,12},{20,16},{24,20},{28,24},{1,29},{... | collective-permute-start | bytes 1966088 | tf_op jit(solution)/shard_map/ppermute | solution.py:35
  49.4 15.4 %collective-permute-start.11 = (bf16[2,256,640]{2,1,0:T(8,128)(2,1)S(1)}, bf16[2,256,640]{2,1,0:T(8,128)(2,1)S(1)}, u32[]{:S(2)}, u32[]{:S(2)}) collective-permute-start(bf16[2,256,640]{2,1,0:T(8,128)(2,1)S(1)} %collective-permute-done.1.refs_1_), channel_id=1, source_target_pairs={{0,2},{2,0},{1,3},{3,1},{4,6},{6,4},{5,7},{7,5},{8,10},{10,8},{9,1... | collective-permute-start | bytes 1966088 | tf_op jit(solution)/shard_map/ppermute | solution.py:35
  52.3 14.8 %collective-permute-start.14 = (bf16[2,256,640]{2,1,0:T(8,128)(2,1)S(1)}, bf16[2,256,640]{2,1,0:T(8,128)(2,1)S(1)}, u32[]{:S(2)}, u32[]{:S(2)}) collective-permute-start(bf16[2,256,640]{2,1,0:T(8,128)(2,1)S(1)} %collective-permute-done.9.refs_11_), channel_id=1, source_target_pairs={{0,64},{64,128},{128,192},{192,0},{1,65},{65,129},{129,193},{193,1... | collective-permute-start | bytes 1966088 | tf_op jit(solution)/shard_map/ppermute | solution.py:35
  53.5 13.6 %collective-permute-start.15 = (bf16[2,256,640]{2,1,0:T(8,128)(2,1)S(1)}, bf16[2,256,640]{2,1,0:T(8,128)(2,1)S(1)}, u32[]{:S(2)}, u32[]{:S(2)}) collective-permute-start(bf16[2,256,640]{2,1,0:T(8,128)(2,1)S(1)} %collective-permute-done.13.refs_14_), channel_id=1, source_target_pairs={{0,192},{64,0},{128,64},{192,128},{1,193},{65,1},{129,65},{193,129... | collective-permute-start | bytes 1966088 | tf_op jit(solution)/shard_map/ppermute | solution.py:35
  62.4 13.5 %collective-permute-start.16 = (bf16[2,256,640]{2,1,0:T(8,128)(2,1)S(1)}, bf16[2,256,640]{2,1,0:T(8,128)(2,1)S(1)}, u32[]{:S(2)}, u32[]{:S(2)}) collective-permute-start(bf16[2,256,640]{2,1,0:T(8,128)(2,1)S(1)} %collective-permute-done.10.refs_8_), channel_id=1, source_target_pairs={{0,28},{4,0},{8,4},{12,8},{16,12},{20,16},{24,20},{28,24},{1,29},{... | collective-permute-start | bytes 1966088 | tf_op jit(solution)/shard_map/ppermute | solution.py:35
  64.9 30.9 %collective-permute-start.19 = (bf16[2,2,256,640]{3,2,1,0:T(8,128)(2,1)S(1)}, bf16[2,2,256,640]{3,2,1,0:T(8,128)(2,1)S(1)}, u32[]{:S(2)}, u32[]{:S(2)}) collective-permute-start(bf16[2,2,256,640]{3,2,1,0:T(8,128)(2,1)S(1)} %pad_maximum_fusion), channel_id=1, source_target_pairs={{0,4},{4,8},{8,12},{12,16},{16,20},{20,24},{24,28},{28,0},{1,5},{5... | collective-permute-start | bytes 3932168 | tf_op jit(solution)/shard_map/ppermute | solution.py:35
  75.9 17.0 %collective-permute-start.17 = (bf16[2,256,640]{2,1,0:T(8,128)(2,1)S(1)}, bf16[2,256,640]{2,1,0:T(8,128)(2,1)S(1)}, u32[]{:S(2)}, u32[]{:S(2)}) collective-permute-start(bf16[2,256,640]{2,1,0:T(8,128)(2,1)S(1)} %collective-permute-done.16.refs_0_), channel_id=1, source_target_pairs={{0,28},{4,0},{8,4},{12,8},{16,12},{20,16},{24,20},{28,24},{1,29},{... | collective-permute-start | bytes 1966088 | tf_op jit(solution)/shard_map/ppermute | solution.py:35
  88.6 18.5 %collective-permute-start.22 = (bf16[90,40,256]{2,1,0:T(8,128)(2,1)S(1)}, bf16[90,40,256]{2,1,0:T(8,128)(2,1)S(1)}, u32[]{:S(2)}, u32[]{:S(2)}) collective-permute-start(bf16[90,40,256]{2,1,0:T(8,128)(2,1)S(1)} %get-tuple-element.69), channel_id=1, source_target_pairs={{0,1},{1,0},{2,3},{3,2},{4,5},{5,4},{6,7},{7,6},{8,9},{9,8},{10,11... | collective-permute-start | bytes 5529608 | tf_op jit(solution)/shard_map/ppermute | solution.py:35
  92.9 17.7 %collective-permute-start.18 = (bf16[2,256,640]{2,1,0:T(8,128)(2,1)S(1)}, bf16[2,256,640]{2,1,0:T(8,128)(2,1)S(1)}, u32[]{:S(2)}, u32[]{:S(2)}) collective-permute-start(bf16[2,256,640]{2,1,0:T(8,128)(2,1)S(1)} %pad_maximum_fusion.1.refs_0_), channel_id=1, source_target_pairs={{0,2},{2,0},{1,3},{3,1},{4,6},{6,4},{5,7},{7,5},{8,10},{10,8},{9,1... | collective-permute-start | bytes 1966088 | tf_op jit(solution)/shard_map/ppermute | solution.py:35
  95.8 14.8 %collective-permute-start.21 = (bf16[2,256,640]{2,1,0:T(8,128)(2,1)S(1)}, bf16[2,256,640]{2,1,0:T(8,128)(2,1)S(1)}, u32[]{:S(2)}, u32[]{:S(2)}) collective-permute-start(bf16[2,256,640]{2,1,0:T(8,128)(2,1)S(1)} %collective-permute-done.17.refs_3_), channel_id=1, source_target_pairs={{0,28},{4,0},{8,4},{12,8},{16,12},{20,16},{24,20},{28,24},{1,29},{... | collective-permute-start | bytes 1966088 | tf_op jit(solution)/shard_map/ppermute | solution.py:35
  95.9 14.7 %collective-permute-start.20 = (bf16[2,256,640]{2,1,0:T(8,128)(2,1)S(1)}, bf16[2,256,640]{2,1,0:T(8,128)(2,1)S(1)}, u32[]{:S(2)}, u32[]{:S(2)}) collective-permute-start(bf16[2,256,640]{2,1,0:T(8,128)(2,1)S(1)} %slice_bitcast_fusion), channel_id=1, source_target_pairs={{0,4},{4,8},{8,12},{12,16},{16,20},{20,24},{24,28},{28,0},{1,5},{5... | collective-permute-start | bytes 1966088 | tf_op jit(solution)/shard_map/ppermute | solution.py:35
  97.4 9.7 %copy-start = (bf16[2,256,512]{2,1,0:T(8,128)(2,1)S(1)}, bf16[2,256,512]{2,1,0:T(8,128)(2,1)}, u32[]{:S(2)}) copy-start(bf16[2,256,512]{2,1,0:T(8,128)(2,1)} %constant.28.table) | copy-start | bytes 1572868
  103.0 16.6 %collective-permute-start.24 = (bf16[40,40,256]{2,1,0:T(8,128)(2,1)S(1)}, bf16[40,40,256]{2,1,0:T(8,128)(2,1)S(1)}, u32[]{:S(2)}, u32[]{:S(2)}) collective-permute-start(bf16[40,40,256]{2,1,0:T(8,128)(2,1)S(1)} %get-tuple-element.81), channel_id=1, source_target_pairs={{0,1},{1,0},{2,3},{3,2},{4,5},{5,4},{6,7},{7,6},{8,9},{9,8},{10,11... | collective-permute-start | bytes 2457608 | tf_op jit(solution)/shard_map/ppermute | solution.py:35
  115.7 6.2 %collective-permute-start.23 = (bf16[30,40,256]{2,1,0:T(8,128)(2,1)S(1)}, bf16[30,40,256]{2,1,0:T(8,128)(2,1)S(1)}, u32[]{:S(2)}, u32[]{:S(2)}) collective-permute-start(bf16[30,40,256]{2,1,0:T(8,128)(2,1)S(1)} %get-tuple-element.75), channel_id=1, source_target_pairs={{0,1},{1,0},{2,3},{3,2},{4,5},{5,4},{6,7},{7,6},{8,9},{9,8},{10,11... | collective-permute-start | bytes 1843208 | tf_op jit(solution)/shard_map/ppermute | solution.py:35
